TPU v7x, 32 devices: a whole 2x2x4 slice. The times are simulated.
32 devices in a mesh: rep: 4 (over x, core), shard: 8 (over z, y).
Axes of the slice: x: 2, y: 2, z: 4, core: 2. Of those that a mesh axis runs over, the one named last changes fastest.
Arguments:
- tokens: bfloat16 [16384, 1024], P(('rep', 'shard')), may hold values from -6 to 6
- lengths: int32 [32], P(('rep', 'shard')), may hold values from 1 to 512, 12288 in all
- cotangent: bfloat16 [16384, 1024], P(('rep', 'shard')), may hold values from -6 to 6
- norm_gain: bfloat16 [6, 1024], P(None, 'shard'), may hold values from 0.25 to 1.75
- norm_shift: bfloat16 [6, 1024], P(None, 'shard'), may hold values from -2.5 to 2.5
- feed_in: bfloat16 [2, 1024, 4096], P(None, 'shard'), may hold values from -0.1875 to 0.1875
- feed_in_bias: bfloat16 [2, 4096], P(None, 'shard'), may hold values from -2.5 to 2.5
- feed_out: bfloat16 [2, 4096, 1024], P(None, 'shard'), may hold values from -0.09375 to 0.09375
- feed_out_bias: bfloat16 [2, 1024], P(None, 'shard'), may hold values from -2.5 to 2.5
- attention_in: bfloat16 [1024, 3072], P('shard'), may hold values from -0.1875 to 0.1875
- attention_in_bias: bfloat16 [2, 1024], P(None, 'shard'), may hold values from -2.5 to 2.5
- attention_out: bfloat16 [1024, 1024], P('shard'), may hold values from -0.75 to 0.75
- attention_out_bias: bfloat16 [1024], P('shard'), may hold values from -2.5 to 2.5
- relative_table: bfloat16 [73, 64], replicated, may hold values from -6 to 6
- pointwise_in: bfloat16 [1024, 2048], P('shard'), may hold values from -0.1875 to 0.1875
- depthwise: bfloat16 [31, 1024], P(None, 'shard'), may hold values from -1 to 1
- pointwise_out: bfloat16 [1024, 1024], P('shard'), may hold values from -0.1875 to 0.1875
Outputs:
- activations: bfloat16 [16384, 1024], P(('rep', 'shard'))
- tokens_grad: bfloat16 [16384, 1024], P(('rep', 'shard'))
- norm_gain_grad: float32 [6, 1024], P(None, 'shard')
- norm_shift_grad: float32 [6, 1024], P(None, 'shard')
- feed_in_grad: float32 [2, 1024, 4096], P(None, 'shard')
- feed_in_bias_grad: float32 [2, 4096], P(None, 'shard')
- feed_out_grad: float32 [2, 4096, 1024], P(None, 'shard')
- feed_out_bias_grad: float32 [2, 1024], P(None, 'shard')
- attention_in_grad: float32 [1024, 3072], P('shard')
- attention_in_bias_grad: float32 [2, 1024], P(None, 'shard')
- attention_out_grad: float32 [1024, 1024], P('shard')
- attention_out_bias_grad: float32 [1024], P('shard')
- relative_table_grad: float32 [73, 64], replicated
- pointwise_in_grad: float32 [1024, 2048], P('shard')
- depthwise_grad: float32 [31, 1024], P(None, 'shard')
- pointwise_out_grad: float32 [1024, 1024], P('shard')
Inputs may be any that keep to these rules, and one draw needn't show every extreme that they name: `lengths`: each device's block holds one clip; its length is the number of live rows at the block's start.
All inputs are finite; a program needn't handle non-finite values.
Results may differ from a plain program's by a relative error of at most 0.02.
Values may be sent and summed in bfloat16 or wider, within the bound.
A program may use at most 320 MiB of HBM per device.

v0:
```python
import math

import jax
import jax.numpy as jnp
from jax import lax
from jax.sharding import PartitionSpec as P

HEADS = 16
LEFT = 64
RIGHT = 8


def round_plain(value):
    return lax.optimization_barrier(value.astype(jnp.bfloat16)).astype(jnp.float32)


def pass_plain(value):
    return value


def round_keep(value):
    return (round_plain(value), None)


def round_pass(kept, grad):
    return (grad,)


def pass_keep(value):
    return (value, None)


def project_plain(inputs, matrix):
    return jnp.dot(inputs.astype(jnp.bfloat16), matrix, preferred_element_type=jnp.float32)


def project_keep(inputs, matrix):
    return (project_plain(inputs, matrix), matrix)


def project_back(matrix, grad):
    back = lax.dot_general(
        grad.astype(jnp.bfloat16),
        matrix,
        (((1,), (1,)), ((), ())),
        preferred_element_type=jnp.float32,
    )
    return (back, jnp.zeros_like(matrix))


def pair_plain(query, keys):
    return jnp.einsum(
        "hqd,hkd->hqk",
        query.astype(jnp.bfloat16),
        keys.astype(jnp.bfloat16),
        preferred_element_type=jnp.float32,
    )


def pair_keep(query, keys):
    return (pair_plain(query, keys), (query.astype(jnp.bfloat16), keys.astype(jnp.bfloat16)))


def pair_back(kept, grad):
    query, keys = kept
    rounded = grad.astype(jnp.bfloat16)
    return (
        jnp.einsum("hqk,hkd->hqd", rounded, keys, preferred_element_type=jnp.float32),
        jnp.einsum("hqk,hqd->hkd", rounded, query, preferred_element_type=jnp.float32),
    )


def weigh_plain(probs, values):
    return jnp.einsum(
        "hqk,hkd->hqd",
        probs.astype(jnp.bfloat16),
        values.astype(jnp.bfloat16),
        preferred_element_type=jnp.float32,
    )


def weigh_keep(probs, values):
    return (weigh_plain(probs, values), (probs.astype(jnp.bfloat16), values.astype(jnp.bfloat16)))


def weigh_back(kept, grad):
    probs, values = kept
    rounded = grad.astype(jnp.bfloat16)
    return (
        jnp.einsum("hqd,hkd->hqk", rounded, values, preferred_element_type=jnp.float32),
        jnp.einsum("hqk,hqd->hkd", probs, rounded, preferred_element_type=jnp.float32),
    )


def relative_plain(query, table):
    return jnp.einsum(
        "hqd,rd->hqr",
        query.astype(jnp.bfloat16),
        table.astype(jnp.bfloat16),
        preferred_element_type=jnp.float32,
    )


def relative_keep(query, table):
    return (relative_plain(query, table), (query.astype(jnp.bfloat16), table.astype(jnp.bfloat16)))


def relative_back(kept, grad):
    query, table = kept
    rounded = grad.astype(jnp.bfloat16)
    return (
        jnp.einsum("hqr,rd->hqd", rounded, table, preferred_element_type=jnp.float32),
        jnp.einsum("hqr,hqd->rd", rounded, query, preferred_element_type=jnp.float32),
    )


def make_tools():
    rounder = jax.custom_vjp(round_plain)
    rounder.defvjp(round_keep, round_pass)
    back_rounder = jax.custom_vjp(pass_plain)

    def back_round(kept, grad):
        return (rounder(grad),)

    back_rounder.defvjp(pass_keep, back_round)
    project = jax.custom_vjp(project_plain)
    project.defvjp(project_keep, project_back)
    pair_scores = jax.custom_vjp(pair_plain)
    pair_scores.defvjp(pair_keep, pair_back)
    weigh_values = jax.custom_vjp(weigh_plain)
    weigh_values.defvjp(weigh_keep, weigh_back)
    relative = jax.custom_vjp(relative_plain)
    relative.defvjp(relative_keep, relative_back)
    return (rounder, back_rounder, project, pair_scores, weigh_values, relative)


def layer_norm(state, gain, shift):
    center = state - jnp.mean(state, axis=-1, keepdims=True)
    spread = jnp.mean(center * center, axis=-1, keepdims=True)
    return center * lax.rsqrt(spread + 1e-05) * gain + shift


def causal(signal, kernel):
    steps = signal.shape[0]
    taps = kernel.shape[0]
    padded = jnp.pad(signal, ((taps - 1, 0), (0, 0)))
    total = kernel[0] * padded[0:steps]
    for offset in range(1, taps):
        total = total + kernel[offset] * padded[offset : offset + steps]
    return total


def spread_offsets(rel, steps, table_rows):
    span = 2 * steps - 1
    offsets = jnp.arange(span, dtype=jnp.int32) - (steps - 1)
    rows_for = jnp.clip(offsets, -LEFT, RIGHT) + LEFT
    picker = (jnp.arange(table_rows, dtype=jnp.int32)[:, None] == rows_for[None, :]).astype(
        jnp.float32
    )
    widened = jnp.einsum("hqr,rm->hqm", rel, picker, precision=lax.Precision.HIGHEST)
    heads = rel.shape[0]
    flat = widened.reshape(heads, steps * span)
    skewed = flat[:, steps - 1 : steps - 1 + steps * (span - 1)].reshape(heads, steps, span - 1)
    return skewed[:, :, :steps]


def layer_forward(state, small, probes, large, valid, tools):
    low, low_back, project, pair_scores, weigh_values, relative = tools
    gains, shifts, inner_bias, outer_bias, packed_bias, mixed_bias, table, kernel = small
    inner_full, outer_full, packed_full, mixed_full, widen_full, narrow_full = large
    steps, width = state.shape
    saved = []

    def feed(inputs, norm, layer, probe_in, probe_out):
        hidden = low(layer_norm(inputs, gains[norm], shifts[norm]))
        pre = low_back(project(hidden, inner_full[layer]) + inner_bias[layer] + probe_in)
        active = low(jax.nn.silu(pre))
        saved.append(hidden.astype(jnp.bfloat16))
        saved.append(active.astype(jnp.bfloat16))
        return low_back(project(active, outer_full[layer]) + outer_bias[layer] + probe_out)

    first = state + 0.5 * feed(state, 0, 0, probes[0], probes[1])
    hidden = low(layer_norm(first, gains[1], shifts[1]))
    zeros = jnp.zeros((width,), jnp.float32)
    bias_full = jnp.concatenate([packed_bias[0], zeros, packed_bias[1]])
    packed = low(low_back(project(hidden, packed_full) + bias_full + probes[2]))
    heads = HEADS
    size = width // heads
    block = min(4, heads)
    split = packed.reshape(steps, 3, heads // block, block, size).transpose(2, 1, 3, 0, 4)
    table_rows = table.shape[0]

    def head_block(part):
        query, keys, values = (part[0], part[1], part[2])
        rel = low_back(relative(query, table))
        rel_full = spread_offsets(rel, steps, table_rows)
        scores = low_back((pair_scores(query, keys) + rel_full) * (1.0 / math.sqrt(size)))
        scores = jnp.where(valid[None, None, :] > 0, scores, -1e30)
        probs = low(jax.nn.softmax(scores, axis=-1))
        return low(low_back(weigh_values(probs, values)))

    mixed = lax.map(jax.checkpoint(head_block), split)
    mixed = mixed.reshape(heads, steps, size).transpose(1, 0, 2).reshape(steps, width)
    saved.append(hidden.astype(jnp.bfloat16))
    saved.append(mixed.astype(jnp.bfloat16))
    second = first + low_back(project(mixed, mixed_full) + mixed_bias + probes[3])
    chid = low(layer_norm(second, gains[2], shifts[2]))
    upward = low_back(project(chid, widen_full) + probes[4])
    glu = upward[:, :width] * jax.nn.sigmoid(upward[:, width:]) * valid[:, None]
    depth = causal(glu, kernel)
    cact = low(jax.nn.silu(layer_norm(depth, gains[3], shifts[3])))
    saved.append(chid.astype(jnp.bfloat16))
    saved.append(cact.astype(jnp.bfloat16))
    third = second + low_back(project(cact, narrow_full) + probes[5])
    fourth = third + 0.5 * feed(third, 4, 1, probes[6], probes[7])
    result = layer_norm(fourth, gains[5], shifts[5]) * valid[:, None]
    return (result, tuple(saved))


def contract_rows(inputs, grad):
    return lax.dot_general(
        inputs,
        grad.astype(jnp.bfloat16),
        (((0,), (0,)), ((), ())),
        preferred_element_type=jnp.float32,
    )


def local(
    tokens,
    lengths,
    cotangent,
    norm_gain,
    norm_shift,
    feed_in,
    feed_in_bias,
    feed_out,
    feed_out_bias,
    attention_in,
    attention_in_bias,
    attention_out,
    attention_out_bias,
    relative_table,
    pointwise_in,
    depthwise,
    pointwise_out,
):
    tools = make_tools()
    gathered = (
        lax.all_gather(norm_gain, "shard", axis=1, tiled=True),
        lax.all_gather(norm_shift, "shard", axis=1, tiled=True),
        lax.all_gather(feed_in, "shard", axis=1, tiled=True),
        lax.all_gather(feed_in_bias, "shard", axis=1, tiled=True),
        lax.all_gather(feed_out, "shard", axis=1, tiled=True),
        lax.all_gather(feed_out_bias, "shard", axis=1, tiled=True),
        lax.all_gather(attention_in, "shard", axis=0, tiled=True),
        lax.all_gather(attention_in_bias, "shard", axis=1, tiled=True),
        lax.all_gather(attention_out, "shard", axis=0, tiled=True),
        lax.all_gather(attention_out_bias, "shard", axis=0, tiled=True),
        lax.all_gather(pointwise_in, "shard", axis=0, tiled=True),
        lax.all_gather(depthwise, "shard", axis=1, tiled=True),
        lax.all_gather(pointwise_out, "shard", axis=0, tiled=True),
    )
    steps, width = tokens.shape
    valid = (jnp.arange(steps, dtype=jnp.int32) < lengths[0]).astype(jnp.float32)
    small = (
        gathered[0].astype(jnp.float32),
        gathered[1].astype(jnp.float32),
        gathered[3].astype(jnp.float32),
        gathered[5].astype(jnp.float32),
        gathered[7].astype(jnp.float32),
        gathered[9].astype(jnp.float32),
        relative_table.astype(jnp.float32),
        gathered[11].astype(jnp.float32),
    )
    large = (gathered[2], gathered[4], gathered[6], gathered[8], gathered[10], gathered[12])
    hidden_units = gathered[2].shape[2]
    probes = (
        jnp.zeros((steps, hidden_units), jnp.float32),
        jnp.zeros((steps, width), jnp.float32),
        jnp.zeros((steps, 3 * width), jnp.float32),
        jnp.zeros((steps, width), jnp.float32),
        jnp.zeros((steps, 2 * width), jnp.float32),
        jnp.zeros((steps, width), jnp.float32),
        jnp.zeros((steps, hidden_units), jnp.float32),
        jnp.zeros((steps, width), jnp.float32),
    )

    def local_layer(state, small_set, probe_set):
        return layer_forward(state, small_set, probe_set, large, valid, tools)

    result, pullback, saved = jax.vjp(
        local_layer, tokens.astype(jnp.float32), small, probes, has_aux=True
    )
    token_grad, small_grad, probe_grad = pullback(cotangent.astype(jnp.float32))
    weight_grad = [contract_rows(saved[slot], probe_grad[slot]) for slot in range(8)]
    full = [
        small_grad[0],
        small_grad[1],
        jnp.stack([weight_grad[0], weight_grad[6]]),
        small_grad[2],
        jnp.stack([weight_grad[1], weight_grad[7]]),
        small_grad[3],
        weight_grad[2],
        small_grad[4],
        weight_grad[3],
        small_grad[5],
        weight_grad[4],
        small_grad[7],
        weight_grad[5],
    ]
    pieces = (
        lax.psum_scatter(
            full[0].astype(jnp.bfloat16), "shard", scatter_dimension=1, tiled=True
        ).astype(jnp.float32),
        lax.psum_scatter(
            full[1].astype(jnp.bfloat16), "shard", scatter_dimension=1, tiled=True
        ).astype(jnp.float32),
        lax.psum_scatter(
            full[2].astype(jnp.bfloat16), "shard", scatter_dimension=1, tiled=True
        ).astype(jnp.float32),
        lax.psum_scatter(
            full[3].astype(jnp.bfloat16), "shard", scatter_dimension=1, tiled=True
        ).astype(jnp.float32),
        lax.psum_scatter(
            full[4].astype(jnp.bfloat16), "shard", scatter_dimension=1, tiled=True
        ).astype(jnp.float32),
        lax.psum_scatter(
            full[5].astype(jnp.bfloat16), "shard", scatter_dimension=1, tiled=True
        ).astype(jnp.float32),
        lax.psum_scatter(
            full[6].astype(jnp.bfloat16), "shard", scatter_dimension=0, tiled=True
        ).astype(jnp.float32),
        lax.psum_scatter(
            full[7].astype(jnp.bfloat16), "shard", scatter_dimension=1, tiled=True
        ).astype(jnp.float32),
        lax.psum_scatter(
            full[8].astype(jnp.bfloat16), "shard", scatter_dimension=0, tiled=True
        ).astype(jnp.float32),
        lax.psum_scatter(
            full[9].astype(jnp.bfloat16), "shard", scatter_dimension=0, tiled=True
        ).astype(jnp.float32),
        lax.psum_scatter(
            full[10].astype(jnp.bfloat16), "shard", scatter_dimension=0, tiled=True
        ).astype(jnp.float32),
        lax.psum_scatter(
            full[11].astype(jnp.bfloat16), "shard", scatter_dimension=1, tiled=True
        ).astype(jnp.float32),
        lax.psum_scatter(
            full[12].astype(jnp.bfloat16), "shard", scatter_dimension=0, tiled=True
        ).astype(jnp.float32),
    )
    reduced = (
        lax.psum(pieces[0].astype(jnp.bfloat16), "rep").astype(jnp.float32),
        lax.psum(pieces[1].astype(jnp.bfloat16), "rep").astype(jnp.float32),
        lax.psum(pieces[2].astype(jnp.bfloat16), "rep").astype(jnp.float32),
        lax.psum(pieces[3].astype(jnp.bfloat16), "rep").astype(jnp.float32),
        lax.psum(pieces[4].astype(jnp.bfloat16), "rep").astype(jnp.float32),
        lax.psum(pieces[5].astype(jnp.bfloat16), "rep").astype(jnp.float32),
        lax.psum(pieces[6].astype(jnp.bfloat16), "rep").astype(jnp.float32),
        lax.psum(pieces[7].astype(jnp.bfloat16), "rep").astype(jnp.float32),
        lax.psum(pieces[8].astype(jnp.bfloat16), "rep").astype(jnp.float32),
        lax.psum(pieces[9].astype(jnp.bfloat16), "rep").astype(jnp.float32),
        lax.psum(pieces[10].astype(jnp.bfloat16), "rep").astype(jnp.float32),
        lax.psum(pieces[11].astype(jnp.bfloat16), "rep").astype(jnp.float32),
        lax.psum(pieces[12].astype(jnp.bfloat16), "rep").astype(jnp.float32),
    )
    table_grad = lax.psum(small_grad[6], ("rep", "shard"))
    return (
        result.astype(jnp.bfloat16),
        token_grad.astype(jnp.bfloat16),
        reduced[0],
        reduced[1],
        reduced[2],
        reduced[3],
        reduced[4],
        reduced[5],
        reduced[6],
        reduced[7],
        reduced[8],
        reduced[9],
        table_grad,
        reduced[10],
        reduced[11],
        reduced[12],
    )


def solution(mesh):
    placed = (
        P(("rep", "shard"), None),
        P(("rep", "shard")),
        P(("rep", "shard"), None),
        P(None, "shard"),
        P(None, "shard"),
        P(None, "shard", None),
        P(None, "shard"),
        P(None, "shard", None),
        P(None, "shard"),
        P("shard", None),
        P(None, "shard"),
        P("shard", None),
        P("shard"),
        P(),
        P("shard", None),
        P(None, "shard"),
        P("shard", None),
    )
    return jax.shard_map(
        local,
        mesh=mesh,
        in_specs=placed,
        out_specs=(
            P(("rep", "shard"), None),
            P(("rep", "shard"), None),
            P(None, "shard"),
            P(None, "shard"),
            P(None, "shard", None),
            P(None, "shard"),
            P(None, "shard", None),
            P(None, "shard"),
            P("shard", None),
            P(None, "shard"),
            P("shard", None),
            P("shard"),
            P(),
            P("shard", None),
            P(None, "shard"),
            P("shard", None),
        ),
        check_vma=False,
    )
```

profile of v0, /device:TPU:0, one launch (start us, length us, event | category | flops | bytes accessed | tf_op | source)
XLA Modules:
  0.0 2819.3 jit_solution(11395793174473698642)
XLA Ops:
  11.3 28.4 %all_gather.49 = bf16[31,1024]{1,0:T(8,128)(2,1)S(1)} all-gather(bf16[31,128]{1,0:T(8,128)(2,1)S(1)} %copy-done.124), channel_id=1, replica_groups=mesh['rep'=4,'shard'=8] {'shard'}, dimensions={1}, use_global_device_ids=true | all-gather | bytes 71424 | tf_op jit(solution)/shard_map/all_gather | solution.py:261
  41.0 26.5 all_gather.39
  68.9 26.4 all_gather.40
  96.4 26.4 all_gather.42
  123.5 16.6 all_gather.44
  140.7 19.7 all_gather.46
  161.0 17.2 all-gather
  179.4 62.6 %all-gather.8.cloned.1.call-done = bf16[2,1024,4096]{2,1,0:T(8,128)(2,1)} async-done(((bf16[2,128,4096]{2,1,0:T(8,128)(2,1)}), bf16[2,1024,4096]{2,1,0:T(8,128)(2,1)}) %all-gather.8.cloned.1.call-update) | async-done | bytes 16777232 | tf_op jit(solution)/shard_map/all_gather | solution.py:252
  252.8 217.2 %all-gather.10.cloned.1.call-done = bf16[2,4096,1024]{2,1,0:T(8,128)(2,1)} async-done(((bf16[2,512,1024]{2,1,0:T(8,128)(2,1)}), bf16[2,4096,1024]{2,1,0:T(8,128)(2,1)}) %all-gather.10.cloned.1.call-update) | async-done | bytes 16777232 | tf_op jit(solution)/shard_map/all_gather | solution.py:254
  480.1 89.4 %all-gather.12.cloned.1.call-done = bf16[1024,3072]{1,0:T(8,128)(2,1)} async-done(((bf16[128,3072]{1,0:T(8,128)(2,1)}), bf16[1024,3072]{1,0:T(8,128)(2,1)}) %all-gather.12.cloned.1.call-update) | async-done | bytes 6291472 | tf_op jit(solution)/shard_map/all_gather | solution.py:256
  585.6 291.0 %while.29 = (s32[]{:T(128)}, bf16[4,4,512,64]{2,3,1,0:T(8,128)(2,1)}, bf16[4,3,4,512,64]{3,4,2,1,0:T(8,128)(2,1)}, bf16[73,64]{0,1:T(8,128)(2,1)S(1)}, s32[1023]...) while((s32[]{:T(128)}, bf16[4,4,512,64]{2,3,1,0:T(8,128)(2,1)}, ...), condition=%wide.region_7.8_spmd.clone, body=%wide.region_4.7_spmd.clone.sunk | while | flops 2130635136 | bytes 97088592 | solution.py:202
  596.4 15.0 reshape.627
  620.7 15.8 reshape.628
  667.4 15.0 reshape.627
  691.7 15.8 reshape.628
  737.9 15.0 reshape.627
  762.2 15.8 reshape.628
  808.3 15.0 reshape.627
  832.6 15.8 reshape.628
  984.1 19.6 pad_add_fusion
  1039.1 562.2 %while.30 = (s32[]{:T(128)}, f32[73,64]{0,1:T(8,128)S(1)}, bf16[4,3,4,512,64]{3,4,2,0,1:T(8,128)(2,1)}, bf16[4,3,4,512,64]{3,4,2,1,0:T(8,128)(2,1)}, bf16[4,4,51...) while((s32[]{:T(128)}, f32[73,64]{0,1:T(8,128)S(1)}, ...), condition=%wide.region_28.29_spmd.clone, body=%wide.region_24.28_spmd.clone.sunk | while | flops 4424472576 | bytes 243012752 | solution.py:202
  1047.9 15.0 reshape.629
  1072.4 15.9 reshape.630
  1125.3 15.0 reshape.631
  1149.7 15.8 reshape.632
  1186.8 15.2 reshape.629
  1211.4 15.8 reshape.630
  1264.1 14.9 reshape.631
  1288.4 15.8 reshape.632
  1325.5 14.9 reshape.629
  1349.8 15.7 reshape.630
  1402.2 14.9 reshape.631
  1426.5 15.8 reshape.632
  1463.6 14.9 reshape.629
  1487.9 15.7 reshape.630
  1540.3 14.9 reshape.631
  1564.7 15.8 reshape.632
  1699.6 25.9 reduce-scatter.29.cloned.1.call-done
  1725.5 285.4 %reduce-scatter.27.cloned.1.call-done = bf16[2,512,1024]{2,1,0:T(8,128)(2,1)} async-done(((bf16[2,4096,1024]{2,1,0:T(8,128)(2,1)}), bf16[2,512,1024]{2,1,0:T(8,128)(2,1)}) %reduce-scatter.27.cloned.1.call-update) | async-done | bytes 2097168 | tf_op jit(solution)/shard_map/reduce_scatter | solution.py:325
  2010.9 284.7 %reduce-scatter.25.cloned.1.call-done = bf16[2,128,4096]{2,1,0:T(8,128)(2,1)} async-done(((bf16[2,1024,4096]{2,1,0:T(8,128)(2,1)}), bf16[2,128,4096]{2,1,0:T(8,128)(2,1)}) %reduce-scatter.25.cloned.1.call-update) | async-done | bytes 2097168 | tf_op jit(solution)/shard_map/reduce_scatter | solution.py:319
  2298.9 19.6 all-reduce.88
  2318.6 37.6 %psum.108 = f32[73,64]{0,1:T(8,128)} all-reduce(f32[73,64]{0,1:T(8,128)S(1)} %get-tuple-element.220), channel_id=1, replica_groups=mesh['rep'=4,'shard'=8] {'rep','shard'}, use_global_device_ids=true, to_apply=%region_71.72 | all-reduce | flops 4672 | bytes 37376 | tf_op jit(solution)/shard_map/psum | solution.py:368
  2360.5 63.6 %reduce-scatter.43.cloned.1.call-done = bf16[128,2]{1,0:T(8,128)(2,1)} async-done(((bf16[1024,2]{1,0:T(8,128)(2,1)}), bf16[128,2]{1,0:T(8,128)(2,1)}) %reduce-scatter.43.cloned.1.call-update) | async-done | bytes 528
  2424.8 63.6 %reduce-scatter.39.cloned.1.call-done = bf16[128,6]{1,0:T(8,128)(2,1)} async-done(((bf16[1024,6]{1,0:T(8,128)(2,1)}), bf16[128,6]{1,0:T(8,128)(2,1)}) %reduce-scatter.39.cloned.1.call-update) | async-done | bytes 1552
  2489.3 63.5 %reduce-scatter.37.cloned.1.call-done = bf16[128,6]{1,0:T(8,128)(2,1)} async-done(((bf16[1024,6]{1,0:T(8,128)(2,1)}), bf16[128,6]{1,0:T(8,128)(2,1)}) %reduce-scatter.37.cloned.1.call-update) | async-done | bytes 1552
  2553.6 65.8 %reduce-scatter.41.cloned.1.call-done = bf16[512,2]{1,0:T(8,128)(2,1)} async-done(((bf16[4096,2]{1,0:T(8,128)(2,1)}), bf16[512,2]{1,0:T(8,128)(2,1)}) %reduce-scatter.41.cloned.1.call-update) | async-done | bytes 2064
  2620.4 63.0 %reduce-scatter.47.cloned.1.call-done = bf16[128,31]{1,0:T(8,128)(2,1)} async-done(((bf16[1024,31]{1,0:T(8,128)(2,1)}), bf16[128,31]{1,0:T(8,128)(2,1)}) %reduce-scatter.47.cloned.1.call-update) | async-done | bytes 7952
  2698.9 102.6 %all-reduce.93.cloned.1.call-done = (bf16[2,128,4096]{2,1,0:T(8,128)(2,1)}, bf16[2,512,1024]{2,1,0:T(8,128)(2,1)}, bf16[128,3072]{1,0:T(8,128)(2,1)}, bf16[128,1...) async-done(((bf16[2,128,4096]{2,1,0:T(8,128)(2,1)}, bf16[2,512,1024]{2,1,0:T(8,128)(2,1)}, bf16[128,3072]{1,0:T(8,128)(2,1)}, ...) | async-done | bytes 6029328 | tf_op jit(solution)/shard_map/psum | solution.py:356
  (646 shorter events, 787.7 us)
Async XLA Ops:
  7.2 234.8 %all-gather.8.cloned.1.call-start = ((), (), s32[]{:S(2)}) async-start(), calls=%async_computation.12 | async-start | bytes 18874368 | tf_op jit(solution)/shard_map/all_gather | solution.py:252
  7.9 33.1 %copy-start.133 = (bf16[6,128]{1,0:T(8,128)(2,1)S(1)}, bf16[6,128]{1,0:T(8,128)(2,1)}, u32[]{:S(2)}) copy-start(bf16[6,128]{1,0:T(8,128)(2,1)} %param.24) | copy-start | bytes 4612
  7.9 60.2 %copy-start.8 = (bf16[512,1024]{1,0:T(8,128)(2,1)S(1)}, bf16[512,1024]{1,0:T(8,128)(2,1)}, u32[]{:S(2)}) copy-start(bf16[512,1024]{1,0:T(8,128)(2,1)} %param.21) | copy-start | bytes 3145732
  7.9 462.1 %all-gather.10.cloned.1.call-start = ((), (), s32[]{:S(2)}) async-start(), calls=%async_computation.13 | async-start | bytes 18874368 | tf_op jit(solution)/shard_map/all_gather | solution.py:254
  8.7 60.2 %copy-start.134 = (bf16[6,128]{1,0:T(8,128)(2,1)S(1)}, bf16[6,128]{1,0:T(8,128)(2,1)}, u32[]{:S(2)}) copy-start(bf16[6,128]{1,0:T(8,128)(2,1)} %param.25) | copy-start | bytes 4612
  8.7 560.7 %all-gather.12.cloned.1.call-start = ((), (), s32[]{:S(2)}) async-start(), calls=%async_computation.14 | async-start | bytes 7077888 | tf_op jit(solution)/shard_map/all_gather | solution.py:256
  9.4 867.2 %all-gather.14.cloned.1.call-start = ((), (), s32[]{:S(2)}) async-start(), calls=%async_computation.15 | async-start | bytes 2359296 | tf_op jit(solution)/shard_map/all_gather | solution.py:258
  10.0 871.8 %all-gather.16.cloned.1.call-start = ((), (), s32[]{:S(2)}) async-start(), calls=%async_computation.16 | async-start | bytes 4718592 | tf_op jit(solution)/shard_map/all_gather | solution.py:260
  10.6 891.9 %all-gather.18.cloned.1.call-start = ((), (), s32[]{:S(2)}) async-start(), calls=%async_computation.17 | async-start | bytes 2359296 | tf_op jit(solution)/shard_map/all_gather | solution.py:262
  11.2 1688.3 %reduce-scatter.31.cloned.1.call-start = ((), (), s32[]{:S(2)}) async-start(), calls=%async_computation.21 | async-start | bytes 2359296 | tf_op jit(solution)/shard_map/reduce_scatter | solution.py:337
  68.1 27.8 copy-start.45
  68.1 411.5 %copy-start.83 = (f32[1,1024]{1,0:T(1,128)}, f32[1,1024]{1,0:T(1,128)S(1)}, u32[]{:S(2)}) copy-start(f32[1,1024]{1,0:T(1,128)S(1)} %get-tuple-element.478) | copy-start | bytes 12292
  68.2 28.2 %copy-start.135 = (bf16[2,512]{1,0:T(2,128)(2,1)S(1)}, bf16[2,512]{1,0:T(2,128)(2,1)}, u32[]{:S(2)}) copy-start(bf16[2,512]{1,0:T(2,128)(2,1)} %param.27) | copy-start | bytes 6148
  68.2 55.3 %copy-start.136 = (bf16[2,128]{1,0:T(2,128)(2,1)S(1)}, bf16[2,128]{1,0:T(2,128)(2,1)}, u32[]{:S(2)}) copy-start(bf16[2,128]{1,0:T(2,128)(2,1)} %param.29) | copy-start | bytes 1540
  68.2 72.5 %copy-start.137 = (bf16[2,128]{1,0:T(2,128)(2,1)S(1)}, bf16[2,128]{1,0:T(2,128)(2,1)}, u32[]{:S(2)}) copy-start(bf16[2,128]{1,0:T(2,128)(2,1)} %param.31) | copy-start | bytes 1540
  68.2 92.8 %copy-start.138 = (bf16[128]{0:T(256)(128)(2,1)S(1)}, bf16[128]{0:T(256)(128)(2,1)}, u32[]{:S(2)}) copy-start(bf16[128]{0:T(256)(128)(2,1)} %param.33) | copy-start | bytes 772
  68.4 27.5 copy-start.48
  68.8 27.1 copy-start.95
  68.9 27.0 copy-start.89
  96.4 156.4 %copy-start.35 = (bf16[512,1024]{1,0:T(8,128)(2,1)}, bf16[512,1024]{1,0:T(8,128)(2,1)S(1)}, u32[]{:S(2)}) copy-start(bf16[512,1024]{1,0:T(8,128)(2,1)S(1)} %fusion.55) | copy-start | bytes 3145732
  123.5 129.3 %copy-start.120 = (f32[1,4096]{1,0:T(1,128)}, f32[1,4096]{1,0:T(1,128)S(1)}, u32[]{:S(2)}) copy-start(f32[1,4096]{1,0:T(1,128)S(1)} %get-tuple-element.487) | copy-start | bytes 49156
  478.4 398.3 %copy-start.14 = (f32[512,1024]{1,0:T(8,128)}, f32[512,1024]{1,0:T(8,128)S(1)}, u32[]{:S(2)}) copy-start(f32[512,1024]{1,0:T(8,128)S(1)} %get-tuple-element.495) | copy-start | bytes 6291460
  480.1 96.9 %copy-start.37 = (bf16[512,1024]{1,0:T(8,128)(2,1)}, bf16[512,1024]{1,0:T(8,128)(2,1)S(1)}, u32[]{:S(2)}) copy-start(bf16[512,1024]{1,0:T(8,128)(2,1)S(1)} %add_convert_fusion.5) | copy-start | bytes 3145732
  585.6 291.0 %copy-start.131 = (f32[8,1,128]{2,1,0:T(1,128)S(1)}, f32[8,1,128]{2,1,0:T(1,128)}, u32[]{:S(2)}) copy-start(f32[8,1,128]{2,1,0:T(1,128)} %convert_element_type.477) | copy-start | bytes 12292
  889.3 88.1 %copy-start.4 = (f32[512,1024]{1,0:T(8,128)}, f32[512,1024]{1,0:T(8,128)S(1)}, u32[]{:S(2)}) copy-start(f32[512,1024]{1,0:T(8,128)S(1)} %multiply_multiply_fusion) | copy-start | bytes 6291460
  907.5 10.3 copy-start.132
  930.1 9.3 copy-start.27
  939.4 10.0 copy-start.21
  957.2 20.2 copy-start.2
  957.2 20.2 copy-start.50
  1019.7 14.5 copy-start.20
  1023.9 675.6 %reduce-scatter.35.cloned.1.call-start = ((), (), s32[]{:S(2)}) async-start(), calls=%async_computation.23 | async-start | bytes 2359296 | tf_op jit(solution)/shard_map/reduce_scatter | solution.py:349
  1028.3 671.2 %reduce-scatter.33.cloned.1.call-start = ((), (), s32[]{:S(2)}) async-start(), calls=%async_computation.22 | async-start | bytes 4718592 | tf_op jit(solution)/shard_map/reduce_scatter | solution.py:343
  1034.1 691.4 %reduce-scatter.29.cloned.1.call-start = ((), (), s32[]{:S(2)}) async-start(), calls=%async_computation.20 | async-start | bytes 7077888 | tf_op jit(solution)/shard_map/reduce_scatter | solution.py:331
  1609.7 8.7 copy-start.98
  1609.7 401.2 %reduce-scatter.27.cloned.1.call-start = ((), (), s32[]{:S(2)}) async-start(), calls=%async_computation.19 | async-start | bytes 18874368 | tf_op jit(solution)/shard_map/reduce_scatter | solution.py:325
  1640.4 655.2 %reduce-scatter.25.cloned.1.call-start = ((), (), s32[]{:S(2)}) async-start(), calls=%async_computation.18 | async-start | bytes 18874368 | tf_op jit(solution)/shard_map/reduce_scatter | solution.py:319
  1641.1 10.6 copy-start.22
  1641.1 10.6 copy-start.39
  1668.2 691.4 %reduce-scatter.45.cloned.1.call-start = ((), (), s32[]{:S(2)}) async-start(), calls=%async_computation.28 | async-start | bytes 294912
  1672.1 9.7 copy-start.96
  1672.1 9.7 copy-start.25
  1692.4 731.6 %reduce-scatter.43.cloned.1.call-start = ((), (), s32[]{:S(2)}) async-start(), calls=%async_computation.27 | async-start | bytes 294912
  1693.4 795.0 %reduce-scatter.39.cloned.1.call-start = ((), (), s32[]{:S(2)}) async-start(), calls=%async_computation.25 | async-start | bytes 294912
  1694.5 858.3 %reduce-scatter.37.cloned.1.call-start = ((), (), s32[]{:S(2)}) async-start(), calls=%async_computation.24 | async-start | bytes 294912
  1696.6 922.7 %reduce-scatter.41.cloned.1.call-start = ((), (), s32[]{:S(2)}) async-start(), calls=%async_computation.26 | async-start | bytes 1179648
  1698.1 985.3 %reduce-scatter.47.cloned.1.call-start = ((), (), s32[]{:S(2)}) async-start(), calls=%async_computation.29 | async-start | bytes 294912
  1699.4 1102.1 %all-reduce.93.cloned.1.call-start = ((), (), s32[]{:S(2)}) async-start(), calls=%async_computation.30 | async-start | bytes 12058624 | tf_op jit(solution)/shard_map/psum | solution.py:356
  (128 other events, 344.5 us)
Sparse Core Ops, SparseCore 0:
  10.2 231.7 all-gather.7
  244.2 225.7 all-gather.9
  472.2 97.2 all-gather.11
  571.4 47.6 all-gather.13
  621.1 71.8 all-gather.15
  695.0 47.5 all-gather.17
  1024.0 65.3 reduce-scatter.30
  1093.0 66.5 reduce-scatter.34
  1163.7 86.9 reduce-scatter.32
  1609.8 115.6 reduce-scatter.28
  1729.8 281.1 reduce-scatter.26
  2014.6 280.9 reduce-scatter.24
  2299.3 60.2 reduce-scatter.44
  2363.8 60.2 reduce-scatter.42
  2428.1 60.2 reduce-scatter.38
  2492.5 60.1 reduce-scatter.36
  2557.0 62.3 reduce-scatter.40
  2623.1 60.2 reduce-scatter.46
  2686.1 115.2 all-reduce.92
where the time goes:
time: 2830 us; the launch traced here: 2820 us
  waiting for transfers between devices  1390 us (49%)
  local copies, waits for them, and re-layouts  674 us (24%)
  matrix products  317 us (11%)
  blocking collectives  229 us (8%)
  other arithmetic  171 us (6%)
    unnamed x25, waiting for transfers between devices  324 us
    reduce_scatter x1, waiting for transfers between devices, local(): lax.psum_scatter(full[4].astype(jnp.bfloat16), 'shard', scatter_dimension...  285 us
    reduce_scatter x1, waiting for transfers between devices, local(): lax.psum_scatter(full[2].astype(jnp.bfloat16), 'shard', scatter_dimension...  285 us
    all_gather x1, waiting for transfers between devices, local(): lax.all_gather(feed_out, 'shard', axis=1, tiled=True)  217 us
    reshape x12, local copies, waits for them, and re-layouts, spread_offsets(): flat[:, steps - 1:steps - 1 + steps * (span - 1)]  186 us
    reshape x12, local copies, waits for them, and re-layouts, spread_offsets(): flat = widened.reshape(heads, steps * span)  183 us
    psum x1, waiting for transfers between devices, local(): lax.psum(pieces[2].astype(jnp.bfloat16), 'rep').astype(jnp.float32)  103 us
    dot_general x12, matrix products, spread_offsets(): jnp.einsum('hqr,rm->hqm', rel, picker, precision=lax.Precision.HIGHEST)  90.6 us
  transfers between devices with their start and end apart: 19, of which 13 were waited for; matrix products, arithmetic and copies ran while one was open for 36% of the time, Pallas kernels for 0%

commit v1 on v0

v1 whole, which is shorter than its diff:
```python
import functools, math
import numpy as np
import jax, jax.numpy as jnp
from jax import lax
from jax.experimental import pallas as pl
from jax.experimental.pallas import tpu as pltpu
from jax.sharding import PartitionSpec as P
LEFT=64; RIGHT=8
BF=jnp.bfloat16; F32=jnp.float32

def nn(a,b): return lax.dot_general(a,b,(((1,),(0,)),((),())),preferred_element_type=F32)
def nt(a,b): return lax.dot_general(a,b,(((1,),(1,)),((),())),preferred_element_type=F32)
def tn(a,b): return lax.dot_general(a,b,(((0,),(0,)),((),())),preferred_element_type=F32)

def picker_table(steps, block):
    span=steps+block
    n=np.arange(span)
    rows=[]
    for i in range(steps//block):
        off=np.where(n<steps, n, n-span)-block*i
        row=np.clip(off,-LEFT,RIGHT)+LEFT
        rows.append(np.arange(128)[:,None]==row[None,:])
    return np.stack(rows)

QB=128

MESH=pl.DeviceIdType.MESH
def al(v,m): return pl.multiple_of(v,m)
def during(lo,hi,body):
    def run(i,c):
        body(i); return c
    lax.fori_loop(lo,hi,run,0)

class Place:
    def __init__(self,S):
        self.S=S; self.Z=S//2
        r=lax.axis_index('rep'); s=lax.axis_index('shard')
        self.r,self.s=r,s
        self.c=lax.rem(r,2); self.x=lax.rem(r//2,2); self.y=lax.rem(s,2); self.z=s//2
        base=r-2*self.x-self.c
        self.d=1-2*self.c
        self.next=(r,2*self.zat(1)+self.y); self.prev=(r,2*self.zat(-1)+self.y)
        self.over_y=(r,2*self.z+1-self.y); self.over_x=(base+2*(1-self.x)+self.c,s); self.twin=(base+2*self.x+1-self.c,s)
    def zat(self,k): return lax.rem(self.z+self.d*k+2*self.Z,self.Z)
    def greet(self):
        bar=pltpu.get_barrier_semaphore()
        for dev in (self.next,self.prev,self.over_y,self.over_x,self.twin):
            pl.semaphore_signal(bar,inc=1,device_id=dev,device_id_type=MESH)
        pl.semaphore_wait(bar,5)

SUB=(128,512)
class Scatter:
    OWN=18; RING=6; GAP=2
    def __init__(self,S,sources,common=None):
        self.common=common
        self.S=S; Z=S//2
        counts=[a if isinstance(a,int) else a.shape[0] for a in sources]
        n=self.n=sum(counts)
        (rows,wide)=SUB
        h,q=rows//2,rows//4
        self.h,self.q,self.Z=h,q,Z
        self.made=[isinstance(a,int) for a in sources]
        self.at=np.cumsum([0]+counts).tolist(); self.counts=counts
        self.inputs=[a.reshape(a.shape[0],Z,2,2,h,wide) for a in sources if not isinstance(a,int)]
        self.out_shapes=[jax.ShapeDtypeStruct((n,rows,wide),BF)]+[jax.ShapeDtypeStruct((k,Z,2,2,h,wide),BF) for k,m in zip(counts,self.made) if m]
        G=self.GAP
        self.lag=[0]+[G*k for k in range(1,5+Z)]
        self.lag[4+Z]=self.lag[3+Z]+1
        self.lag.append(self.lag[4+Z]+1)
        self.ticks=n+self.lag[-1]
        own,ring=min(n,self.OWN),min(n,self.RING)
        self.slots=own; self.ring=ring
        assert own>=self.lag[-1] or own==n
        V=lambda *d: pltpu.VMEM(d,BF)
        self.scratch=[V(n,rows,wide),V(own,Z,2,h,wide),V(ring,Z,2,h,wide),V(ring,Z,q,wide),V(ring,Z,q,wide),V(ring,Z-1,h,wide),V(ring,h,wide),
            pltpu.SemaphoreType.DMA((n,)),pltpu.SemaphoreType.DMA((n,5+Z)),pltpu.SemaphoreType.DMA((n,5+Z)),pltpu.SemaphoreType.DMA((n,2)),pltpu.SemaphoreType.REGULAR((4+Z,))]
        if common:
            self.out_shapes.append(jax.ShapeDtypeStruct((Z,2,common[2],wide),BF))
            self.scratch+=[V(Z,2,common[2],wide),pltpu.SemaphoreType.DMA((Z,)),pltpu.SemaphoreType.DMA((Z,)),pltpu.SemaphoreType.DMA((1,))]
            self.begin_common=common[0]+self.lag[-1]+1
            self.ticks=max(self.ticks,self.begin_common+Z+1)
        self.out_specs=[pl.BlockSpec(memory_space=pl.ANY)]*len(self.out_shapes)
    def bind(self,ins,outs,scr):
        self.out=outs[0]; ins,made=list(ins),list(outs[1:1+sum(self.made)])
        self.makes=list(made)
        self.g=[made.pop(0) if m else ins.pop(0) for m in self.made]
        if self.common: self.all,self.cs,self.ct,self.co=scr[-4:]; self.all_out=outs[-1]; scr=scr[:-4]
        self.o,self.own,self.cr,self.xr,self.yr,self.zr,self.fr,self.os,self.ss,self.rs,self.ls,self.free=scr
        self.p=Place(self.S); return self
    def slot(self,i): return i if self.slots==self.n else lax.rem(i,self.slots)
    def land(self,i): return i if self.ring==self.n else lax.rem(i,self.ring)
    def remote(self,i,k,src,dst,dev):
        return pltpu.make_async_remote_copy(src,dst,self.ss.at[i,k],self.rs.at[i,k],device_id=dev,device_id_type=MESH)
    def column(self,yy): return 1-self.p.y if yy else self.p.y
    def first(self,ref,i,yy):
        return self.remote(i,yy,ref.at[:,self.column(yy),1-self.p.c],self.cr.at[self.land(i),:,self.column(yy)],self.p.twin)
    def load(self,ref,i,yy):
        return pltpu.make_async_copy(ref.at[:,self.column(yy),self.p.c],self.own.at[self.slot(i),:,self.column(yy)],self.ls.at[i,yy])
    def part(self,i,col,x): return self.own.at[self.slot(i),:,col,pl.ds(al(x*self.q,self.q),self.q)]
    def cross(self,i): return self.remote(i,2,self.part(i,1-self.p.y,1-self.p.x),self.xr.at[self.land(i)],self.p.over_x)
    def side(self,i): return self.remote(i,3,self.part(i,1-self.p.y,self.p.x),self.yr.at[self.land(i)],self.p.over_y)
    def hop(self,i,s): return self.remote(i,3+s,self.own.at[self.slot(i),self.p.zat(-s),self.p.y],self.zr.at[self.land(i),s-1],self.p.next)
    def swap(self,i): return self.remote(i,3+self.Z,self.own.at[self.slot(i),self.p.z,self.p.y],self.fr.at[self.land(i)],self.p.over_x)
    def half(self,i): return self.o.at[i,pl.ds(al(self.p.c*self.h,self.h),self.h)]
    def share(self,i): return self.remote(i,4+self.Z,self.half(i),self.half(i),self.p.twin)
    def save(self,i): return pltpu.make_async_copy(self.o.at[i],self.out.at[i],self.os.at[i])
    def ask(self,i,k):
        if self.ring<self.n:
            @pl.when(i>=self.ring)
            def _(): pl.semaphore_wait(self.free.at[k],1)
    def tell(self,i,k,dev):
        if self.ring<self.n:
            @pl.when(i<self.n-self.ring)
            def _(): pl.semaphore_signal(self.free.at[k],inc=1,device_id=dev,device_id_type=MESH)
    def begin(self): self.p.greet()
    def phase(self,k,i):
        p=self.p; Z=self.Z; some=self.g[0].at[0]; here=self.slot(i); land=self.land(i)
        if k==0:
            self.ask(i,0)
            for at,count,ref in zip(self.at,self.counts,self.g):
                @pl.when((i>=at)&(i<at+count))
                def _(at=at,ref=ref):
                    for yy in (1,0): self.first(ref.at[i-at],i,yy).start(); self.load(ref.at[i-at],i,yy).start()
        elif k==1:
            for yy in (1,0):
                col=self.column(yy)
                self.load(some,i,yy).wait(); self.first(some,i,yy).wait_recv()
                self.own[here,:,col]=self.own[here,:,col]+self.cr[land,:,col]
                if yy: self.ask(i,1); self.cross(i).start()
            self.tell(i,0,p.twin)
        elif k==2:
            self.cross(i).wait_recv()
            ref=self.part(i,1-p.y,p.x); ref[...]=ref[...]+self.xr[land]
            self.tell(i,1,p.over_x)
            self.ask(i,2); self.side(i).start()
        elif k==3:
            self.side(i).wait_recv()
            ref=self.part(i,p.y,p.x); ref[...]=ref[...]+self.yr[land]
            self.tell(i,2,p.over_y)
            self.ask(i,3); self.hop(i,1).start()
        elif k<3+Z:
            s=k-3
            self.hop(i,s).wait_recv()
            ref=self.own.at[here,p.zat(-1-s),p.y]; ref[...]=ref[...]+self.zr[land,s-1]
            self.tell(i,2+s,p.prev)
            self.ask(i,3+s)
            (self.hop(i,s+1) if s+1<Z else self.swap(i)).start()
        elif k==3+Z:
            self.swap(i).wait_recv()
            ref=self.half(i); ref[...]=self.own[here,p.z,p.y]+self.fr[land]
            self.tell(i,2+Z,p.over_x)
            self.share(i).start()
        elif k==4+Z:
            for yy in (0,1): self.first(some,i,yy).wait_send()
            self.cross(i).wait_send(); self.side(i).wait_send()
            for s in range(1,Z): self.hop(i,s).wait_send()
            self.swap(i).wait_send(); self.share(i).wait()
            self.save(i).start()
        else: self.save(i).wait()
    def relay(self,s):
        p=self.p
        ref=self.all.at[p.z,p.y] if s==0 else self.all.at[p.zat(1-s)]
        return pltpu.make_async_remote_copy(ref,ref,self.cs.at[s],self.ct.at[s],device_id=p.over_y if s==0 else p.next,device_id_type=MESH)
    def spread_common(self,k):
        p=self.p; unit,at,count=self.common
        if k==0: self.all[p.z,p.y]=self.o[unit,at:at+count]
        else: self.relay(k-1).wait()
        if k<self.Z: self.relay(k).start()
        else:
            cp=pltpu.make_async_copy(self.all,self.all_out,self.co.at[0]); cp.start(); cp.wait()
    def run(self,lo,count):
        def tick(u):
            for k in reversed(range(len(self.lag))):
                i=u-self.lag[k]
                @pl.when((i>=0)&(i<self.n))
                def _(k=k,i=i): self.phase(k,i)
            if self.common:
                for k in range(self.Z+1):
                    @pl.when(u==self.begin_common+k)
                    def _(k=k): self.spread_common(k)
        during(0,count,lambda v:tick(lo+v))
    def spread(self,step,steps):
        per=-(-self.ticks//steps)
        self.run(step*per,per)

class Gather:
    def __init__(self,S,shards,cuts=None,modes=None,lag=1,ahead=None):
        self.S=S; self.Z=S//2
        pick=lambda a: a if isinstance(a,tuple) else (a,None)
        self.local=[isinstance(a,tuple) and isinstance(a[0],int) for a in shards]
        pairs=[pick(a) for a,m in zip(shards,self.local) if not m]
        self.inputs=[]; self.source=[]
        for a,layer in pairs:
            k=next((k for k,v in enumerate(self.inputs) if v is a),None)
            if k is None: k=len(self.inputs); self.inputs.append(a)
            self.source.append((k,layer))
        self.shapes=[a if m else pick(a)[0].shape[-2:] for a,m in zip(shards,self.local)]
        self.cuts=cuts or [1]*len(shards)
        self.units=[(w,a) for w,k in enumerate(self.cuts) for a in range(k)]
        self.modes=[m for k,ms in zip(self.cuts,modes or ['h']*len(shards)) for m in (ms*k)[:k]]
        self.lag=lag; Z=self.Z
        n=len(self.units); k=6*Z-2+2*(Z-1)
        self.out_shapes=[jax.ShapeDtypeStruct((a*S,b),BF) for a,b in self.shapes]
        self.out_specs=[pl.BlockSpec(memory_space=pl.ANY)]*len(shards)
        self.scratch=[pltpu.VMEM(a,BF) for a,m in zip(self.shapes,self.local) if m]+[pltpu.SemaphoreType.DMA((n,k)),pltpu.SemaphoreType.DMA((n,k)),pltpu.SemaphoreType.DMA((n,))]
        D=lag
        self.plan={}
        add=lambda at,*stage: self.plan.setdefault(at,[]).append(stage)
        for t in range(1,Z): add(D*t,'z',t)
        for t in range(Z): add(D*(t+1),'y',t)
        for t in range(1,Z): add(D*(t+1),'u',t)
        for t in range(Z): add(D*(t+2),'x',t)
        add(D*(Z+2),'end',0)
        self.last=D*(Z+2)
        self.ahead=n if ahead is None else ahead
        self.ticks=n+self.last
    def bind(self,ins,outs,scr):
        mine=list(scr[:-3]); source=list(self.source); self.i=[]
        for m in self.local:
            if m: self.i.append(mine.pop(0))
            else:
                k,layer=source.pop(0)
                self.i.append(ins[k] if layer is None else ins[k].at[layer])
        self.o=outs; self.ss,self.rs,self.ls=scr[-3:]; self.p=Place(self.S); return self
    def cols(self,u):
        w,a=self.units[u]; wide=self.shapes[w][1]//self.cuts[w]
        return pl.ds(a*wide,wide)
    def rows(self,u,zo,yy,off,ln):
        w=self.units[u][0]; n=self.shapes[w][0]; q=n//4
        return self.o[w].at[pl.ds(al((2*zo+yy)*n+off*q,q),ln*q),self.cols(u)]
    def half(self,u,t): return self.rows(u,self.p.zat(-t),self.p.y,2*self.p.c,2)
    def quarter(self,u,t,yy,x): return self.rows(u,self.p.zat(-t),yy,2*self.p.c+x,1)
    def mine(self,u,off,ln):
        w=self.units[u][0]; q=self.shapes[w][0]//4
        return self.i[w].at[pl.ds(al(off*q,q),ln*q),self.cols(u)]
    def cp(self,u,kind,t):
        p=self.p; Z=self.Z; h=self.modes[u]=='h'
        k={'z':t-1,'y':Z-1+t,'x':2*Z-1+t,'cz':3*Z-1+t-1,'cy':4*Z-2+t,'cx':5*Z-2+t,'u':6*Z-2+t-1,'cu':7*Z-3+t-1}[kind]
        if kind=='z':
            dst=self.half(u,t-1) if h else self.quarter(u,t-1,p.y,p.x); src=dst; dev=p.next
            if t==1: src=self.mine(u,2*p.c,2) if h else self.mine(u,2*p.c+p.x,1)
        elif kind=='y': dst=self.quarter(u,t,p.y,p.x); src=self.mine(u,2*p.c+p.x,1) if t==0 else dst; dev=p.over_y
        elif kind=='x': src=dst=self.quarter(u,t,1-p.y,p.x); dev=p.over_x
        elif kind=='u': src=dst=self.quarter(u,t,p.y,p.x); dev=p.over_x
        elif kind=='cz': src=dst=self.half(u,t) if h else self.quarter(u,t,p.y,p.x); dev=p.twin
        elif kind=='cu': src=dst=self.quarter(u,t,p.y,1-p.x); dev=p.twin
        elif kind=='cy': src=dst=self.quarter(u,t,1-p.y,p.x); dev=p.twin
        else: src=dst=self.quarter(u,t,1-p.y,1-p.x); dev=p.twin
        return pltpu.make_async_remote_copy(src,dst,self.ss.at[u,k],self.rs.at[u,k],device_id=dev,device_id_type=MESH)
    def own(self,u):
        w=self.units[u][0]; n=self.shapes[w][0]
        return pltpu.make_async_copy(self.i[w].at[:,self.cols(u)],self.o[w].at[pl.ds(al(self.p.s*n,n),n),self.cols(u)],self.ls.at[u])
    def open(self,u):
        self.cp(u,'z',1).start(); self.cp(u,'y',0).start(); self.own(u).start()
    def begin(self):
        self.p.greet()
        for u in range(min(self.ahead,len(self.units))): self.open(u)
    def stage(self,u,kind,t):
        Z=self.Z; q=self.modes[u]=='q'
        if kind=='z':
            self.cp(u,'z',t).wait_recv()
            if t+1<Z: self.cp(u,'z',t+1).start()
            self.cp(u,'y',t).start()
            if q: self.cp(u,'u',t).start()
            self.cp(u,'cz',t).start()
        elif kind=='y':
            self.cp(u,'y',t).wait_recv()
            self.cp(u,'x',t).start(); self.cp(u,'cy',t).start()
        elif kind=='u':
            if q: self.cp(u,'u',t).wait_recv(); self.cp(u,'cu',t).start()
        elif kind=='x':
            self.cp(u,'x',t).wait_recv(); self.cp(u,'cx',t).start()
        else:
            for t in range(1,Z):
                self.cp(u,'z',t).wait_send(); self.cp(u,'cz',t).wait()
                if q: self.cp(u,'u',t).wait_send(); self.cp(u,'cu',t).wait()
            for t in range(Z):
                self.cp(u,'y',t).wait_send(); self.cp(u,'x',t).wait_send(); self.cp(u,'cy',t).wait(); self.cp(u,'cx',t).wait()
            self.own(u).wait()
    def run(self,lo,count):
        for i in range(lo,min(lo+count,self.ticks)):
            for u in range(len(self.units)):
                if u>=self.ahead and i==u-self.ahead: self.open(u)
            for u in range(len(self.units)):
                for s in self.plan.get(i-u,[]): self.stage(u,*s)
    def done(self,w):
        return max(u for u,(a,_) in enumerate(self.units) if a==w)+self.last+1
    def spread(self,step,steps):
        per=-(-self.ticks//steps)
        for g in range(steps):
            if g*per>=self.ticks: break
            @pl.when(step==g)
            def _(g=g): self.run(g*per,per)

VM=60<<20
def call(body,name,grid,ins,in_specs,outs,out_specs,scratch,side=None,cid=None):
    any_=pl.BlockSpec(memory_space=pl.ANY)
    extra=side.inputs if side else []
    a,b,c,d,e=len(ins),len(extra),len(outs),len(side.out_shapes) if side else 0,len(scratch)
    def kernel(*refs):
        comm=None
        cut=np.cumsum([0,a,b,c,d,e]).tolist()
        part=[refs[x:y] for x,y in zip(cut,cut[1:]+[len(refs)])]
        if side:
            comm=side.bind(part[1],part[3],part[5])
        body(comm,*part[0],*part[2],*part[4])
    out=pl.pallas_call(kernel,grid=grid,out_shape=list(outs)+(side.out_shapes if side else []),in_specs=list(in_specs)+[any_]*b,
        out_specs=list(out_specs)+(side.out_specs if side else []),scratch_shapes=list(scratch)+(side.scratch if side else []),
        compiler_params=pltpu.CompilerParams(vmem_limit_bytes=VM,**(dict(collective_id=cid,has_side_effects=True) if side else {})),name=name)(*ins,*extra)
    return out[:c],out[c:]

def alone(comm):
    comm.begin(); comm.run(0,comm.ticks)
def gather(S,shards,cid,**kw):
    return call(alone,'gather_weights',(),[],[],[],[],[],Gather(S,shards,**kw),cid)[1]
def scatter(S,grads,cid):
    return call(alone,'sum_gradients',(),[],[],[],[],[],Scatter(S,grads),cid)[1][0]


CH=64

def aside(body):
    def run(comm,*refs):
        if comm:
            @pl.when(pl.program_id(0)==0)
            def _(): comm.begin()
        body(*refs)
        if comm: comm.spread(pl.program_id(0),pl.num_programs(0))
    return run
def whole(shape):
    return pl.BlockSpec(shape,lambda *i:(0,)*len(shape),pipeline_mode=pl.Buffered(1))
def chunks(steps,body):
    def run(i,c):
        body(pl.ds(pl.multiple_of(i*CH,CH),CH)); return c
    lax.fori_loop(0,steps//CH,run,0)
def stats(v):
    center=v-jnp.mean(v,axis=-1,keepdims=True)
    rstd=lax.rsqrt(jnp.mean(center*center,axis=-1,keepdims=True)+1e-5)
    return center*rstd,rstd
def norm_back(dy,gain,xhat,rstd):
    g=dy*gain
    return rstd*(g-jnp.mean(g,axis=-1,keepdims=True)-xhat*jnp.mean(g*xhat,axis=-1,keepdims=True))
def sigmoid(v): return 0.5*jnp.tanh(0.5*v)+0.5
def fold(v): return jnp.sum(v.reshape(v.shape[0]//8,8,v.shape[1]),axis=0)

PAD=32
RC=128
def over_columns(width,body):
    def run(i,c):
        body(pl.ds(pl.multiple_of(i*128,128),128)); return c
    lax.fori_loop(0,width//128,run,0)
def taps_of(taps,lead,residue):
    return [(a,k) for k in range(taps) for a in [lead(k)//8] if lead(k)%8==residue]
def slide(pad_ref,w_ref,lead,taps,t0,cols):
    acc=jnp.zeros((RC,128),F32)
    for b in range(8):
        use=taps_of(taps,lead,b)
        if not use: continue
        top=max(a for a,_ in use)
        slab=pad_ref[t0+b:t0+b+RC+8*top,cols]
        for a,k in use: acc=acc+w_ref[k:k+1,cols]*slab[8*a:8*a+RC]
    return acc

def points(comm,count):
    at=[-1]
    def point():
        if not comm: return
        if at[0]<0: comm.begin()
        else:
            per=-(-comm.ticks//count)
            comm.run(at[0]*per,per)
        at[0]+=1
    return point

def into_units(ref,rows):
    n,w=SUB; across=rows.shape[1]//w
    for a in range(rows.shape[0]//n):
        for b in range(across): ref[a*across+b,0]=rows[a*n:a*n+n,b*w:b*w+w]

def feed_back_kernel(norm,d_ref,x_ref,gain_ref,hid_ref,act_ref,dsl_ref,fi_ref,fo_ref,
        out_ref,dfi_ref,dfo_ref,dbin_ref,sums_ref,df_ref,acc_ref,turn_ref):
    steps=x_ref.shape[0]; j=pl.program_id(0)
    @pl.when(j==0)
    def _():
        sums_ref[...]=jnp.zeros_like(sums_ref)
        def body(r):
            df=(0.5*d_ref[r,:]).astype(BF)
            df_ref[r,:]=df
            sums_ref[2]+=fold(df.astype(F32))
        chunks(steps,body)
        turn_ref[...]=hid_ref[...].T
        acc_ref[...]=jnp.zeros_like(acc_ref)
    dpre=(nt(df_ref[...],fo_ref[...])*dsl_ref[...].astype(F32)).astype(BF)
    dbin_ref[...]=fold(dpre.astype(F32))
    acc_ref[...]+=nt(dpre,fi_ref[...])
    dfi_ref[0]=nn(turn_ref[...],dpre).astype(BF)
    into_units(dfo_ref,tn(act_ref[...],df_ref[...]).astype(BF))
    @pl.when(j==pl.num_programs(0)-1)
    def _():
        def body(r):
            xhat,rstd=stats(x_ref[r,:].astype(F32))
            dy=acc_ref[r,:]
            sums_ref[0]+=fold(dy*xhat); sums_ref[1]+=fold(dy)
            out_ref[r,:]=(d_ref[r,:]+norm_back(dy,gain_ref[norm:norm+1,:],xhat,rstd)).astype(out_ref.dtype)
        chunks(steps,body)

def feed_back(d,x,gains,hid,act,dsl,fi,fo,norm,out_type,side=None,cid=None):
    steps,width=x.shape; hidden=fi.shape[1]; tn_=SUB[1]; tiles=hidden//tn_; S=width//SUB[0]
    assert hidden//S==tn_
    units=tn_*width//(SUB[0]*SUB[1])
    ins=[d,x,gains,hid,act,dsl,fi,fo]
    return call(aside(functools.partial(feed_back_kernel,norm)),'feed_forward_back',(tiles,),ins,
        [whole(d.shape),whole(x.shape),whole(gains.shape),whole(hid.shape),pl.BlockSpec((steps,tn_),lambda j:(0,j)),pl.BlockSpec((steps,tn_),lambda j:(0,j)),pl.BlockSpec((width,tn_),lambda j:(0,j)),pl.BlockSpec((tn_,width),lambda j:(j,0))],
        [jax.ShapeDtypeStruct((steps,width),out_type),jax.ShapeDtypeStruct((tiles,width,tn_),BF),jax.ShapeDtypeStruct((units,S)+SUB,BF),jax.ShapeDtypeStruct((8,hidden),F32),jax.ShapeDtypeStruct((3,8,width),F32)],
        [whole((steps,width)),pl.BlockSpec((1,width,tn_),lambda j:(j,0,0)),pl.BlockSpec((units,1)+SUB,lambda j:(0,j,0,0)),pl.BlockSpec((8,tn_),lambda j:(0,j)),whole((3,8,width))],
        [pltpu.VMEM((steps,width),BF),pltpu.VMEM((steps,width),F32),pltpu.VMEM((width,steps),BF)],side,cid)

def in_units(ref,v):
    for j in range(ref.shape[0]): ref[j]=v[:,j*ref.shape[2]:(j+1)*ref.shape[2]]

def middle_back_kernel(taps,comm,d_ref,depth_ref,up_ref,chid_ref,cact_ref,mixed_ref,x2_ref,vec_ref,valid_ref,ao_ref,pi_ref,po_ref,
        dx2_ref,dpv_ref,dpo_ref,dpi_ref,dao_ref,ddw_ref,sums_ref,low_ref,wide_ref,pad_ref,tail_ref):
    steps,width=d_ref.shape
    gain_ref=vec_ref.at[Rows.gain:Rows.gain+8]; shift_ref=vec_ref.at[Rows.shift:Rows.shift+8]; dw_ref=vec_ref.at[Rows.taps:Rows.taps+32]
    point=points(comm,8)
    point()
    sums_ref[...]=jnp.zeros_like(sums_ref)
    def cast(r): low_ref[r,:width]=d_ref[r,:].astype(BF)
    chunks(steps,cast)
    wide_ref[:,:width]=nt(low_ref[:,:width],po_ref[...])
    point()
    in_units(dpo_ref,tn(cact_ref[...],low_ref[:,:width]).astype(BF))
    point()
    tail_ref[steps:steps+PAD,:]=jnp.zeros((PAD,width),F32)
    pad_ref[0:PAD,:]=jnp.zeros((PAD,width),F32)
    def three(i,c):
        r=pl.ds(pl.multiple_of(i*CH,CH),CH)
        xhat,rstd=stats(depth_ref[r,:])
        gain=gain_ref[3:4,:]
        z=xhat*gain+shift_ref[3:4,:]
        sg=sigmoid(z)
        dz=wide_ref[r,:width]*(sg*(1.0+z*(1.0-sg)))
        sums_ref[0]+=fold(dz*xhat); sums_ref[1]+=fold(dz)
        tail_ref[r,:]=norm_back(dz,gain,xhat,rstd)
        pad_ref[pl.ds(pl.multiple_of(i*CH+PAD,PAD),CH),:]=up_ref[r,:width].astype(F32)*sigmoid(up_ref[r,width:].astype(F32))*valid_ref[r,0:1]
        return c
    lax.fori_loop(0,steps//CH,three,0)
    point()
    def conv(cols):
        for t0 in range(0,steps,RC):
            wide_ref[t0:t0+RC,cols]=slide(tail_ref,dw_ref,lambda k:taps-1-k,taps,t0,cols)
        lead=lambda k:k+PAD-taps+1
        for b in range(8):
            use=taps_of(taps,lead,b)
            if not use: continue
            top=max(a for a,_ in use)
            parts={k:jnp.zeros((8,128),F32) for _,k in use}
            for t0 in range(0,steps,RC):
                slab=pad_ref[t0+b:t0+b+RC+8*top,cols]
                dd=tail_ref[t0:t0+RC,cols]
                for a,k in use: parts[k]=parts[k]+fold(slab[8*a:8*a+RC]*dd)
            for k,v in parts.items(): ddw_ref[k:k+1,cols]=jnp.sum(v,axis=0,keepdims=True)
    over_columns(width,conv)
    point()
    def gate(r):
        a=up_ref[r,:width].astype(F32); sg=sigmoid(up_ref[r,width:].astype(F32))
        dg=wide_ref[r,:width]*valid_ref[r,0:1]*sg
        low_ref[r,:width]=dg.astype(BF)
        low_ref[r,width:]=(dg*a*(1.0-sg)).astype(BF)
    chunks(steps,gate)
    in_units(dpi_ref,tn(chid_ref[...],low_ref[...]).astype(BF))
    point()
    wide_ref[:,:width]=nt(low_ref[...],pi_ref[...])
    point()
    def two(r):
        xhat,rstd=stats(x2_ref[r,:])
        dy=wide_ref[r,:width]
        sums_ref[2]+=fold(dy*xhat); sums_ref[3]+=fold(dy)
        dx=d_ref[r,:]+norm_back(dy,gain_ref[2:3,:],xhat,rstd)
        dx2_ref[r,:]=dx
        da=dx.astype(BF)
        low_ref[r,:width]=da
        sums_ref[4]+=fold(da.astype(F32))
    chunks(steps,two)
    point()
    dpv_ref[...]=nt(low_ref[:,:width],ao_ref[...]).astype(BF)
    in_units(dao_ref,tn(mixed_ref[...],low_ref[:,:width]).astype(BF))
    point()

def middle_back(d,depth,up,chid,cact,mixed,x2,vec,valid,ao,pi,po,taps,side=None,cid=None):
    steps,width=d.shape
    ins=[d,depth,up,chid,cact,mixed,x2,vec,valid,ao,pi,po]
    S=jax.ShapeDtypeStruct
    unit=lambda w: S((w.shape[1]//SUB[1],w.shape[0],SUB[1]),BF)
    outs=[S((steps,width),F32),S((steps,width),BF),unit(po),unit(pi),unit(ao),S((32,width),F32),S((5,8,width),F32)]
    return call(functools.partial(middle_back_kernel,taps),'convolution_module_back',(1,),ins,[whole(a.shape) for a in ins],outs,[whole(o.shape) for o in outs],
        [pltpu.VMEM((steps,2*width),BF),pltpu.VMEM((steps,width),F32),pltpu.VMEM((steps+PAD,width),F32),pltpu.VMEM((steps+PAD,width),F32)],side,cid)


def late_kernel(taps,size,vector_rows,comm,q_ref,k_ref,v_ref,p_ref,g_ref,table_ref,pick_ref,hid1_ref,ai_ref,dx2_ref,x1_ref,gain_ref,
        hid0_ref,act_ref,dsl_ref,fi_ref,fo_ref,x_ref,s5_ref,s4_ref,s23_ref,ddw_ref,dbin1_ref,out_ref,
        ds_ref,dpk_ref,dtab_ref,psum_ref,acc_ref,turn_ref,dx1_ref,df_ref,stage_ref,dbin_ref,sums_ref,vec_ref,stage_sem,left_sem):
    steps,width=x1_ref.shape; wide=SUB[1]; S=comm.S
    A=width//128; B=3*width//wide; C=act_ref.shape[1]//wide; D=C
    j=pl.program_id(0)
    made_ai,made_fi,made_small,made_fo=comm.makes
    @pl.when(j==0)
    def _():
        comm.begin()
        dtab_ref[...]=jnp.zeros_like(dtab_ref)
    def put(q,ref):
        return pltpu.make_async_copy(stage_ref.at[lax.rem(q,2)],ref,stage_sem.at[lax.rem(q,2)])
    def unit(q,value,ref):
        @pl.when(q>=2)
        def _(): put(q,ref).wait()
        stage_ref[lax.rem(q,2)]=value.reshape(stage_ref.shape[1:])
        put(q,ref).start()
    def lefts(a,slot):
        rows=act_ref.shape[1]//S
        return [pltpu.make_async_copy(act_ref.at[:,pl.ds(al(s*rows+a*SUB[0],SUB[0]),SUB[0])],dpk_ref.at[slot,:,pl.ds(s*SUB[0],SUB[0])],left_sem.at[slot,s]) for s in range(S)]
    @pl.when(j<A)
    def _():
        flip=(lax.broadcasted_iota(jnp.int32,(QB,QB),0)+lax.broadcasted_iota(jnp.int32,(QB,QB),1)==QB-1).astype(F32).astype(BF)
        here=pl.ds(al(j*128,128),128)
        parts=[]
        for hh in range(128//size):
            cols=slice(hh*size,(hh+1)*size)
            parts.append(one_head_back(q_ref,k_ref,v_ref,p_ref.at[hh],g_ref,table_ref,pick_ref,dtab_ref,ds_ref,flip,cols))
            comm.run(j*2+hh,1)
        for part in range(3):
            dpk_ref[part,:,here]=jnp.concatenate([a[part] for a in parts],axis=1)
        psum_ref[0:1,here]=jnp.sum(dpk_ref[0,:,here].astype(F32),axis=0,keepdims=True)
        psum_ref[1:2,here]=jnp.sum(dpk_ref[2,:,here].astype(F32),axis=0,keepdims=True)
    @pl.when((j>=A)&(j<A+B))
    def _():
        b=j-A; per=width//wide
        @pl.when(b==0)
        def _():
            turn_ref[...]=hid1_ref[...].T
            acc_ref[...]=jnp.zeros_like(acc_ref)
            sums_ref[...]=jnp.zeros_like(sums_ref)
        g=dpk_ref[b//per,:,pl.ds(al(lax.rem(b,per)*wide,wide),wide)]
        acc_ref[...]+=nt(g,ai_ref[...])
        unit(b,nn(turn_ref[...],g).astype(BF),made_ai.at[b])
        @pl.when(b==B-1)
        def _():
            for a in range(3):
                for cp in lefts(a,a): cp.start()
            turn_ref[...]=hid0_ref[...].T
            def body(r):
                xhat,rstd=stats(x1_ref[r,:])
                dy=acc_ref[r,:]
                sums_ref[0]+=fold(dy*xhat); sums_ref[1]+=fold(dy)
                dx=dx2_ref[r,:]+norm_back(dy,gain_ref[1:2,:],xhat,rstd)
                dx1_ref[r,:]=dx
                df=(0.5*dx).astype(BF)
                df_ref[r,:]=df
                sums_ref[4]+=fold(df.astype(F32))
            chunks(steps,body)
            acc_ref[...]=jnp.zeros_like(acc_ref)
        comm.run(2*A+b,1)
    @pl.when((j>=A+B)&(j<A+B+C))
    def _():
        c=j-A-B
        dpre=(nt(df_ref[...],fo_ref[...])*dsl_ref[...].astype(F32)).astype(BF)
        dbin_ref[:,pl.ds(al(c*wide,wide),wide)]=fold(dpre.astype(F32))
        acc_ref[...]+=nt(dpre,fi_ref[...])
        unit(B+c,nn(turn_ref[...],dpre).astype(BF),made_fi.at[c])
        @pl.when(c==C-1)
        def _():
            def body(r):
                xhat,rstd=stats(x_ref[r,:].astype(F32))
                dy=acc_ref[r,:]
                sums_ref[2]+=fold(dy*xhat); sums_ref[3]+=fold(dy)
                out_ref[r,:]=(dx1_ref[r,:]+norm_back(dy,gain_ref[0:1,:],xhat,rstd)).astype(BF)
            chunks(steps,body)
            vec_ref[...]=jnp.zeros_like(vec_ref)
            total=lambda v: jnp.sum(v,axis=0,keepdims=True)
            rows=[sums_ref[2],sums_ref[0],s23_ref[2],s23_ref[0],s4_ref[0],s5_ref[0],sums_ref[3],sums_ref[1],s23_ref[3],s23_ref[1],s4_ref[1],s5_ref[1],sums_ref[4],s4_ref[2]]
            rows=[total(v) for v in rows]+[psum_ref[0:1,:],psum_ref[1:2,:],total(s23_ref[4])]
            L=width//S
            for i,v in enumerate(rows):
                for s in range(S): vec_ref[s,i:i+1,0:L]=v[:,s*L:s*L+L]
            k=len(rows)
            for i,ref in enumerate((dbin_ref,dbin1_ref)):
                v=total(ref[...])
                for s in range(S): vec_ref[s,k+i:k+i+1,:]=v[:,s*wide:s*wide+wide]
            for s in range(S):
                vec_ref[s,32:32+taps,0:L]=ddw_ref[0:taps,s*L:s*L+L]
                n=dtab_ref.shape[0]//S
                vec_ref[s,vector_rows:vector_rows+n,0:size]=dtab_ref[s*n:s*n+n,:]
        comm.run(2*A+B+c,1)
    @pl.when((j>=A+B+C)&(j<A+B+C+D))
    def _():
        d=j-A-B-C; across=width//wide
        @pl.when(d==0)
        def _(): unit(B+C,vec_ref[...].astype(BF).reshape(S*SUB[0],wide),made_small.at[0])
        a=d//across
        for slot in range(3):
            @pl.when((lax.rem(a,3)==slot)&(lax.rem(d,across)==0))
            def _(slot=slot):
                for cp in lefts(a,slot): cp.wait()
        unit(B+C+1+d,tn(dpk_ref[lax.rem(a,3)],df_ref[:,pl.ds(al(lax.rem(d,across)*wide,wide),wide)]).astype(BF),made_fo.at[d])
        @pl.when(d==across-1)
        def _():
            for a in range(3,D//across):
                for cp in lefts(a,a-3): cp.start()
        comm.run(2*A+B+C+d,1)
    @pl.when(j==A+B+C+D)
    def _():
        for q in (0,1): put(B+C+D+1+q,made_fo.at[0]).wait()
        lo=2*A+B+C+D
        comm.run(lo,comm.ticks-lo)

def one_head_back(q_ref,k_ref,v_ref,p_ref,g_ref,table_ref,pick_ref,dtab_ref,ds_ref,flip,cols):
    steps=q_ref.shape[0]; nb=steps//QB; span=steps+QB; size=cols.stop-cols.start
    scale=1.0/math.sqrt(size)
    k=k_ref[:,cols]; v=v_ref[:,cols]; dqs=[]
    for i in range(nb):
        rows=slice(i*QB,(i+1)*QB)
        q=q_ref[rows,cols]
        p=p_ref[rows,:].astype(F32)
        t=p*nt(g_ref[rows,cols],v)
        ds=(t-p*jnp.sum(t,axis=1,keepdims=True)).astype(BF)
        ds_ref[rows,:]=ds
        wide=jnp.concatenate([nn(flip,ds),jnp.zeros((QB,span-steps),F32)],axis=1)
        back=pltpu.roll(wide,span-QB+1,1,stride=1,stride_axis=0).astype(BF)
        drel=nn(flip,(nt(back,pick_ref[i])*scale).astype(BF)).astype(BF)
        dqs.append((nn(ds,k)*scale+nn(drel,table_ref[...])).astype(BF))
        dtab_ref[...]+=tn(drel,q)
    return jnp.concatenate(dqs,axis=0),(tn(ds_ref[...],q_ref[:,cols])*scale).astype(BF),tn(p_ref[...],g_ref[:,cols]).astype(BF)

VECTOR_ROWS=64
def late(S,packed,p,grad,table,pick,heads,hid1,ai,dx2,x1,gains,hid0,act,dsl,fi,fo,tokens,s5,s4,s23,ddw,dbin1,taps,ready,cid):
    steps,width=x1.shape; size=width//heads; wide=SUB[1]
    A=width//128; B=3*width//wide; C=act.shape[1]//wide; D=C; per=128//size
    assert act.shape[1]//S==wide and width//S==SUB[0] and wide//SUB[0]<=4
    comm=Scatter(S,ready+[B,C,1,D],common=(sum(a.shape[0] for a in ready)+B+C,VECTOR_ROWS,table.shape[0]//S))
    head=lambda o:pl.BlockSpec((steps,128),lambda j:(0,o*A+jnp.minimum(j,A-1)))
    tile=lambda lo,n:(lambda j:jnp.minimum(jnp.maximum(j-lo,0),n-1))
    tb,tc=tile(A,B),tile(A+B,C)
    ins=[packed,packed,packed,p,grad,table,pick,hid1,ai,dx2,x1,gains,hid0,act,dsl,fi,fo,tokens,s5,s4,s23,ddw,dbin1]
    specs=[head(0),head(1),head(2),pl.BlockSpec((per,steps,steps),lambda j:(jnp.minimum(j,A-1),0,0)),head(0),whole(table.shape),whole(pick.shape),
        whole(hid1.shape),pl.BlockSpec((width,wide),lambda j:(0,tb(j))),whole(dx2.shape),whole(x1.shape),whole(gains.shape),whole(hid0.shape),pl.BlockSpec(memory_space=pl.ANY),
        pl.BlockSpec((steps,wide),lambda j:(0,tc(j))),pl.BlockSpec((width,wide),lambda j:(0,tc(j))),pl.BlockSpec((wide,width),lambda j:(tc(j),0)),whole(tokens.shape)]
    specs+=[whole(a.shape) for a in (s5,s4,s23,ddw,dbin1)]
    V=pltpu.VMEM; Z=S//2
    scratch=[V((steps,steps),BF),V((3,steps,width),BF),V((128,size),F32),V((8,width),F32),V((steps,width),F32),V((width,steps),BF),V((steps,width),F32),V((steps,width),BF),
        V((2,Z,2,2,SUB[0]//2,wide),BF),V((8,act.shape[1]),F32),V((5,8,width),F32),V((S,)+SUB,F32),pltpu.SemaphoreType.DMA((2,)),pltpu.SemaphoreType.DMA((3,S))]
    return call(functools.partial(late_kernel,taps,size,VECTOR_ROWS),'attend_back_and_sums',(A+B+C+D+1,),ins,specs,[jax.ShapeDtypeStruct((steps,width),BF)],[whole((steps,width))],scratch,comm,cid)

class Rows:
    gain=0; shift=8; inner=16; outer=24; packed=26; mixed=28; taps=32; count=64

def early_kernel(heads,taps,comm,gain_in,shift_in,inner_in,outer_in,packed_in,mixed_in,taps_in,tok_ref,cot_ref,valid_ref,mask_ref,table_ref,pick_ref,
        hid0_ref,act0_ref,dsl0_ref,x1_ref,hid1_ref,packed_ref,mixed_ref,p_ref,x2_ref,chid_ref,up_ref,depth_ref,cact_ref,x3_ref,hid4_ref,act1_ref,dsl1_ref,dx4_ref,res_ref,s5_ref,vec_ref,
        own_ref,land_ref,land_sem,acc_ref,wa_ref,wb_ref,sem_a,sem_b,rel_ref,qkv_ref,pad_ref,wide_ref):
    steps,width=tok_ref.shape; tile=wa_ref.shape[2]; S=comm.S
    small,fi0,fo0,ai,ao,pi,po,fi1,fo1=comm.o
    F=fi0.shape[1]//tile; B=ai.shape[1]//tile; A=width//128; M0,M1,M2=ao.shape[1]//tile,pi.shape[1]//tile,po.shape[1]//tile
    size=width//heads
    cut=np.cumsum([0,F,B,A,M0,M1,M2,F]).tolist()
    j=pl.program_id(0)
    L=width//S
    def row(i): return vec_ref[i:i+1,:]
    def column(w,i,slot): return pltpu.make_async_copy(w.at[:,pl.ds(al(i*tile,tile),tile)],wa_ref.at[slot],sem_a.at[slot])
    def band(w,i,slot): return pltpu.make_async_copy(w.at[pl.ds(al(i*tile,tile),tile)],wb_ref.at[slot],sem_b.at[slot])
    want=[comm.done(2),comm.done(3),comm.done(4),comm.done(5),comm.done(6),comm.done(8)]
    at={}
    def plan(steps_,lo,hi):
        n=len(steps_)
        for i,st in enumerate(steps_):
            a,b=lo+(hi-lo)*i//n,lo+(hi-lo)*(i+1)//n
            if b>a: at[st]=(a,b-a)
    plan(list(range(F//2-1,cut[1],F//2)),want[0],want[1])
    plan([cut[2]-1],want[1],want[2])
    plan(list(range(cut[2]+A//2-1,cut[3],A//2)),want[2],want[4])
    plan([cut[4]-1,cut[6]-1],want[4],comm.ticks-1)
    def ticks():
        for st,(lo,n) in at.items():
            @pl.when(j==st)
            def _(lo=lo,n=n): comm.run(lo,n)
    @pl.when(j==0)
    def _():
        own_ref[...]=jnp.zeros_like(own_ref)
        for at_,ref in ((Rows.gain,gain_in),(Rows.shift,shift_in),(Rows.outer,outer_in),(Rows.packed,packed_in),(Rows.mixed,mixed_in),(Rows.taps,taps_in)):
            own_ref[at_:at_+ref.shape[0],:]=ref[...].astype(F32)
        k=inner_in.shape[1]//L
        for l in range(2):
            for i in range(k): own_ref[Rows.inner+l*k+i:Rows.inner+l*k+i+1,:]=inner_in[l:l+1,i*L:i*L+L].astype(F32)
        comm.i[0][...]=own_ref[...].astype(BF)
        comm.begin()
        comm.run(0,want[0])
        cp=pltpu.make_async_copy(small,land_ref,land_sem.at[0]); cp.start()
        column(fi0,0,0).start(); band(fo0,0,0).start()
        cp.wait()
        for s in range(S): vec_ref[:,s*L:s*L+L]=land_ref[s*Rows.count:(s+1)*Rows.count,:].astype(F32)
        for i in range(steps//QB): rel_ref[i]=tn(table_ref[...],pick_ref[i]).astype(BF)
        def body(r):
            xhat,_r=stats(tok_ref[r,:].astype(F32))
            hid0_ref[r,:]=(xhat*row(Rows.gain)+row(Rows.shift)).astype(BF)
        chunks(steps,body)
        acc_ref[...]=jnp.zeros_like(acc_ref)
        pad_ref[0:PAD,:]=jnp.zeros((PAD,width),F32)
    def feed_tile(i,tau,l,hid_ref,act_ref,dsl_ref,fi,fo):
        slot=lax.rem(tau,2); k=tile//L
        column(fi,i,slot).wait(); band(fo,i,lax.rem(i,2)).wait()
        @pl.when(i+1<F)
        def _(): column(fi,i+1,lax.rem(tau+1,2)).start(); band(fo,i+1,lax.rem(i+1,2)).start()
        bias=jnp.concatenate([vec_ref[Rows.inner+l*k+a:Rows.inner+l*k+a+1,pl.ds(al(i*L,L),L)] for a in range(k)],axis=1)
        pre=nn(hid_ref[...],wa_ref[slot])+bias
        sg=sigmoid(pre)
        act_ref[...]=(pre*sg).astype(BF)
        dsl_ref[...]=(sg*(1.0+pre*(1.0-sg))).astype(BF)
        acc_ref[...]+=nn(act_ref[...],wb_ref[lax.rem(i,2)])
    @pl.when(j<cut[1])
    def _(): feed_tile(j,j,0,hid0_ref,act0_ref,dsl0_ref,fi0,fo0)
    @pl.when(j==cut[1]-1)
    def _():
        def body(r):
            x=tok_ref[r,:].astype(F32)+0.5*(acc_ref[r,:]+row(Rows.outer))
            x1_ref[r,:]=x
            xhat,_r=stats(x)
            hid1_ref[r,:]=(xhat*row(Rows.gain+1)+row(Rows.shift+1)).astype(BF)
        chunks(steps,body)
    def stream(w,lo,n,tau0,use):
        @pl.when((j>=lo)&(j<lo+n))
        def _():
            i=j-lo; slot=lax.rem(tau0+i,2)
            column(w,i,slot).wait()
            @pl.when(i+1<n)
            def _(): column(w,i+1,lax.rem(tau0+i+1,2)).start()
            use(i,slot)
    def after(step,w,tau):
        @pl.when(j==step)
        def _(): column(w,0,lax.rem(tau,2)).start()
    def here(i): return pl.ds(al(i*tile,tile),tile)
    def pack(i,slot):
        v=nn(hid1_ref[...],wa_ref[slot])
        per=width//tile
        @pl.when(i<per)
        def _(): packed_ref[:,here(i)]=(v+vec_ref[Rows.packed:Rows.packed+1,here(lax.rem(i,per))]).astype(BF)
        @pl.when((i>=per)&(i<2*per))
        def _(): packed_ref[:,here(i)]=v.astype(BF)
        @pl.when(i>=2*per)
        def _(): packed_ref[:,here(i)]=(v+vec_ref[Rows.packed+1:Rows.packed+2,here(lax.rem(i,per))]).astype(BF)
    stream(ai,cut[1],B,F,pack)
    @pl.when((j>=cut[2])&(j<cut[3]))
    def _():
        h=j-cut[2]
        for a in range(3): qkv_ref[a]=packed_ref[:,pl.ds(al(a*width+h*128,128),128)]
        scale=1.0/math.sqrt(size)
        for i in range(steps//QB):
            rows=slice(i*QB,(i+1)*QB); outs=[]
            for hh in range(128//size):
                cols=slice(hh*size,(hh+1)*size)
                q=qkv_ref[0,rows,cols]
                rel=pltpu.roll(nn(q,rel_ref[i]),0,1,stride=1,stride_axis=0)[:,:steps]
                s=(nt(q,qkv_ref[1,:,cols])+rel)*scale+mask_ref[0:1,:]
                e=jnp.exp(s-jnp.max(s,axis=1,keepdims=True))
                p=(e*(1.0/jnp.sum(e,axis=1,keepdims=True))).astype(BF)
                p_ref[hh,rows,:]=p
                outs.append(nn(p,qkv_ref[2,:,cols]).astype(BF))
            mixed_ref[rows,pl.ds(al(h*128,128),128)]=jnp.concatenate(outs,axis=1)
    def join(i,slot):
        x2_ref[:,here(i)]=x1_ref[:,here(i)]+nn(mixed_ref[...],wa_ref[slot])+vec_ref[Rows.mixed:Rows.mixed+1,here(i)]
        @pl.when(i==M0-1)
        def _():
            def body(r):
                xhat,_r=stats(x2_ref[r,:])
                chid_ref[r,:]=(xhat*row(Rows.gain+2)+row(Rows.shift+2)).astype(BF)
            chunks(steps,body)
    stream(ao,cut[3],M0,F+B,join)
    def raise_(i,slot):
        wide_ref[:,here(i)]=nn(chid_ref[...],wa_ref[slot])
        @pl.when(i==M1-1)
        def _():
            def gate(k,c):
                r=pl.ds(pl.multiple_of(k*CH,CH),CH)
                a=wide_ref[r,:width]; b=wide_ref[r,width:]
                up_ref[r,:width]=a.astype(BF); up_ref[r,width:]=b.astype(BF)
                pad_ref[pl.ds(pl.multiple_of(k*CH+PAD,PAD),CH),:]=a*sigmoid(b)*valid_ref[r,0:1]
                return c
            lax.fori_loop(0,steps//CH,gate,0)
            weights=vec_ref.at[Rows.taps:Rows.taps+32]
            def conv(cols):
                for t0 in range(0,steps,RC):
                    depth_ref[t0:t0+RC,cols]=slide(pad_ref,weights,lambda k:k+PAD-taps+1,taps,t0,cols)
            over_columns(width,conv)
            def body(r):
                xhat,_r=stats(depth_ref[r,:])
                z=xhat*row(Rows.gain+3)+row(Rows.shift+3)
                cact_ref[r,:]=(z*sigmoid(z)).astype(BF)
            chunks(steps,body)
    stream(pi,cut[4],M1,F+B+M0,raise_)
    def lower(i,slot):
        x3_ref[:,here(i)]=x2_ref[:,here(i)]+nn(cact_ref[...],wa_ref[slot])
        @pl.when(i==M2-1)
        def _():
            def body(r):
                xhat,_r=stats(x3_ref[r,:])
                hid4_ref[r,:]=(xhat*row(Rows.gain+4)+row(Rows.shift+4)).astype(BF)
            chunks(steps,body)
            acc_ref[...]=jnp.zeros_like(acc_ref)
    stream(po,cut[5],M2,F+B+M0+M1,lower)
    ticks()
    tau=F+B+M0+M1+M2
    after(cut[1]-1,ai,F); after(cut[3]-1,ao,F+B); after(cut[4]-1,pi,F+B+M0); after(cut[5]-1,po,F+B+M0+M1)
    @pl.when(j==cut[6]-1)
    def _():
        comm.run(comm.ticks-1,1)
        column(fi1,0,tau%2).start(); band(fo1,0,0).start()
    @pl.when(j>=cut[6])
    def _(): feed_tile(j-cut[6],tau+j-cut[6],1,hid4_ref,act1_ref,dsl1_ref,fi1,fo1)
    @pl.when(j==cut[7]-1)
    def _():
        s5_ref[...]=jnp.zeros_like(s5_ref)
        def body(r):
            y=x3_ref[r,:]+0.5*(acc_ref[r,:]+row(Rows.outer+1))
            xhat,rstd=stats(y)
            ok=valid_ref[r,0:1]
            gain=row(Rows.gain+5)
            res_ref[r,:]=((xhat*gain+row(Rows.shift+5))*ok).astype(BF)
            dy=cot_ref[r,:].astype(F32)*ok
            dx4_ref[r,:]=norm_back(dy,gain,xhat,rstd)
            s5_ref[0]+=fold(dy*xhat)
            s5_ref[1]+=fold(dy)
        chunks(steps,body)

def early(S,vectors,tokens,cot,valid,mask,table,pick,heads,weights,cid):
    steps,width=tokens.shape; tile=512; taps=vectors[-1].shape[0]; L=vectors[0].shape[1]
    comm=Gather(S,[(Rows.count,L)]+weights,cuts=[1,2,2,2,1,1,1,2,2],modes=['h','hq','hh','qh','h','q','h','hq','hh'],ahead=4)
    hidden=comm.shapes[1][1]; size=width//heads
    F,B,A=hidden//tile,comm.shapes[3][1]//tile,width//128
    M=[comm.shapes[i][1]//tile for i in (4,5,6)]
    assert comm.shapes[2][0]*S==hidden and tile==hidden//S
    cut=np.cumsum([0,F,B,A]+M+[F]).tolist()
    within=lambda lo,n:(lambda j:jnp.minimum(jnp.maximum(j-lo,0),n-1))
    f0,at,f1=within(0,F),within(cut[2],A),within(cut[6],F)
    ins=list(vectors)+[tokens,cot,valid,mask,table,pick]
    D=jax.ShapeDtypeStruct
    b=D((steps,width),BF); f=D((steps,width),F32); hid=D((steps,hidden),BF)
    outs=[b,hid,hid,f,b,D((steps,3*width),BF),b,D((heads,steps,steps),BF),f,b,D((steps,2*width),BF),f,b,f,b,hid,hid,f,b,D((2,8,width),F32),D((Rows.count,width),F32)]
    specs=[whole(o.shape) for o in outs]
    for i,t in ((1,f0),(2,f0),(15,f1),(16,f1)): specs[i]=pl.BlockSpec((steps,tile),lambda j,t=t:(0,t(j)))
    specs[7]=pl.BlockSpec((128//size,steps,steps),lambda j:(at(j),0,0))
    V=pltpu.VMEM; sem=lambda n: pltpu.SemaphoreType.DMA((n,))
    scratch=[V((Rows.count,L),F32),V((S*Rows.count,L),BF),sem(1),V((steps,width),F32),V((2,width,tile),BF),V((2,tile,width),BF),sem(2),sem(2),
        V((steps//QB,size,steps+QB),BF),V((3,steps,128),BF),V((steps+PAD,width),F32),V((steps,2*width),F32)]
    return call(functools.partial(early_kernel,heads,taps),'gather_and_forward',(cut[-1],),ins,[whole(a.shape) for a in ins],outs,specs,scratch,comm,cid)


def local(S,R,tokens,lengths,cotangent,norm_gain,norm_shift,feed_in,feed_in_bias,feed_out,feed_out_bias,attention_in,attention_in_bias,attention_out,attention_out_bias,relative_table,pointwise_in,depthwise,pointwise_out):
    steps,width=tokens.shape; taps=depthwise.shape[0]
    live=jnp.arange(steps,dtype=jnp.int32)<lengths[0]
    valid=jnp.broadcast_to(live.astype(F32)[:,None],(steps,128))
    mask=jnp.broadcast_to(jnp.where(live,0.0,-1e30).astype(F32)[None,:],(8,steps))
    rows=relative_table.shape[0]
    table=jnp.pad(relative_table,((0,128-rows),(0,0)))
    pick=jnp.asarray(picker_table(steps,QB).astype(np.float32)).astype(BF)
    vectors=[norm_gain,norm_shift,feed_in_bias,feed_out_bias,attention_in_bias,attention_out_bias.reshape(1,-1),depthwise]
    weights=[(feed_in,0),(feed_out,0),attention_in,attention_out,pointwise_in,pointwise_out,(feed_in,1),(feed_out,1)]
    outs,full=early(S,vectors,tokens,cotangent,valid,mask,table,pick,HEADS,weights,0)
    hid0,act0,dsl0,x1,hid1,packed,mixed,p,x2,chid,up,depth,cact,x3,hid4,act1,dsl1,dx4,result,s5,vec=outs
    fi0,fo0,ai,ao,pi,po,fi1,fo1=full[1:]
    flat=lambda a:a.reshape(a.shape[0],S*SUB[0],SUB[1])
    (dx3,dfi1,dfo1,dbin1,s4),_=feed_back(dx4,x3,vec,hid4,act1,dsl1,fi1,fo1,4,F32)
    (dx2,dpv,dpo,dpi,dao,ddw,s23),_=middle_back(dx3,depth,up,chid,cact,mixed,x2,vec,valid,ao,pi,po,taps)
    ready=[dfi1,flat(dfo1),dpo,dpi,dao]
    (dtok,),outs=late(S,packed,p,dpv,table,pick,HEADS,hid1,ai,dx2,x1,vec,hid0,act0,dsl0,fi0,fo0,tokens,s5,s4,s23,ddw,dbin1,taps,ready,7)
    sums,common=outs[0],outs[-1]
    if R>4:
        groups=[[g*4+i for g in range(R//4)] for i in range(4)]
        sums,common=[lax.psum(a,'rep',axis_index_groups=groups) for a in (sums,common)]
    at=np.cumsum([0]+[a.shape[0] for a in ready]+[3*width//SUB[1],fi0.shape[1]//SUB[1],1,fi0.shape[1]//SUB[1]]).tolist()
    gfi1,gfo1,gpo,gpi,gao,gai,gfi0,small,gfo0=[sums[a:b] for a,b in zip(at,at[1:])]
    def by_column(u): return u.transpose(1,0,2).reshape(SUB[0],-1).astype(F32)
    def by_row(u): return u.reshape(-1,width//SUB[1],*SUB).transpose(0,2,1,3).reshape(-1,width).astype(F32)
    vec=small[0].astype(F32); L=norm_gain.shape[1]
    ggain,gshift,gbout,gpbias,gmbias=[vec[a:b,:L] for a,b in ((0,6),(6,12),(12,14),(14,16),(16,17))]
    gbin=vec[17:19]; gdw=vec[32:32+taps,:L]
    gtab=common.reshape(-1,SUB[1])[:rows,:relative_table.shape[1]].astype(F32)
    return (result,dtok,ggain,gshift,jnp.stack([by_column(gfi0),by_column(gfi1)]),gbin,jnp.stack([by_row(gfo0),by_row(gfo1)]),gbout,by_column(gai),gpbias,by_column(gao),gmbias[0],gtab,by_column(gpi),gdw,by_column(gpo))

HEADS=16

def solution(mesh):
    R,S=mesh.shape['rep'],mesh.shape['shard']
    rows=P(('rep','shard'),None)
    last,mid,first=P(None,'shard'),P(None,'shard',None),P('shard',None)
    weights=(last,last,mid,last,mid,last,first,last,first,P('shard'),P(),first,last,first)
    return jax.shard_map(functools.partial(local,S,R),mesh=mesh,in_specs=(rows,P(('rep','shard')),rows)+weights,out_specs=(rows,rows)+weights,check_vma=False)
```

time: 2830 us -> 679 us (0.24)
  waiting for transfers between devices: 1390 us -> 0 us
  local copies, waits for them, and re-layouts: 674 us -> 34 us
  Pallas kernels: 0 us -> 623 us
  matrix products: 317 us -> 0 us
  blocking collectives: 229 us -> 0 us
  other arithmetic: 171 us -> 9.8 us
    pallas_call x0 -> x4, Pallas kernels: none -> 623 us  [call(): pl.pallas_call(kernel, grid=grid, out_shape=list(outs) + (side.out_shapes...]
    reduce_scatter x6 -> x0, waiting for transfers between devices: 596 us -> none  [the longest x1 285 us: local(): lax.psum_scatter(full[4].astype(jnp.bfloat16), 'shard', scatter_dimension...]
    reshape x24 -> x0, local copies, waits for them, and re-layouts: 369 us -> none  [the longest x12 186 us: spread_offsets(): flat[:, steps - 1:steps - 1 + steps * (span - 1)]]
    all_gather x6 -> x0, waiting for transfers between devices: 369 us -> none  [the longest x1 217 us: local(): lax.all_gather(feed_out, 'shard', axis=1, tiled=True)]
    unnamed x25 -> x0, waiting for transfers between devices: 324 us -> none
    dot_general x72 -> x0, matrix products: 269 us -> none  [the longest x12 90.6 us: spread_offsets(): jnp.einsum('hqr,rm->hqm', rel, picker, precision=lax.Precision.HIGHEST)]
    all_gather x7 -> x0, blocking collectives: 161 us -> none  [the longest x1 28.4 us: local(): lax.all_gather(depthwise, 'shard', axis=1, tiled=True)]
    slice x23 -> x6, local copies, waits for them, and re-layouts: 116 us -> 7.01 us  [the longest x1 3.91 us: local(): sums[a:b]]
  transfers between devices with their start and end apart: 19 -> 0, of which waited for: 13 -> 0; matrix products, arithmetic and copies ran while one was open for 36% -> 0% of each run, Pallas kernels for 0% -> 0%
where the time goes in v1:
time: 679 us; the launch traced here: 668 us
  Pallas kernels  623 us (92%)
  local copies, waits for them, and re-layouts  34 us (5%)
  other arithmetic  9.8 us (1%)
    pallas_call x4, Pallas kernels, call(): pl.pallas_call(kernel, grid=grid, out_shape=list(outs) + (side.out_shapes...  623 us

profile of v1, /device:TPU:0, one launch (start us, length us, event | category | flops | bytes accessed | tf_op | source)
XLA Modules:
  0.0 668.3 jit_solution(2058475941336909208)
XLA Ops:
  1.3 0.6 broadcast_in_dim.23.refs_10_
  1.9 0.8 copy.38
  2.7 0.6 pad.4.refs_11_.refs_5_
  3.4 0.8 broadcast_in_dim.20.refs_9_.refs_8_
  4.2 273.9 %gather_and_forward.1 = (bf16[512,1024]{1,0:T(8,128)(2,1)}, bf16[512,4096]{1,0:T(8,128)(2,1)}, bf16[512,4096]{1,0:T(8,128)(2,1)}, f32[512,1024]{1,0:T(8,128)}, b...) custom-call(bf16[6,128]{1,0:T(8,128)(2,1)} %refs_0_.1, ...), custom_call_target="tpu_custom_call" | custom-call | tf_op jit(solution)/shard_map/gather_and_forward/pallas_call | solution.py:307
  278.1 29.0 %feed_forward_back.1 = (f32[512,1024]{1,0:T(8,128)}, bf16[8,1024,512]{2,1,0:T(8,128)(2,1)}, bf16[8,8,128,512]{3,2,1,0:T(8,128)(2,1)}, f32[8,4096]{1,0:T(8,128)}, f32[3,8,1024]{2,1,0:T(8,128)}) custom-call(f32[512,1024]{1,0:T(8,128)} %get-tuple-element.63.refs_0_, f32[512,1024]{1,0:T(8,128)} %get-tuple-element.64.refs_1_, ...), custom_call_target="tpu_custom_call" | custom-call | tf_op jit(solution)/shard_map/feed_forward_back/pallas_call | solution.py:307
  307.2 47.8 %convolution_module_back.1 = (f32[512,1024]{1,0:T(8,128)}, bf16[512,1024]{1,0:T(8,128)(2,1)}, bf16[2,1024,512]{2,1,0:T(8,128)(2,1)}, bf16[4,1024,512]{2,1,0:T(8,...) custom-call(f32[512,1024]{1,0:T(8,128)} %get-tuple-element.71.refs_0_, ...), custom_call_target="tpu_custom_call" | custom-call | tf_op jit(solution)/shard_map/convolution_module_back/pallas_call | solution.py:307
  355.0 271.9 %attend_back_and_sums.1 = (bf16[512,1024]{1,0:T(8,128)(2,1)}, bf16[47,128,512]{2,1,0:T(8,128)(2,1)}, bf16[6,4,2,2,64,512]{5,4,3,2,1,0:T(8,128)(2,1)}, bf16[8,4,2...) custom-call(bf16[512,3072]{1,0:T(8,128)(2,1)} %get-tuple-element.61., ...), custom_call_target="tpu_custom_call" | custom-call | tf_op jit(solution)/shard_map/attend_back_and_sums/pallas_call | solution.py:307
  626.9 0.7 slice.78
  627.6 0.1 copy.53
  627.7 0.6 convert_element_type.139
  628.3 0.9 slice_convert_fusion
  629.3 0.6 slice_bitcast_fusion.2
  629.9 0.5 slice_bitcast_fusion.3
  630.4 0.6 fusion.4
  631.0 0.6 fusion.5
  631.6 0.6 slice.79
  632.2 1.2 convert_bitcast_fusion.1
  633.3 0.3 copy.46
  633.7 1.3 copy.51
  635.0 1.1 convert_bitcast_fusion.2
  636.1 0.2 copy.47
  636.3 1.0 copy.52
  637.3 0.2 copy.44
  637.5 1.0 copy.50
  638.5 1.3 convert_bitcast_fusion
  639.9 3.9 fusion.3
  643.8 1.1 copy.41
  644.9 1.6 convert_element_type.129
  646.4 2.3 copy.42
  648.7 1.5 convert_element_type.132
  650.3 0.5 copy.43
  650.8 1.6 copy.49
  652.4 1.6 copy.40
  654.0 1.6 copy.39
  655.6 2.3 maximum_convert_fusion
  657.9 0.0 copy-start
  657.9 0.0 copy-start.1
  657.9 5.7 copy.48
  663.7 0.0 copy-done
  663.7 0.0 copy-done.1
  663.7 0.0 copy-start.2
  663.7 0.0 copy-start.3
  663.7 2.3 maximum_convert_fusion.1
  666.0 0.0 copy-done.2
  666.0 1.0 copy.57
  666.9 0.0 copy-done.3
  666.9 1.0 copy.58
  (2 shorter events, 0.0 us)
Async XLA Ops:
  657.9 5.8 copy-start
  657.9 5.8 copy-start.1
  663.7 2.3 copy-start.2
  663.7 3.3 copy-start.3

commit v2 on v1

--- a/solution.py
+++ b/solution.py
@@ -51,7 +51,8 @@
 SUB=(128,512)
 class Scatter:
     OWN=18; RING=6; GAP=2
-    def __init__(self,S,sources,common=None):
+    def __init__(self,S,sources,places,out_shapes,common=None):
+        self.places=places
         self.common=common
         self.S=S; Z=S//2
         counts=[a if isinstance(a,int) else a.shape[0] for a in sources]
@@ -62,7 +63,8 @@
         self.made=[isinstance(a,int) for a in sources]
         self.at=np.cumsum([0]+counts).tolist(); self.counts=counts
         self.inputs=[a.reshape(a.shape[0],Z,2,2,h,wide) for a in sources if not isinstance(a,int)]
-        self.out_shapes=[jax.ShapeDtypeStruct((n,rows,wide),BF)]+[jax.ShapeDtypeStruct((k,Z,2,2,h,wide),BF) for k,m in zip(counts,self.made) if m]
+        self.finals=len(out_shapes)
+        self.out_shapes=[jax.ShapeDtypeStruct(a,BF) for a in out_shapes]+[jax.ShapeDtypeStruct((k,Z,2,2,h,wide),BF) for k,m in zip(counts,self.made) if m]
         G=self.GAP
         self.lag=[0]+[G*k for k in range(1,5+Z)]
         self.lag[4+Z]=self.lag[3+Z]+1
@@ -81,7 +83,7 @@
             self.ticks=max(self.ticks,self.begin_common+Z+1)
         self.out_specs=[pl.BlockSpec(memory_space=pl.ANY)]*len(self.out_shapes)
     def bind(self,ins,outs,scr):
-        self.out=outs[0]; ins,made=list(ins),list(outs[1:1+sum(self.made)])
+        k=self.finals; self.out=outs[:k]; ins,made=list(ins),list(outs[k:k+sum(self.made)])
         self.makes=list(made)
         self.g=[made.pop(0) if m else ins.pop(0) for m in self.made]
         if self.common: self.all,self.cs,self.ct,self.co=scr[-4:]; self.all_out=outs[-1]; scr=scr[:-4]
@@ -103,7 +105,10 @@
     def swap(self,i): return self.remote(i,3+self.Z,self.own.at[self.slot(i),self.p.z,self.p.y],self.fr.at[self.land(i)],self.p.over_x)
     def half(self,i): return self.o.at[i,pl.ds(al(self.p.c*self.h,self.h),self.h)]
     def share(self,i): return self.remote(i,4+self.Z,self.half(i),self.half(i),self.p.twin)
-    def save(self,i): return pltpu.make_async_copy(self.o.at[i],self.out.at[i],self.os.at[i])
+    def save(self,i,place,unit):
+        index,layer,across=place; rows,wide=SUB
+        ref=self.out[index] if layer is None else self.out[index].at[layer]
+        return pltpu.make_async_copy(self.o.at[i],ref.at[pl.ds(al(unit//across*rows,rows),rows),pl.ds(al(lax.rem(unit,across)*wide,wide),wide)],self.os.at[i])
     def ask(self,i,k):
         if self.ring<self.n:
             @pl.when(i>=self.ring)
@@ -155,8 +160,10 @@
             self.cross(i).wait_send(); self.side(i).wait_send()
             for s in range(1,Z): self.hop(i,s).wait_send()
             self.swap(i).wait_send(); self.share(i).wait()
-            self.save(i).start()
-        else: self.save(i).wait()
+            for at,count,place in zip(self.at,self.counts,self.places):
+                @pl.when((i>=at)&(i<at+count))
+                def _(at=at,place=place): self.save(i,place,i-at).start()
+        else: self.save(i,self.places[0],0).wait()
     def relay(self,s):
         p=self.p
         ref=self.all.at[p.z,p.y] if s==0 else self.all.at[p.zat(1-s)]
@@ -184,35 +191,31 @@
         self.run(step*per,per)
 
 class Gather:
-    def __init__(self,S,shards,cuts=None,modes=None,lag=1,ahead=None):
-        self.S=S; self.Z=S//2
+    def __init__(self,S,shards,cuts,modes,lag=2,ahead=1):
+        self.S=S; Z=self.Z=S//2
         pick=lambda a: a if isinstance(a,tuple) else (a,None)
         self.local=[isinstance(a,tuple) and isinstance(a[0],int) for a in shards]
         pairs=[pick(a) for a,m in zip(shards,self.local) if not m]
-        self.inputs=[]; self.source=[]
+        held=[]; self.source=[]
         for a,layer in pairs:
-            k=next((k for k,v in enumerate(self.inputs) if v is a),None)
-            if k is None: k=len(self.inputs); self.inputs.append(a)
+            k=next((k for k,v in enumerate(held) if v is a),None)
+            if k is None: k=len(held); held.append(a)
             self.source.append((k,layer))
+        fold_=lambda s: s[:-2]+(2,2,s[-2]//4,s[-1])
+        self.inputs=[a.reshape(fold_(a.shape)) for a in held]
         self.shapes=[a if m else pick(a)[0].shape[-2:] for a,m in zip(shards,self.local)]
-        self.cuts=cuts or [1]*len(shards)
-        self.units=[(w,a) for w,k in enumerate(self.cuts) for a in range(k)]
-        self.modes=[m for k,ms in zip(self.cuts,modes or ['h']*len(shards)) for m in (ms*k)[:k]]
-        self.lag=lag; Z=self.Z
-        n=len(self.units); k=6*Z-2+2*(Z-1)
-        self.out_shapes=[jax.ShapeDtypeStruct((a*S,b),BF) for a,b in self.shapes]
+        self.cuts=cuts
+        self.units=[(w,a) for w,k in enumerate(cuts) for a in range(k)]
+        self.modes=''.join(modes)
+        n=len(self.units); k=3*Z+1
+        self.out_shapes=[jax.ShapeDtypeStruct((Z,2)+fold_(a),BF) for a in self.shapes]
         self.out_specs=[pl.BlockSpec(memory_space=pl.ANY)]*len(shards)
-        self.scratch=[pltpu.VMEM(a,BF) for a,m in zip(self.shapes,self.local) if m]+[pltpu.SemaphoreType.DMA((n,k)),pltpu.SemaphoreType.DMA((n,k)),pltpu.SemaphoreType.DMA((n,))]
-        D=lag
+        self.scratch=[pltpu.VMEM(fold_(a),BF) for a,m in zip(self.shapes,self.local) if m]+[pltpu.SemaphoreType.DMA((n,k)),pltpu.SemaphoreType.DMA((n,k)),pltpu.SemaphoreType.DMA((n,))]
         self.plan={}
-        add=lambda at,*stage: self.plan.setdefault(at,[]).append(stage)
-        for t in range(1,Z): add(D*t,'z',t)
-        for t in range(Z): add(D*(t+1),'y',t)
-        for t in range(1,Z): add(D*(t+1),'u',t)
-        for t in range(Z): add(D*(t+2),'x',t)
-        add(D*(Z+2),'end',0)
-        self.last=D*(Z+2)
-        self.ahead=n if ahead is None else ahead
+        for t in range(1,Z): self.plan[lag*t]=('z',t)
+        self.plan[lag*Z]=('y',0); self.plan[lag*(Z+1)]=('x',0); self.plan[lag*(Z+2)]=('end',0)
+        self.last=lag*(Z+2)
+        self.ahead=ahead
         self.ticks=n+self.last
     def bind(self,ins,outs,scr):
         mine=list(scr[:-3]); source=list(self.source); self.i=[]
@@ -222,34 +225,24 @@
                 k,layer=source.pop(0)
                 self.i.append(ins[k] if layer is None else ins[k].at[layer])
         self.o=outs; self.ss,self.rs,self.ls=scr[-3:]; self.p=Place(self.S); return self
-    def cols(self,u):
-        w,a=self.units[u]; wide=self.shapes[w][1]//self.cuts[w]
-        return pl.ds(a*wide,wide)
-    def rows(self,u,zo,yy,off,ln):
-        w=self.units[u][0]; n=self.shapes[w][0]; q=n//4
-        return self.o[w].at[pl.ds(al((2*zo+yy)*n+off*q,q),ln*q),self.cols(u)]
-    def half(self,u,t): return self.rows(u,self.p.zat(-t),self.p.y,2*self.p.c,2)
-    def quarter(self,u,t,yy,x): return self.rows(u,self.p.zat(-t),yy,2*self.p.c+x,1)
-    def mine(self,u,off,ln):
-        w=self.units[u][0]; q=self.shapes[w][0]//4
-        return self.i[w].at[pl.ds(al(off*q,q),ln*q),self.cols(u)]
-    def cp(self,u,kind,t):
-        p=self.p; Z=self.Z; h=self.modes[u]=='h'
-        k={'z':t-1,'y':Z-1+t,'x':2*Z-1+t,'cz':3*Z-1+t-1,'cy':4*Z-2+t,'cx':5*Z-2+t,'u':6*Z-2+t-1,'cu':7*Z-3+t-1}[kind]
+    def cp(self,u,kind,t=0):
+        p=self.p; Z=self.Z; h=self.modes[u]=='h'; w,a=self.units[u]
+        wide=self.shapes[w][1]//self.cuts[w]; cs=pl.ds(a*wide,wide); o=self.o[w]; i=self.i[w]
+        k={'z':t-1,'y':Z-1+t,'u':2*Z-1+t-1,'x':3*Z-2,'a':3*Z-1,'b':3*Z}[kind]
         if kind=='z':
-            dst=self.half(u,t-1) if h else self.quarter(u,t-1,p.y,p.x); src=dst; dev=p.next
-            if t==1: src=self.mine(u,2*p.c,2) if h else self.mine(u,2*p.c+p.x,1)
-        elif kind=='y': dst=self.quarter(u,t,p.y,p.x); src=self.mine(u,2*p.c+p.x,1) if t==0 else dst; dev=p.over_y
-        elif kind=='x': src=dst=self.quarter(u,t,1-p.y,p.x); dev=p.over_x
-        elif kind=='u': src=dst=self.quarter(u,t,p.y,p.x); dev=p.over_x
-        elif kind=='cz': src=dst=self.half(u,t) if h else self.quarter(u,t,p.y,p.x); dev=p.twin
-        elif kind=='cu': src=dst=self.quarter(u,t,p.y,1-p.x); dev=p.twin
-        elif kind=='cy': src=dst=self.quarter(u,t,1-p.y,p.x); dev=p.twin
-        else: src=dst=self.quarter(u,t,1-p.y,1-p.x); dev=p.twin
+            zo=p.zat(1-t); dev=p.next
+            dst=o.at[zo,p.y,p.c,:,:,cs] if h else o.at[zo,p.y,p.c,p.x,:,cs]; src=dst
+            if t==1: src=i.at[p.c,:,:,cs] if h else i.at[p.c,p.x,:,cs]
+        elif kind=='y':
+            dst=src=o.at[p.zat(-t),p.y,p.c,p.x,:,cs]; dev=p.over_y
+            if t==0: src=i.at[p.c,p.x,:,cs]
+        elif kind=='u': src=dst=o.at[p.zat(-t),p.y,p.c,p.x,:,cs]; dev=p.over_x
+        elif kind=='x': src=dst=o.at[:,1-p.y,p.c,p.x,:,cs]; dev=p.over_x
+        else: src=dst=o.at[:,p.y if kind=='a' else 1-p.y,p.c,:,:,cs]; dev=p.twin
         return pltpu.make_async_remote_copy(src,dst,self.ss.at[u,k],self.rs.at[u,k],device_id=dev,device_id_type=MESH)
     def own(self,u):
-        w=self.units[u][0]; n=self.shapes[w][0]
-        return pltpu.make_async_copy(self.i[w].at[:,self.cols(u)],self.o[w].at[pl.ds(al(self.p.s*n,n),n),self.cols(u)],self.ls.at[u])
+        p=self.p; w,a=self.units[u]; wide=self.shapes[w][1]//self.cuts[w]; cs=pl.ds(a*wide,wide)
+        return pltpu.make_async_copy(self.i[w].at[p.c,:,:,cs],self.o[w].at[p.z,p.y,p.c,:,:,cs],self.ls.at[u])
     def open(self,u):
         self.cp(u,'z',1).start(); self.cp(u,'y',0).start(); self.own(u).start()
     def begin(self):
@@ -262,35 +255,31 @@
             if t+1<Z: self.cp(u,'z',t+1).start()
             self.cp(u,'y',t).start()
             if q: self.cp(u,'u',t).start()
-            self.cp(u,'cz',t).start()
         elif kind=='y':
-            self.cp(u,'y',t).wait_recv()
-            self.cp(u,'x',t).start(); self.cp(u,'cy',t).start()
-        elif kind=='u':
-            if q: self.cp(u,'u',t).wait_recv(); self.cp(u,'cu',t).start()
+            for t in range(Z): self.cp(u,'y',t).wait_recv()
+            self.cp(u,'x').start()
+            self.own(u).wait()
+            if not q: self.cp(u,'a').start()
         elif kind=='x':
-            self.cp(u,'x',t).wait_recv(); self.cp(u,'cx',t).start()
+            if q:
+                for t in range(1,Z): self.cp(u,'u',t).wait_recv()
+                self.cp(u,'a').start()
+            self.cp(u,'x').wait_recv(); self.cp(u,'b').start()
         else:
             for t in range(1,Z):
-                self.cp(u,'z',t).wait_send(); self.cp(u,'cz',t).wait()
-                if q: self.cp(u,'u',t).wait_send(); self.cp(u,'cu',t).wait()
-            for t in range(Z):
-                self.cp(u,'y',t).wait_send(); self.cp(u,'x',t).wait_send(); self.cp(u,'cy',t).wait(); self.cp(u,'cx',t).wait()
-            self.own(u).wait()
+                self.cp(u,'z',t).wait_send()
+                if q: self.cp(u,'u',t).wait_send()
+            for t in range(Z): self.cp(u,'y',t).wait_send()
+            self.cp(u,'x').wait_send(); self.cp(u,'a').wait(); self.cp(u,'b').wait()
     def run(self,lo,count):
+        n=len(self.units)
         for i in range(lo,min(lo+count,self.ticks)):
-            for u in range(len(self.units)):
-                if u>=self.ahead and i==u-self.ahead: self.open(u)
-            for u in range(len(self.units)):
-                for s in self.plan.get(i-u,[]): self.stage(u,*s)
+            if self.ahead<=i+self.ahead<n: self.open(i+self.ahead)
+            for u in range(n):
+                s=self.plan.get(i-u)
+                if s: self.stage(u,*s)
     def done(self,w):
         return max(u for u,(a,_) in enumerate(self.units) if a==w)+self.last+1
-    def spread(self,step,steps):
-        per=-(-self.ticks//steps)
-        for g in range(steps):
-            if g*per>=self.ticks: break
-            @pl.when(step==g)
-            def _(g=g): self.run(g*per,per)
 
 VM=60<<20
 def call(body,name,grid,ins,in_specs,outs,out_specs,scratch,side=None,cid=None):
@@ -308,13 +297,6 @@
         out_specs=list(out_specs)+(side.out_specs if side else []),scratch_shapes=list(scratch)+(side.scratch if side else []),
         compiler_params=pltpu.CompilerParams(vmem_limit_bytes=VM,**(dict(collective_id=cid,has_side_effects=True) if side else {})),name=name)(*ins,*extra)
     return out[:c],out[c:]
-
-def alone(comm):
-    comm.begin(); comm.run(0,comm.ticks)
-def gather(S,shards,cid,**kw):
-    return call(alone,'gather_weights',(),[],[],[],[],[],Gather(S,shards,**kw),cid)[1]
-def scatter(S,grads,cid):
-    return call(alone,'sum_gradients',(),[],[],[],[],[],Scatter(S,grads),cid)[1][0]
 
 
 CH=64
@@ -631,11 +613,11 @@
     return jnp.concatenate(dqs,axis=0),(tn(ds_ref[...],q_ref[:,cols])*scale).astype(BF),tn(p_ref[...],g_ref[:,cols]).astype(BF)
 
 VECTOR_ROWS=64
-def late(S,packed,p,grad,table,pick,heads,hid1,ai,dx2,x1,gains,hid0,act,dsl,fi,fo,tokens,s5,s4,s23,ddw,dbin1,taps,ready,cid):
+def late(S,packed,p,grad,table,pick,heads,hid1,ai,dx2,x1,gains,hid0,act,dsl,fi,fo,tokens,s5,s4,s23,ddw,dbin1,taps,ready,places,out_shapes,cid):
     steps,width=x1.shape; size=width//heads; wide=SUB[1]
     A=width//128; B=3*width//wide; C=act.shape[1]//wide; D=C; per=128//size
     assert act.shape[1]//S==wide and width//S==SUB[0] and wide//SUB[0]<=4
-    comm=Scatter(S,ready+[B,C,1,D],common=(sum(a.shape[0] for a in ready)+B+C,VECTOR_ROWS,table.shape[0]//S))
+    comm=Scatter(S,ready+[B,C,1,D],places,out_shapes,common=(sum(a.shape[0] for a in ready)+B+C,VECTOR_ROWS,table.shape[0]//S))
     head=lambda o:pl.BlockSpec((steps,128),lambda j:(0,o*A+jnp.minimum(j,A-1)))
     tile=lambda lo,n:(lambda j:jnp.minimum(jnp.maximum(j-lo,0),n-1))
     tb,tc=tile(A,B),tile(A+B,C)
@@ -655,27 +637,25 @@
 def early_kernel(heads,taps,comm,gain_in,shift_in,inner_in,outer_in,packed_in,mixed_in,taps_in,tok_ref,cot_ref,valid_ref,mask_ref,table_ref,pick_ref,
         hid0_ref,act0_ref,dsl0_ref,x1_ref,hid1_ref,packed_ref,mixed_ref,p_ref,x2_ref,chid_ref,up_ref,depth_ref,cact_ref,x3_ref,hid4_ref,act1_ref,dsl1_ref,dx4_ref,res_ref,s5_ref,vec_ref,
         own_ref,land_ref,land_sem,acc_ref,wa_ref,wb_ref,sem_a,sem_b,rel_ref,qkv_ref,pad_ref,wide_ref):
-    steps,width=tok_ref.shape; tile=wa_ref.shape[2]; S=comm.S
+    steps,width=tok_ref.shape; tile=wa_ref.shape[-1]; S=comm.S
     small,fi0,fo0,ai,ao,pi,po,fi1,fo1=comm.o
-    F=fi0.shape[1]//tile; B=ai.shape[1]//tile; A=width//128; M0,M1,M2=ao.shape[1]//tile,pi.shape[1]//tile,po.shape[1]//tile
+    F,B,M0,M1,M2=[w.shape[-1]//tile for w in (fi0,ai,ao,pi,po)]; A=width//128
     size=width//heads
     cut=np.cumsum([0,F,B,A,M0,M1,M2,F]).tolist()
     j=pl.program_id(0)
     L=width//S
     def row(i): return vec_ref[i:i+1,:]
-    def column(w,i,slot): return pltpu.make_async_copy(w.at[:,pl.ds(al(i*tile,tile),tile)],wa_ref.at[slot],sem_a.at[slot])
-    def band(w,i,slot): return pltpu.make_async_copy(w.at[pl.ds(al(i*tile,tile),tile)],wb_ref.at[slot],sem_b.at[slot])
+    def column(w,i,slot): return pltpu.make_async_copy(w.at[:,:,:,:,:,pl.ds(al(i*tile,tile),tile)],wa_ref.at[slot],sem_a.at[slot])
+    def band(w,i,slot): return pltpu.make_async_copy(w.at[i//2,lax.rem(i,2)],wb_ref.at[slot],sem_b.at[slot])
+    def wa(slot): return wa_ref[slot].reshape(width,tile)
     want=[comm.done(2),comm.done(3),comm.done(4),comm.done(5),comm.done(6),comm.done(8)]
-    at={}
-    def plan(steps_,lo,hi):
-        n=len(steps_)
-        for i,st in enumerate(steps_):
-            a,b=lo+(hi-lo)*i//n,lo+(hi-lo)*(i+1)//n
-            if b>a: at[st]=(a,b-a)
-    plan(list(range(F//2-1,cut[1],F//2)),want[0],want[1])
-    plan([cut[2]-1],want[1],want[2])
-    plan(list(range(cut[2]+A//2-1,cut[3],A//2)),want[2],want[4])
-    plan([cut[4]-1,cut[6]-1],want[4],comm.ticks-1)
+    at={}; done=want[0]
+    times=[20/F]*F+[10/B]*B+[35/A]*A+[3]*M0+[2]*(M1-1)+[14]+[3]*M2
+    need={cut[1]-1:want[1],cut[3]-1:want[2],cut[4]-1:want[3],cut[5]-1:want[4],cut[6]-1:comm.ticks-1}
+    for st in range(cut[6]):
+        target=want[0]+int((comm.ticks-1-want[0])*sum(times[:st+1])/sum(times))
+        target=max(target,need.get(st,0))
+        if target>done: at[st]=(done,target-done); done=target
     def ticks():
         for st,(lo,n) in at.items():
             @pl.when(j==st)
@@ -688,13 +668,13 @@
         k=inner_in.shape[1]//L
         for l in range(2):
             for i in range(k): own_ref[Rows.inner+l*k+i:Rows.inner+l*k+i+1,:]=inner_in[l:l+1,i*L:i*L+L].astype(F32)
-        comm.i[0][...]=own_ref[...].astype(BF)
+        comm.i[0][...]=own_ref[...].astype(BF).reshape(comm.i[0].shape)
         comm.begin()
         comm.run(0,want[0])
         cp=pltpu.make_async_copy(small,land_ref,land_sem.at[0]); cp.start()
         column(fi0,0,0).start(); band(fo0,0,0).start()
         cp.wait()
-        for s in range(S): vec_ref[:,s*L:s*L+L]=land_ref[s*Rows.count:(s+1)*Rows.count,:].astype(F32)
+        for s in range(S): vec_ref[:,s*L:s*L+L]=land_ref[s//2,s%2].reshape(Rows.count,L).astype(F32)
         for i in range(steps//QB): rel_ref[i]=tn(table_ref[...],pick_ref[i]).astype(BF)
         def body(r):
             xhat,_r=stats(tok_ref[r,:].astype(F32))
@@ -708,11 +688,11 @@
         @pl.when(i+1<F)
         def _(): column(fi,i+1,lax.rem(tau+1,2)).start(); band(fo,i+1,lax.rem(i+1,2)).start()
         bias=jnp.concatenate([vec_ref[Rows.inner+l*k+a:Rows.inner+l*k+a+1,pl.ds(al(i*L,L),L)] for a in range(k)],axis=1)
-        pre=nn(hid_ref[...],wa_ref[slot])+bias
+        pre=nn(hid_ref[...],wa(slot))+bias
         sg=sigmoid(pre)
         act_ref[...]=(pre*sg).astype(BF)
         dsl_ref[...]=(sg*(1.0+pre*(1.0-sg))).astype(BF)
-        acc_ref[...]+=nn(act_ref[...],wb_ref[lax.rem(i,2)])
+        acc_ref[...]+=nn(act_ref[...],wb_ref[lax.rem(i,2)].reshape(tile,width))
     @pl.when(j<cut[1])
     def _(): feed_tile(j,j,0,hid0_ref,act0_ref,dsl0_ref,fi0,fo0)
     @pl.when(j==cut[1]-1)
@@ -736,7 +716,7 @@
         def _(): column(w,0,lax.rem(tau,2)).start()
     def here(i): return pl.ds(al(i*tile,tile),tile)
     def pack(i,slot):
-        v=nn(hid1_ref[...],wa_ref[slot])
+        v=nn(hid1_ref[...],wa(slot))
         per=width//tile
         @pl.when(i<per)
         def _(): packed_ref[:,here(i)]=(v+vec_ref[Rows.packed:Rows.packed+1,here(lax.rem(i,per))]).astype(BF)
@@ -763,7 +743,7 @@
                 outs.append(nn(p,qkv_ref[2,:,cols]).astype(BF))
             mixed_ref[rows,pl.ds(al(h*128,128),128)]=jnp.concatenate(outs,axis=1)
     def join(i,slot):
-        x2_ref[:,here(i)]=x1_ref[:,here(i)]+nn(mixed_ref[...],wa_ref[slot])+vec_ref[Rows.mixed:Rows.mixed+1,here(i)]
+        x2_ref[:,here(i)]=x1_ref[:,here(i)]+nn(mixed_ref[...],wa(slot))+vec_ref[Rows.mixed:Rows.mixed+1,here(i)]
         @pl.when(i==M0-1)
         def _():
             def body(r):
@@ -772,7 +752,7 @@
             chunks(steps,body)
     stream(ao,cut[3],M0,F+B,join)
     def raise_(i,slot):
-        wide_ref[:,here(i)]=nn(chid_ref[...],wa_ref[slot])
+        wide_ref[:,here(i)]=nn(chid_ref[...],wa(slot))
         @pl.when(i==M1-1)
         def _():
             def gate(k,c):
@@ -794,7 +774,7 @@
             chunks(steps,body)
     stream(pi,cut[4],M1,F+B+M0,raise_)
     def lower(i,slot):
-        x3_ref[:,here(i)]=x2_ref[:,here(i)]+nn(cact_ref[...],wa_ref[slot])
+        x3_ref[:,here(i)]=x2_ref[:,here(i)]+nn(cact_ref[...],wa(slot))
         @pl.when(i==M2-1)
         def _():
             def body(r):
@@ -827,9 +807,10 @@
             s5_ref[1]+=fold(dy)
         chunks(steps,body)
 
+LAG=2; CUTS=[1,4,4,3,1,2,1,4,4]; MODES=['h','qhhq','hhqh','hqh','h','qh','h','qhhq','hhqh']
 def early(S,vectors,tokens,cot,valid,mask,table,pick,heads,weights,cid):
     steps,width=tokens.shape; tile=512; taps=vectors[-1].shape[0]; L=vectors[0].shape[1]
-    comm=Gather(S,[(Rows.count,L)]+weights,cuts=[1,2,2,2,1,1,1,2,2],modes=['h','hq','hh','qh','h','q','h','hq','hh'],ahead=4)
+    comm=Gather(S,[(Rows.count,L)]+weights,cuts=CUTS,modes=MODES,lag=LAG)
     hidden=comm.shapes[1][1]; size=width//heads
     F,B,A=hidden//tile,comm.shapes[3][1]//tile,width//128
     M=[comm.shapes[i][1]//tile for i in (4,5,6)]
@@ -845,9 +826,10 @@
     for i,t in ((1,f0),(2,f0),(15,f1),(16,f1)): specs[i]=pl.BlockSpec((steps,tile),lambda j,t=t:(0,t(j)))
     specs[7]=pl.BlockSpec((128//size,steps,steps),lambda j:(at(j),0,0))
     V=pltpu.VMEM; sem=lambda n: pltpu.SemaphoreType.DMA((n,))
-    scratch=[V((Rows.count,L),F32),V((S*Rows.count,L),BF),sem(1),V((steps,width),F32),V((2,width,tile),BF),V((2,tile,width),BF),sem(2),sem(2),
+    scratch=[V((Rows.count,L),F32),V(comm.out_shapes[0].shape,BF),sem(1),V((steps,width),F32),V((2,)+comm.out_shapes[1].shape[:-1]+(tile,),BF),V((2,)+comm.out_shapes[2].shape[2:],BF),sem(2),sem(2),
         V((steps//QB,size,steps+QB),BF),V((3,steps,128),BF),V((steps+PAD,width),F32),V((steps,2*width),F32)]
-    return call(functools.partial(early_kernel,heads,taps),'gather_and_forward',(cut[-1],),ins,[whole(a.shape) for a in ins],outs,specs,scratch,comm,cid)
+    out=call(functools.partial(early_kernel,heads,taps),'gather_and_forward',(cut[-1],),ins,[whole(a.shape) for a in ins],outs,specs,scratch,comm,cid)
+    return out[0],[a.reshape(-1,a.shape[-1]) for a in out[1]]
 
 
 def local(S,R,tokens,lengths,cotangent,norm_gain,norm_shift,feed_in,feed_in_bias,feed_out,feed_out_bias,attention_in,attention_in_bias,attention_out,attention_out_bias,relative_table,pointwise_in,depthwise,pointwise_out):
@@ -867,20 +849,20 @@
     (dx3,dfi1,dfo1,dbin1,s4),_=feed_back(dx4,x3,vec,hid4,act1,dsl1,fi1,fo1,4,F32)
     (dx2,dpv,dpo,dpi,dao,ddw,s23),_=middle_back(dx3,depth,up,chid,cact,mixed,x2,vec,valid,ao,pi,po,taps)
     ready=[dfi1,flat(dfo1),dpo,dpi,dao]
-    (dtok,),outs=late(S,packed,p,dpv,table,pick,HEADS,hid1,ai,dx2,x1,vec,hid0,act0,dsl0,fi0,fo0,tokens,s5,s4,s23,ddw,dbin1,taps,ready,7)
-    sums,common=outs[0],outs[-1]
+    across=width//SUB[1]; k=dfi1.shape[0]
+    places=[(0,1,k),(1,1,across),(5,None,across),(4,None,2*across),(3,None,across),(2,None,3*across),(0,0,k),(6,None,1),(1,0,across)]
+    shapes=[feed_in.shape,feed_out.shape]+[a.shape for a in (attention_in,attention_out,pointwise_in,pointwise_out)]+[SUB]
+    (dtok,),outs=late(S,packed,p,dpv,table,pick,HEADS,hid1,ai,dx2,x1,vec,hid0,act0,dsl0,fi0,fo0,tokens,s5,s4,s23,ddw,dbin1,taps,ready,places,shapes,7)
+    sums=list(outs[:7])+[outs[-1]]
     if R>4:
         groups=[[g*4+i for g in range(R//4)] for i in range(4)]
-        sums,common=[lax.psum(a,'rep',axis_index_groups=groups) for a in (sums,common)]
-    at=np.cumsum([0]+[a.shape[0] for a in ready]+[3*width//SUB[1],fi0.shape[1]//SUB[1],1,fi0.shape[1]//SUB[1]]).tolist()
-    gfi1,gfo1,gpo,gpi,gao,gai,gfi0,small,gfo0=[sums[a:b] for a,b in zip(at,at[1:])]
-    def by_column(u): return u.transpose(1,0,2).reshape(SUB[0],-1).astype(F32)
-    def by_row(u): return u.reshape(-1,width//SUB[1],*SUB).transpose(0,2,1,3).reshape(-1,width).astype(F32)
-    vec=small[0].astype(F32); L=norm_gain.shape[1]
-    ggain,gshift,gbout,gpbias,gmbias=[vec[a:b,:L] for a,b in ((0,6),(6,12),(12,14),(14,16),(16,17))]
-    gbin=vec[17:19]; gdw=vec[32:32+taps,:L]
-    gtab=common.reshape(-1,SUB[1])[:rows,:relative_table.shape[1]].astype(F32)
-    return (result,dtok,ggain,gshift,jnp.stack([by_column(gfi0),by_column(gfi1)]),gbin,jnp.stack([by_row(gfo0),by_row(gfo1)]),gbout,by_column(gai),gpbias,by_column(gao),gmbias[0],gtab,by_column(gpi),gdw,by_column(gpo))
+        sums=[lax.psum(a,'rep',axis_index_groups=groups) for a in sums]
+    gfi,gfo,gai,gao,gpi,gpo,small,common=[a.astype(F32) for a in sums]
+    L=norm_gain.shape[1]
+    ggain,gshift,gbout,gpbias,gmbias=[small[a:b,:L] for a,b in ((0,6),(6,12),(12,14),(14,16),(16,17))]
+    gbin=small[17:19]; gdw=small[32:32+taps,:L]
+    gtab=common.reshape(-1,SUB[1])[:rows,:relative_table.shape[1]]
+    return (result,dtok,ggain,gshift,gfi,gbin,gfo,gbout,gai,gpbias,gao,gmbias[0],gtab,gpi,gdw,gpo)
 
 HEADS=16
 

time: 679 us -> 647 us (0.953)
  local copies, waits for them, and re-layouts: 34 us -> 11.5 us
  Pallas kernels: 623 us -> 615 us
    convert_element_type x10 -> x0, local copies, waits for them, and re-layouts: 10.9 us -> none  [the longest x4 6.49 us: by_row(): u.reshape(-1, width // SUB[1], *SUB).transpose(0, 2, 1, 3)]
    unnamed x17 -> x14, local copies, waits for them, and re-layouts: 13.5 us -> 2.87 us
    convert_element_type x5 -> x7, other arithmetic: 5.22 us -> 12.9 us  [local(): gfi, gfo, gai, gao, gpi, gpo, small, common = [a.astype(F32) for a in sums]]
    pallas_call x4, Pallas kernels: 623 us -> 615 us  [call(): pl.pallas_call(kernel, grid=grid, out_shape=list(outs) + (side.out_shapes...]
where the time goes in v2:
time: 647 us; the launch traced here: 642 us
  Pallas kernels  615 us (95%)
  other arithmetic  13.5 us (2%)
  local copies, waits for them, and re-layouts  11.5 us (2%)
    pallas_call x4, Pallas kernels, call(): pl.pallas_call(kernel, grid=grid, out_shape=list(outs) + (side.out_shapes...  615 us

profile of v2, /device:TPU:0, one launch (start us, length us, event | category | flops | bytes accessed | tf_op | source)
XLA Modules:
  0.0 642.0 jit_solution(2023839599212994536)
XLA Ops:
  1.3 0.6 broadcast_in_dim.23.refs_10_
  1.9 0.8 copy.34
  2.7 0.6 pad.4.refs_11_.refs_5_
  3.4 0.8 broadcast_in_dim.20.refs_9_.refs_8_
  4.2 258.4 %gather_and_forward.1 = (bf16[512,1024]{1,0:T(8,128)(2,1)}, bf16[512,4096]{1,0:T(8,128)(2,1)}, bf16[512,4096]{1,0:T(8,128)(2,1)}, f32[512,1024]{1,0:T(8,128)}, b...) custom-call(bf16[6,128]{1,0:T(8,128)(2,1)} %refs_0_.1, ...), custom_call_target="tpu_custom_call" | custom-call | tf_op jit(solution)/shard_map/gather_and_forward/pallas_call | solution.py:296
  262.6 29.1 %feed_forward_back.1 = (f32[512,1024]{1,0:T(8,128)}, bf16[8,1024,512]{2,1,0:T(8,128)(2,1)}, bf16[8,8,128,512]{3,2,1,0:T(8,128)(2,1)}, f32[8,4096]{1,0:T(8,128)}, f32[3,8,1024]{2,1,0:T(8,128)}) custom-call(f32[512,1024]{1,0:T(8,128)} %get-tuple-element.69.refs_0_, f32[512,1024]{1,0:T(8,128)} %get-tuple-element.70.refs_1_, ...), custom_call_target="tpu_custom_call" | custom-call | tf_op jit(solution)/shard_map/feed_forward_back/pallas_call | solution.py:296
  291.7 47.8 %convolution_module_back.1 = (f32[512,1024]{1,0:T(8,128)}, bf16[512,1024]{1,0:T(8,128)(2,1)}, bf16[2,1024,512]{2,1,0:T(8,128)(2,1)}, bf16[4,1024,512]{2,1,0:T(8,...) custom-call(f32[512,1024]{1,0:T(8,128)} %get-tuple-element.77.refs_0_, ...), custom_call_target="tpu_custom_call" | custom-call | tf_op jit(solution)/shard_map/convolution_module_back/pallas_call | solution.py:296
  339.5 280.1 %attend_back_and_sums.1 = (bf16[512,1024]{1,0:T(8,128)(2,1)}, bf16[2,128,4096]{2,1,0:T(8,128)(2,1)}, bf16[2,512,1024]{2,1,0:T(8,128)(2,1)}, bf16[128,3072]{1,0:T...) custom-call(bf16[512,3072]{1,0:T(8,128)(2,1)} %get-tuple-element.67., ...), custom_call_target="tpu_custom_call" | custom-call | tf_op jit(solution)/shard_map/attend_back_and_sums/pallas_call | solution.py:296
  619.6 0.0 copy-start.4
  619.6 0.0 copy-start.1
  619.6 1.4 fusion.2
  621.0 1.3 slice.38
  622.3 1.3 fusion.3
  623.6 1.3 slice.43
  624.9 0.7 slice.42
  625.6 0.1 copy.36
  625.7 0.6 slice.34
  626.4 0.9 convert_element_type.36
  627.3 0.5 slice_bitcast_fusion
  627.8 1.8 convert_element_type.40
  629.6 1.8 convert_element_type.42
  631.4 2.1 convert_element_type.41
  633.5 0.0 copy-done.4
  633.5 0.0 copy-start
  633.5 1.3 convert_element_type.39
  634.8 0.0 copy-done.1
  634.8 2.5 convert_element_type.37
  637.3 0.0 copy-done
  637.3 0.0 copy-start.2
  637.3 0.0 copy-start.3
  637.3 2.5 convert_element_type.38
  639.8 0.0 copy-done.2
  639.8 1.0 copy.40
  640.8 0.0 copy-done.3
  640.8 1.0 copy.41
  (2 shorter events, 0.0 us)
Async XLA Ops:
  619.6 14.0 %copy-start.4 = (bf16[128,3072]{1,0:T(8,128)(2,1)S(1)}, bf16[128,3072]{1,0:T(8,128)(2,1)}, u32[]{:S(2)}) copy-start(bf16[128,3072]{1,0:T(8,128)(2,1)} %get-tuple-element.111) | copy-start | bytes 2359300
  619.6 15.3 %copy-start.1 = (bf16[2,128,4096]{2,1,0:T(8,128)(2,1)S(1)}, bf16[2,128,4096]{2,1,0:T(8,128)(2,1)}, u32[]{:S(2)}) copy-start(bf16[2,128,4096]{2,1,0:T(8,128)(2,1)} %get-tuple-element.109) | copy-start | bytes 6291460
  633.5 3.8 copy-start
  637.3 2.5 copy-start.2
  637.3 3.5 copy-start.3

commit v3 on v2

--- a/solution.py
+++ b/solution.py
@@ -51,41 +51,38 @@
 SUB=(128,512)
 class Scatter:
     OWN=18; RING=6; GAP=2
-    def __init__(self,S,sources,places,out_shapes,common=None):
-        self.places=places
+    def __init__(self,S,counts,places,out_shapes,common=None,pause=None):
+        self.places=places; self.counts=counts
         self.common=common
         self.S=S; Z=S//2
-        counts=[a if isinstance(a,int) else a.shape[0] for a in sources]
         n=self.n=sum(counts)
         (rows,wide)=SUB
         h,q=rows//2,rows//4
         self.h,self.q,self.Z=h,q,Z
-        self.made=[isinstance(a,int) for a in sources]
-        self.at=np.cumsum([0]+counts).tolist(); self.counts=counts
-        self.inputs=[a.reshape(a.shape[0],Z,2,2,h,wide) for a in sources if not isinstance(a,int)]
+        self.at=np.cumsum([0]+counts).tolist()
+        self.inputs=[]
         self.finals=len(out_shapes)
-        self.out_shapes=[jax.ShapeDtypeStruct(a,BF) for a in out_shapes]+[jax.ShapeDtypeStruct((k,Z,2,2,h,wide),BF) for k,m in zip(counts,self.made) if m]
+        self.out_shapes=[jax.ShapeDtypeStruct(a,BF) for a in out_shapes]+[jax.ShapeDtypeStruct((n,Z,2,2,h,wide),BF)]
         G=self.GAP
         self.lag=[0]+[G*k for k in range(1,5+Z)]
         self.lag[4+Z]=self.lag[3+Z]+1
         self.lag.append(self.lag[4+Z]+1)
-        self.ticks=n+self.lag[-1]
+        self.gate,self.wait=pause or (n,0)
+        self.ticks=n+self.wait+self.lag[-1]
         own,ring=min(n,self.OWN),min(n,self.RING)
         self.slots=own; self.ring=ring
-        assert own>=self.lag[-1] or own==n
+        assert own>self.lag[-1] and n+self.wait<2*(self.gate+self.wait)
         V=lambda *d: pltpu.VMEM(d,BF)
         self.scratch=[V(n,rows,wide),V(own,Z,2,h,wide),V(ring,Z,2,h,wide),V(ring,Z,q,wide),V(ring,Z,q,wide),V(ring,Z-1,h,wide),V(ring,h,wide),
             pltpu.SemaphoreType.DMA((n,)),pltpu.SemaphoreType.DMA((n,5+Z)),pltpu.SemaphoreType.DMA((n,5+Z)),pltpu.SemaphoreType.DMA((n,2)),pltpu.SemaphoreType.REGULAR((4+Z,))]
         if common:
             self.out_shapes.append(jax.ShapeDtypeStruct((Z,2,common[2],wide),BF))
             self.scratch+=[V(Z,2,common[2],wide),pltpu.SemaphoreType.DMA((Z,)),pltpu.SemaphoreType.DMA((Z,)),pltpu.SemaphoreType.DMA((1,))]
-            self.begin_common=common[0]+self.lag[-1]+1
+            self.begin_common=common[0]+self.wait+self.lag[-1]+1
             self.ticks=max(self.ticks,self.begin_common+Z+1)
         self.out_specs=[pl.BlockSpec(memory_space=pl.ANY)]*len(self.out_shapes)
     def bind(self,ins,outs,scr):
-        k=self.finals; self.out=outs[:k]; ins,made=list(ins),list(outs[k:k+sum(self.made)])
-        self.makes=list(made)
-        self.g=[made.pop(0) if m else ins.pop(0) for m in self.made]
+        self.out=outs[:self.finals]; self.made=outs[self.finals]
         if self.common: self.all,self.cs,self.ct,self.co=scr[-4:]; self.all_out=outs[-1]; scr=scr[:-4]
         self.o,self.own,self.cr,self.xr,self.yr,self.zr,self.fr,self.os,self.ss,self.rs,self.ls,self.free=scr
         self.p=Place(self.S); return self
@@ -94,10 +91,10 @@
     def remote(self,i,k,src,dst,dev):
         return pltpu.make_async_remote_copy(src,dst,self.ss.at[i,k],self.rs.at[i,k],device_id=dev,device_id_type=MESH)
     def column(self,yy): return 1-self.p.y if yy else self.p.y
-    def first(self,ref,i,yy):
-        return self.remote(i,yy,ref.at[:,self.column(yy),1-self.p.c],self.cr.at[self.land(i),:,self.column(yy)],self.p.twin)
-    def load(self,ref,i,yy):
-        return pltpu.make_async_copy(ref.at[:,self.column(yy),self.p.c],self.own.at[self.slot(i),:,self.column(yy)],self.ls.at[i,yy])
+    def first(self,i,yy):
+        return self.remote(i,yy,self.made.at[i,:,self.column(yy),1-self.p.c],self.cr.at[self.land(i),:,self.column(yy)],self.p.twin)
+    def load(self,i,yy):
+        return pltpu.make_async_copy(self.made.at[i,:,self.column(yy),self.p.c],self.own.at[self.slot(i),:,self.column(yy)],self.ls.at[i,yy])
     def part(self,i,col,x): return self.own.at[self.slot(i),:,col,pl.ds(al(x*self.q,self.q),self.q)]
     def cross(self,i): return self.remote(i,2,self.part(i,1-self.p.y,1-self.p.x),self.xr.at[self.land(i)],self.p.over_x)
     def side(self,i): return self.remote(i,3,self.part(i,1-self.p.y,self.p.x),self.yr.at[self.land(i)],self.p.over_y)
@@ -119,17 +116,14 @@
             def _(): pl.semaphore_signal(self.free.at[k],inc=1,device_id=dev,device_id_type=MESH)
     def begin(self): self.p.greet()
     def phase(self,k,i):
-        p=self.p; Z=self.Z; some=self.g[0].at[0]; here=self.slot(i); land=self.land(i)
+        p=self.p; Z=self.Z; here=self.slot(i); land=self.land(i)
         if k==0:
             self.ask(i,0)
-            for at,count,ref in zip(self.at,self.counts,self.g):
-                @pl.when((i>=at)&(i<at+count))
-                def _(at=at,ref=ref):
-                    for yy in (1,0): self.first(ref.at[i-at],i,yy).start(); self.load(ref.at[i-at],i,yy).start()
+            for yy in (1,0): self.first(i,yy).start(); self.load(i,yy).start()
         elif k==1:
             for yy in (1,0):
                 col=self.column(yy)
-                self.load(some,i,yy).wait(); self.first(some,i,yy).wait_recv()
+                self.load(i,yy).wait(); self.first(i,yy).wait_recv()
                 self.own[here,:,col]=self.own[here,:,col]+self.cr[land,:,col]
                 if yy: self.ask(i,1); self.cross(i).start()
             self.tell(i,0,p.twin)
@@ -156,7 +150,7 @@
             self.tell(i,2+Z,p.over_x)
             self.share(i).start()
         elif k==4+Z:
-            for yy in (0,1): self.first(some,i,yy).wait_send()
+            for yy in (0,1): self.first(i,yy).wait_send()
             self.cross(i).wait_send(); self.side(i).wait_send()
             for s in range(1,Z): self.hop(i,s).wait_send()
             self.swap(i).wait_send(); self.share(i).wait()
@@ -178,9 +172,9 @@
     def run(self,lo,count):
         def tick(u):
             for k in reversed(range(len(self.lag))):
-                i=u-self.lag[k]
-                @pl.when((i>=0)&(i<self.n))
-                def _(k=k,i=i): self.phase(k,i)
+                v=u-self.lag[k]; turn=self.gate+self.wait
+                @pl.when((v>=0)&(v<self.n+self.wait)&((v<self.gate)|(v>=turn)))
+                def _(k=k,v=v): self.phase(k,v-self.wait*(v//turn) if self.wait else v)
             if self.common:
                 for k in range(self.Z+1):
                     @pl.when(u==self.begin_common+k)
@@ -343,293 +337,341 @@
         for a,k in use: acc=acc+w_ref[k:k+1,cols]*slab[8*a:8*a+RC]
     return acc
 
-def points(comm,count):
-    at=[-1]
-    def point():
-        if not comm: return
-        if at[0]<0: comm.begin()
-        else:
-            per=-(-comm.ticks//count)
-            comm.run(at[0]*per,per)
-        at[0]+=1
-    return point
-
-def into_units(ref,rows):
-    n,w=SUB; across=rows.shape[1]//w
-    for a in range(rows.shape[0]//n):
-        for b in range(across): ref[a*across+b,0]=rows[a*n:a*n+n,b*w:b*w+w]
-
-def feed_back_kernel(norm,d_ref,x_ref,gain_ref,hid_ref,act_ref,dsl_ref,fi_ref,fo_ref,
-        out_ref,dfi_ref,dfo_ref,dbin_ref,sums_ref,df_ref,acc_ref,turn_ref):
-    steps=x_ref.shape[0]; j=pl.program_id(0)
-    @pl.when(j==0)
-    def _():
+VECTOR_ROWS=64
+def plan_ticks(comm,phases,pace,limit):
+    at=[]; done=0; spent=0.0
+    for st,t in enumerate(phases):
+        spent+=t
+        target=max(done,min(int(spent/pace),limit(st),comm.ticks))
+        at.append((done,target-done)); done=target
+    return at
+
+def backward_kernel(taps,size,comm,q_ref,k_ref,v_ref,p_ref,table_ref,pick_ref,vec_ref,valid_ref,tok_ref,s5_ref,
+        dx4,x3,x2,x1,hid4,hid1,hid0,chid,cact,mixed,up,depth,act1,act0,dsl1,dsl0,fi1,fo1,ai,ao,pi,po,fi0,fo0,out_ref,
+        d_ref,x_ref,acc_ref,low_ref,turn_ref,hid_ref,big_ref,stage_ref,ds_ref,grad_ref,wa_ref,wb_ref,wd_ref,pad_ref,tail_ref,rows_ref,sums_ref,ddw_ref,dbin_ref,psum_ref,dtab_ref,
+        sem_d,sem_x,sem_hid,sem_big,sem_a,sem_b,sem_c,stage_sem):
+    steps,width=d_ref.shape; wide=SUB[1]; S=comm.S; across=width//wide; CUT=act1.shape[1]//S
+    F=act1.shape[1]//wide; A=width//128; B=ai.shape[1]//wide; M0,M1,M2=po.shape[1]//wide,pi.shape[1]//wide,ao.shape[1]//wide
+    cut=np.cumsum([0,F,F,M0,1,M1,M2,A,B,F,F,1]).tolist()
+    FB,FD,MP,MC,MI,MO,AT,PB,CB,CD,EN=cut[:11]
+    units=np.cumsum([0,F,F,M0,M1,M2,B,F,1,F]).tolist()
+    j=pl.program_id(0)
+    made=[]; n=0
+    for st in range(cut[-1]):
+        n+=0 if MC<=st<MI or AT<=st<PB or st==EN else 1
+        if st==CD: n+=1
+        made.append(n)
+    def limit(st):
+        if AT<=st<PB: return comm.gate+comm.wait
+        return made[st]-2+(comm.wait if st>=PB else 0)
+    times=[2.9]*F+[1.0]*F+[3]*M0+[15]+[2.5]*(M1-1)+[5]+[3]*M2+[4.7]*A+[2.8]*B+[3.8]*F+[1.0]*F+[0]
+    at=plan_ticks(comm,times,PACE,limit)
+    def ticks(step,share=(0,1)):
+        lo,n=at[step]; a,b=n*share[0]//share[1],n*(share[0]+1)//share[1]
+        if b>a: comm.run(lo+a,b-a)
+    def ticks_of(lo,hi):
+        for st in range(lo,hi):
+            if at[st][1]:
+                @pl.when(j==st)
+                def _(st=st): ticks(st)
+    def phase(lo,hi):
+        return pl.when((j>=lo)&(j<hi))
+    def last(step): return pl.when(j==step)
+    def fill(src,dst,sem): return pltpu.make_async_copy(src,dst,sem)
+    def row(i): return vec_ref[i:i+1,:]
+    def here(i): return pl.ds(al(i*wide,wide),wide)
+    def column(w,i,slot): return fill(w.at[:,here(i)],wa_ref.at[slot],sem_a.at[slot])
+    def band(w,i): return fill(w.at[here(i)],wb_ref.at[lax.rem(i,2)],sem_b.at[lax.rem(i,2)])
+    def slope(w,i): return fill(w.at[:,here(i)],wd_ref.at[lax.rem(i,2)],sem_c.at[lax.rem(i,2)])
+    def load(ref,dst,sem): return fill(ref,dst,sem.at[0])
+    def lefts(act,a,slot):
+        return [fill(act.at[:,pl.ds(al(s*CUT+a*SUB[0],SUB[0]),SUB[0])],big_ref.at[slot,:,pl.ds(s*SUB[0],SUB[0])],sem_big.at[slot,s]) for s in range(S)]
+    def whole_big(src,slot): return fill(src,big_ref.at[slot],sem_big.at[slot,0])
+    def put(q): return fill(stage_ref.at[lax.rem(q,2)],comm.made.at[q],stage_sem.at[lax.rem(q,2)])
+    first_late=units[5]
+    def unit(q,value):
+        @pl.when((q>=2)&((q<first_late)|(q>=first_late+2)))
+        def _(): put(q-2).wait()
+        stage_ref[lax.rem(q,2)]=value.reshape(stage_ref.shape[1:])
+        put(q).start()
+    def stream(w,lo,n,tau0,use):
+        @phase(lo,lo+n)
+        def _():
+            i=j-lo; slot=lax.rem(tau0+i,2)
+            column(w,i,slot).wait()
+            @pl.when(i+1<n)
+            def _(): column(w,i+1,lax.rem(tau0+i+1,2)).start()
+            use(i,wa_ref.at[slot])
+    def ahead(w,tau): column(w,0,tau%2).start()
+    tau=np.cumsum([0,F,M0,M1,M2,B]).tolist()
+
+    def feed_step(i,w_out,slopes,q,side,fi):
+        band(w_out,i).wait(); slope(slopes,i).wait()
+        @pl.when(i+1<F)
+        def _(): band(w_out,i+1).start(); slope(slopes,i+1).start()
+        s=lax.rem(i,2)
+        dpre=(nt(low_ref[:,:width],wb_ref[s])*wd_ref[s].astype(F32)).astype(BF)
+        dbin_ref[side,:,here(i)]=fold(dpre.astype(F32))
+        acc_ref[...]+=nt(dpre,fi[...])
+        unit(q+i,nn(turn_ref[...],dpre).astype(BF))
+    def norm_step(source,i,at_,after):
+        def body(r):
+            xhat,rstd=stats(source[r,:].astype(F32))
+            dy=acc_ref[r,:]
+            sums_ref[at_]+=fold(dy*xhat); sums_ref[at_+1]+=fold(dy)
+            after(r,d_ref[r,:]+norm_back(dy,row(Rows.gain+i),xhat,rstd))
+        chunks(steps,body)
+    def out_units(act,lo,q):
+        @phase(lo,lo+F)
+        def _():
+            d=j-lo; a=d//across
+            for slot in range(3):
+                @pl.when((lax.rem(a,3)==slot)&(lax.rem(d,across)==0))
+                def _(slot=slot):
+                    for cp in lefts(act,a,slot): cp.wait()
+            unit(q+d,tn(big_ref[lax.rem(a,3)],low_ref[:,here(lax.rem(d,across))]).astype(BF))
+            @pl.when(d==across-1)
+            def _():
+                for a in range(3,F//across):
+                    for cp in lefts(act,a,a-3): cp.start()
+    def start_feed(act,fo,slopes):
+        for a in range(3):
+            for cp in lefts(act,a,a): cp.start()
+        band(fo,0).start(); slope(slopes,0).start()
+
+    @last(0)
+    def _():
+        comm.begin()
+        load(dx4,d_ref,sem_d).start(); load(hid4,hid_ref,sem_hid).start(); load(x3,x_ref,sem_x).start()
+        ahead(fi1,0); start_feed(act1,fo1,dsl1)
         sums_ref[...]=jnp.zeros_like(sums_ref)
+        dtab_ref[...]=jnp.zeros_like(dtab_ref)
+        acc_ref[...]=jnp.zeros_like(acc_ref)
+        tail_ref[steps:steps+PAD,:]=jnp.zeros((PAD,width),F32)
+        pad_ref[0:PAD,:]=jnp.zeros((PAD,width),F32)
+        load(dx4,d_ref,sem_d).wait()
         def body(r):
             df=(0.5*d_ref[r,:]).astype(BF)
-            df_ref[r,:]=df
-            sums_ref[2]+=fold(df.astype(F32))
+            low_ref[r,:width]=df
+            sums_ref[12]+=fold(df.astype(F32))
         chunks(steps,body)
+        load(hid4,hid_ref,sem_hid).wait()
         turn_ref[...]=hid_ref[...].T
+        load(chid,hid_ref,sem_hid).start()
+    stream(fi1,FB,F,tau[0],lambda i,w: feed_step(i,fo1,dsl1,units[0],0,w))
+    @last(FD-1)
+    def _():
+        load(x3,x_ref,sem_x).wait()
+        def after(r,v): d_ref[r,:]=v
+        norm_step(x_ref,4,8,after)
+        load(depth,x_ref,sem_x).start()
+        ahead(po,tau[1])
+    out_units(act1,FD,units[1])
+    @last(MP-1)
+    def _():
+        whole_big(up.at[:,:width],0).start(); whole_big(up.at[:,width:],1).start(); whole_big(cact,2).start()
+        def body(r): low_ref[r,:width]=d_ref[r,:].astype(BF)
+        chunks(steps,body)
         acc_ref[...]=jnp.zeros_like(acc_ref)
-    dpre=(nt(df_ref[...],fo_ref[...])*dsl_ref[...].astype(F32)).astype(BF)
-    dbin_ref[...]=fold(dpre.astype(F32))
-    acc_ref[...]+=nt(dpre,fi_ref[...])
-    dfi_ref[0]=nn(turn_ref[...],dpre).astype(BF)
-    into_units(dfo_ref,tn(act_ref[...],df_ref[...]).astype(BF))
-    @pl.when(j==pl.num_programs(0)-1)
-    def _():
-        def body(r):
-            xhat,rstd=stats(x_ref[r,:].astype(F32))
-            dy=acc_ref[r,:]
-            sums_ref[0]+=fold(dy*xhat); sums_ref[1]+=fold(dy)
-            out_ref[r,:]=(d_ref[r,:]+norm_back(dy,gain_ref[norm:norm+1,:],xhat,rstd)).astype(out_ref.dtype)
-        chunks(steps,body)
-
-def feed_back(d,x,gains,hid,act,dsl,fi,fo,norm,out_type,side=None,cid=None):
-    steps,width=x.shape; hidden=fi.shape[1]; tn_=SUB[1]; tiles=hidden//tn_; S=width//SUB[0]
-    assert hidden//S==tn_
-    units=tn_*width//(SUB[0]*SUB[1])
-    ins=[d,x,gains,hid,act,dsl,fi,fo]
-    return call(aside(functools.partial(feed_back_kernel,norm)),'feed_forward_back',(tiles,),ins,
-        [whole(d.shape),whole(x.shape),whole(gains.shape),whole(hid.shape),pl.BlockSpec((steps,tn_),lambda j:(0,j)),pl.BlockSpec((steps,tn_),lambda j:(0,j)),pl.BlockSpec((width,tn_),lambda j:(0,j)),pl.BlockSpec((tn_,width),lambda j:(j,0))],
-        [jax.ShapeDtypeStruct((steps,width),out_type),jax.ShapeDtypeStruct((tiles,width,tn_),BF),jax.ShapeDtypeStruct((units,S)+SUB,BF),jax.ShapeDtypeStruct((8,hidden),F32),jax.ShapeDtypeStruct((3,8,width),F32)],
-        [whole((steps,width)),pl.BlockSpec((1,width,tn_),lambda j:(j,0,0)),pl.BlockSpec((units,1)+SUB,lambda j:(0,j,0,0)),pl.BlockSpec((8,tn_),lambda j:(0,j)),whole((3,8,width))],
-        [pltpu.VMEM((steps,width),BF),pltpu.VMEM((steps,width),F32),pltpu.VMEM((width,steps),BF)],side,cid)
-
-def in_units(ref,v):
-    for j in range(ref.shape[0]): ref[j]=v[:,j*ref.shape[2]:(j+1)*ref.shape[2]]
-
-def middle_back_kernel(taps,comm,d_ref,depth_ref,up_ref,chid_ref,cact_ref,mixed_ref,x2_ref,vec_ref,valid_ref,ao_ref,pi_ref,po_ref,
-        dx2_ref,dpv_ref,dpo_ref,dpi_ref,dao_ref,ddw_ref,sums_ref,low_ref,wide_ref,pad_ref,tail_ref):
-    steps,width=d_ref.shape
-    gain_ref=vec_ref.at[Rows.gain:Rows.gain+8]; shift_ref=vec_ref.at[Rows.shift:Rows.shift+8]; dw_ref=vec_ref.at[Rows.taps:Rows.taps+32]
-    point=points(comm,8)
-    point()
-    sums_ref[...]=jnp.zeros_like(sums_ref)
-    def cast(r): low_ref[r,:width]=d_ref[r,:].astype(BF)
-    chunks(steps,cast)
-    wide_ref[:,:width]=nt(low_ref[:,:width],po_ref[...])
-    point()
-    in_units(dpo_ref,tn(cact_ref[...],low_ref[:,:width]).astype(BF))
-    point()
-    tail_ref[steps:steps+PAD,:]=jnp.zeros((PAD,width),F32)
-    pad_ref[0:PAD,:]=jnp.zeros((PAD,width),F32)
-    def three(i,c):
-        r=pl.ds(pl.multiple_of(i*CH,CH),CH)
-        xhat,rstd=stats(depth_ref[r,:])
-        gain=gain_ref[3:4,:]
-        z=xhat*gain+shift_ref[3:4,:]
-        sg=sigmoid(z)
-        dz=wide_ref[r,:width]*(sg*(1.0+z*(1.0-sg)))
-        sums_ref[0]+=fold(dz*xhat); sums_ref[1]+=fold(dz)
-        tail_ref[r,:]=norm_back(dz,gain,xhat,rstd)
-        pad_ref[pl.ds(pl.multiple_of(i*CH+PAD,PAD),CH),:]=up_ref[r,:width].astype(F32)*sigmoid(up_ref[r,width:].astype(F32))*valid_ref[r,0:1]
-        return c
-    lax.fori_loop(0,steps//CH,three,0)
-    point()
-    def conv(cols):
-        for t0 in range(0,steps,RC):
-            wide_ref[t0:t0+RC,cols]=slide(tail_ref,dw_ref,lambda k:taps-1-k,taps,t0,cols)
-        lead=lambda k:k+PAD-taps+1
-        for b in range(8):
-            use=taps_of(taps,lead,b)
-            if not use: continue
-            top=max(a for a,_ in use)
-            parts={k:jnp.zeros((8,128),F32) for _,k in use}
+    def lower(i,w):
+        @pl.when(i==0)
+        def _(): whole_big(cact,2).wait()
+        acc_ref[...]+=nt(low_ref[:,here(i)],w[...])
+        unit(units[2]+i,tn(big_ref[2],low_ref[:,here(i)]).astype(BF))
+        @pl.when(i==M0-1)
+        def _(): ahead(pi,tau[2])
+    stream(po,MP,M0,tau[1],lower)
+    @last(MC)
+    def _():
+        weights=vec_ref.at[Rows.taps:Rows.taps+32]
+        load(depth,x_ref,sem_x).wait(); whole_big(cact,0).wait(); whole_big(cact,1).wait()
+        def three(i,c):
+            r=pl.ds(pl.multiple_of(i*CH,CH),CH)
+            xhat,rstd=stats(x_ref[r,:])
+            gain=row(Rows.gain+3)
+            z=xhat*gain+row(Rows.shift+3)
+            sg=sigmoid(z)
+            dz=acc_ref[r,:]*(sg*(1.0+z*(1.0-sg)))
+            sums_ref[6]+=fold(dz*xhat); sums_ref[7]+=fold(dz)
+            tail_ref[r,:]=norm_back(dz,gain,xhat,rstd)
+            pad_ref[pl.ds(pl.multiple_of(i*CH+PAD,PAD),CH),:]=big_ref[0,r,:].astype(F32)*sigmoid(big_ref[1,r,:].astype(F32))*valid_ref[r,0:1]
+            return c
+        lax.fori_loop(0,steps//CH,three,0)
+        load(x2,x_ref,sem_x).start()
+        ticks(MC,(0,3))
+        def conv(cols):
             for t0 in range(0,steps,RC):
-                slab=pad_ref[t0+b:t0+b+RC+8*top,cols]
-                dd=tail_ref[t0:t0+RC,cols]
-                for a,k in use: parts[k]=parts[k]+fold(slab[8*a:8*a+RC]*dd)
-            for k,v in parts.items(): ddw_ref[k:k+1,cols]=jnp.sum(v,axis=0,keepdims=True)
-    over_columns(width,conv)
-    point()
-    def gate(r):
-        a=up_ref[r,:width].astype(F32); sg=sigmoid(up_ref[r,width:].astype(F32))
-        dg=wide_ref[r,:width]*valid_ref[r,0:1]*sg
-        low_ref[r,:width]=dg.astype(BF)
-        low_ref[r,width:]=(dg*a*(1.0-sg)).astype(BF)
-    chunks(steps,gate)
-    in_units(dpi_ref,tn(chid_ref[...],low_ref[...]).astype(BF))
-    point()
-    wide_ref[:,:width]=nt(low_ref[...],pi_ref[...])
-    point()
-    def two(r):
-        xhat,rstd=stats(x2_ref[r,:])
-        dy=wide_ref[r,:width]
-        sums_ref[2]+=fold(dy*xhat); sums_ref[3]+=fold(dy)
-        dx=d_ref[r,:]+norm_back(dy,gain_ref[2:3,:],xhat,rstd)
-        dx2_ref[r,:]=dx
-        da=dx.astype(BF)
-        low_ref[r,:width]=da
-        sums_ref[4]+=fold(da.astype(F32))
-    chunks(steps,two)
-    point()
-    dpv_ref[...]=nt(low_ref[:,:width],ao_ref[...]).astype(BF)
-    in_units(dao_ref,tn(mixed_ref[...],low_ref[:,:width]).astype(BF))
-    point()
-
-def middle_back(d,depth,up,chid,cact,mixed,x2,vec,valid,ao,pi,po,taps,side=None,cid=None):
-    steps,width=d.shape
-    ins=[d,depth,up,chid,cact,mixed,x2,vec,valid,ao,pi,po]
-    S=jax.ShapeDtypeStruct
-    unit=lambda w: S((w.shape[1]//SUB[1],w.shape[0],SUB[1]),BF)
-    outs=[S((steps,width),F32),S((steps,width),BF),unit(po),unit(pi),unit(ao),S((32,width),F32),S((5,8,width),F32)]
-    return call(functools.partial(middle_back_kernel,taps),'convolution_module_back',(1,),ins,[whole(a.shape) for a in ins],outs,[whole(o.shape) for o in outs],
-        [pltpu.VMEM((steps,2*width),BF),pltpu.VMEM((steps,width),F32),pltpu.VMEM((steps+PAD,width),F32),pltpu.VMEM((steps+PAD,width),F32)],side,cid)
-
-
-def late_kernel(taps,size,vector_rows,comm,q_ref,k_ref,v_ref,p_ref,g_ref,table_ref,pick_ref,hid1_ref,ai_ref,dx2_ref,x1_ref,gain_ref,
-        hid0_ref,act_ref,dsl_ref,fi_ref,fo_ref,x_ref,s5_ref,s4_ref,s23_ref,ddw_ref,dbin1_ref,out_ref,
-        ds_ref,dpk_ref,dtab_ref,psum_ref,acc_ref,turn_ref,dx1_ref,df_ref,stage_ref,dbin_ref,sums_ref,vec_ref,stage_sem,left_sem):
-    steps,width=x1_ref.shape; wide=SUB[1]; S=comm.S
-    A=width//128; B=3*width//wide; C=act_ref.shape[1]//wide; D=C
-    j=pl.program_id(0)
-    made_ai,made_fi,made_small,made_fo=comm.makes
-    @pl.when(j==0)
-    def _():
-        comm.begin()
-        dtab_ref[...]=jnp.zeros_like(dtab_ref)
-    def put(q,ref):
-        return pltpu.make_async_copy(stage_ref.at[lax.rem(q,2)],ref,stage_sem.at[lax.rem(q,2)])
-    def unit(q,value,ref):
-        @pl.when(q>=2)
-        def _(): put(q,ref).wait()
-        stage_ref[lax.rem(q,2)]=value.reshape(stage_ref.shape[1:])
-        put(q,ref).start()
-    def lefts(a,slot):
-        rows=act_ref.shape[1]//S
-        return [pltpu.make_async_copy(act_ref.at[:,pl.ds(al(s*rows+a*SUB[0],SUB[0]),SUB[0])],dpk_ref.at[slot,:,pl.ds(s*SUB[0],SUB[0])],left_sem.at[slot,s]) for s in range(S)]
-    @pl.when(j<A)
-    def _():
-        flip=(lax.broadcasted_iota(jnp.int32,(QB,QB),0)+lax.broadcasted_iota(jnp.int32,(QB,QB),1)==QB-1).astype(F32).astype(BF)
-        here=pl.ds(al(j*128,128),128)
-        parts=[]
-        for hh in range(128//size):
-            cols=slice(hh*size,(hh+1)*size)
-            parts.append(one_head_back(q_ref,k_ref,v_ref,p_ref.at[hh],g_ref,table_ref,pick_ref,dtab_ref,ds_ref,flip,cols))
-            comm.run(j*2+hh,1)
-        for part in range(3):
-            dpk_ref[part,:,here]=jnp.concatenate([a[part] for a in parts],axis=1)
-        psum_ref[0:1,here]=jnp.sum(dpk_ref[0,:,here].astype(F32),axis=0,keepdims=True)
-        psum_ref[1:2,here]=jnp.sum(dpk_ref[2,:,here].astype(F32),axis=0,keepdims=True)
-    @pl.when((j>=A)&(j<A+B))
-    def _():
-        b=j-A; per=width//wide
+                acc_ref[t0:t0+RC,cols]=slide(tail_ref,weights,lambda k:taps-1-k,taps,t0,cols)
+        over_columns(width,conv)
+        ticks(MC,(1,3))
+        def gate(r):
+            a=big_ref[0,r,:].astype(F32); sg=sigmoid(big_ref[1,r,:].astype(F32))
+            dg=acc_ref[r,:]*valid_ref[r,0:1]*sg
+            low_ref[r,:width]=dg.astype(BF)
+            low_ref[r,width:]=(dg*a*(1.0-sg)).astype(BF)
+        chunks(steps,gate)
+        acc_ref[...]=jnp.zeros_like(acc_ref)
+        ticks(MC,(2,3))
+    def raised(i,w):
+        @pl.when(i==0)
+        def _(): load(chid,hid_ref,sem_hid).wait()
+        acc_ref[...]+=nt(low_ref[:,here(i)],w[...])
+        unit(units[3]+i,tn(hid_ref[...],low_ref[:,here(i)]).astype(BF))
+        @pl.when(i==M1-1)
+        def _():
+            load(mixed,hid_ref,sem_hid).start()
+            ahead(ao,tau[3])
+            load(x2,x_ref,sem_x).wait()
+            def after(r,v):
+                d_ref[r,:]=v
+                da=v.astype(BF)
+                low_ref[r,:width]=da
+                sums_ref[13]+=fold(da.astype(F32))
+            norm_step(x_ref,2,4,after)
+            load(x1,x_ref,sem_x).start()
+            acc_ref[...]=jnp.zeros_like(acc_ref)
+    stream(pi,MI,M1,tau[2],raised)
+    def joined(i,w):
+        @pl.when(i==0)
+        def _(): load(mixed,hid_ref,sem_hid).wait()
+        acc_ref[...]+=nt(low_ref[:,here(i)],w[...])
+        unit(units[4]+i,tn(hid_ref[...],low_ref[:,here(i)]).astype(BF))
+        @pl.when(i==M2-1)
+        def _():
+            load(hid1,hid_ref,sem_hid).start()
+            ahead(ai,tau[4])
+            low_ref[:,width:]=acc_ref[...].astype(BF)
+            acc_ref[...]=jnp.zeros_like(acc_ref)
+    stream(ao,MO,M2,tau[3],joined)
+    ticks_of(FB,MC); ticks_of(MI,AT)
+    @last(AT)
+    def _():
+        for q in (first_late-2,first_late-1): put(q).wait()
+    lo_at=at[AT][0]
+    @phase(AT,PB)
+    def _():
+        h=j-AT
+        mine=pl.ds(al(h*128,128),128)
+        grad_ref[...]=low_ref[:,pl.ds(al(width+h*128,128),128)]
+        parts=heads_back(q_ref,k_ref,v_ref,p_ref,grad_ref,table_ref,pick_ref,dtab_ref,ds_ref,size)
+        for part in range(3): big_ref[part,:,mine]=parts[part]
+        psum_ref[0:1,mine]=jnp.sum(big_ref[0,:,mine].astype(F32),axis=0,keepdims=True)
+        psum_ref[1:2,mine]=jnp.sum(big_ref[2,:,mine].astype(F32),axis=0,keepdims=True)
+        comm.run(lo_at+h*ATICKS,ATICKS)
+    start=lo_at+ATICKS*A
+    assert start<=comm.gate+comm.wait
+    late=plan_ticks(comm,times[PB:],PACE2,lambda st: limit(PB+st)-start)
+    for st in range(PB,EN): at[st]=(start+late[st-PB][0],late[st-PB][1])
+    def packed_back(b,w):
         @pl.when(b==0)
         def _():
-            turn_ref[...]=hid1_ref[...].T
-            acc_ref[...]=jnp.zeros_like(acc_ref)
-            sums_ref[...]=jnp.zeros_like(sums_ref)
-        g=dpk_ref[b//per,:,pl.ds(al(lax.rem(b,per)*wide,wide),wide)]
-        acc_ref[...]+=nt(g,ai_ref[...])
-        unit(b,nn(turn_ref[...],g).astype(BF),made_ai.at[b])
+            load(hid1,hid_ref,sem_hid).wait()
+            turn_ref[...]=hid_ref[...].T
+            load(hid0,hid_ref,sem_hid).start()
+        g=big_ref[b//across,:,here(lax.rem(b,across))]
+        acc_ref[...]+=nt(g,w[...])
+        unit(units[5]+b,nn(turn_ref[...],g).astype(BF))
         @pl.when(b==B-1)
         def _():
-            for a in range(3):
-                for cp in lefts(a,a): cp.start()
-            turn_ref[...]=hid0_ref[...].T
-            def body(r):
-                xhat,rstd=stats(x1_ref[r,:])
-                dy=acc_ref[r,:]
-                sums_ref[0]+=fold(dy*xhat); sums_ref[1]+=fold(dy)
-                dx=dx2_ref[r,:]+norm_back(dy,gain_ref[1:2,:],xhat,rstd)
-                dx1_ref[r,:]=dx
-                df=(0.5*dx).astype(BF)
-                df_ref[r,:]=df
-                sums_ref[4]+=fold(df.astype(F32))
-            chunks(steps,body)
+            ahead(fi0,tau[5]); start_feed(act0,fo0,dsl0)
+            load(x1,x_ref,sem_x).wait(); load(hid0,hid_ref,sem_hid).wait()
+            turn_ref[...]=hid_ref[...].T
+            def after(r,v):
+                d_ref[r,:]=v
+                df=(0.5*v).astype(BF)
+                low_ref[r,:width]=df
+                sums_ref[11]+=fold(df.astype(F32))
+            norm_step(x_ref,1,2,after)
             acc_ref[...]=jnp.zeros_like(acc_ref)
-        comm.run(2*A+b,1)
-    @pl.when((j>=A+B)&(j<A+B+C))
-    def _():
-        c=j-A-B
-        dpre=(nt(df_ref[...],fo_ref[...])*dsl_ref[...].astype(F32)).astype(BF)
-        dbin_ref[:,pl.ds(al(c*wide,wide),wide)]=fold(dpre.astype(F32))
-        acc_ref[...]+=nt(dpre,fi_ref[...])
-        unit(B+c,nn(turn_ref[...],dpre).astype(BF),made_fi.at[c])
-        @pl.when(c==C-1)
-        def _():
-            def body(r):
-                xhat,rstd=stats(x_ref[r,:].astype(F32))
-                dy=acc_ref[r,:]
-                sums_ref[2]+=fold(dy*xhat); sums_ref[3]+=fold(dy)
-                out_ref[r,:]=(dx1_ref[r,:]+norm_back(dy,gain_ref[0:1,:],xhat,rstd)).astype(BF)
-            chunks(steps,body)
-            vec_ref[...]=jnp.zeros_like(vec_ref)
-            total=lambda v: jnp.sum(v,axis=0,keepdims=True)
-            rows=[sums_ref[2],sums_ref[0],s23_ref[2],s23_ref[0],s4_ref[0],s5_ref[0],sums_ref[3],sums_ref[1],s23_ref[3],s23_ref[1],s4_ref[1],s5_ref[1],sums_ref[4],s4_ref[2]]
-            rows=[total(v) for v in rows]+[psum_ref[0:1,:],psum_ref[1:2,:],total(s23_ref[4])]
-            L=width//S
-            for i,v in enumerate(rows):
-                for s in range(S): vec_ref[s,i:i+1,0:L]=v[:,s*L:s*L+L]
-            k=len(rows)
-            for i,ref in enumerate((dbin_ref,dbin1_ref)):
-                v=total(ref[...])
-                for s in range(S): vec_ref[s,k+i:k+i+1,:]=v[:,s*wide:s*wide+wide]
-            for s in range(S):
-                vec_ref[s,32:32+taps,0:L]=ddw_ref[0:taps,s*L:s*L+L]
-                n=dtab_ref.shape[0]//S
-                vec_ref[s,vector_rows:vector_rows+n,0:size]=dtab_ref[s*n:s*n+n,:]
-        comm.run(2*A+B+c,1)
-    @pl.when((j>=A+B+C)&(j<A+B+C+D))
-    def _():
-        d=j-A-B-C; across=width//wide
-        @pl.when(d==0)
-        def _(): unit(B+C,vec_ref[...].astype(BF).reshape(S*SUB[0],wide),made_small.at[0])
-        a=d//across
-        for slot in range(3):
-            @pl.when((lax.rem(a,3)==slot)&(lax.rem(d,across)==0))
-            def _(slot=slot):
-                for cp in lefts(a,slot): cp.wait()
-        unit(B+C+1+d,tn(dpk_ref[lax.rem(a,3)],df_ref[:,pl.ds(al(lax.rem(d,across)*wide,wide),wide)]).astype(BF),made_fo.at[d])
-        @pl.when(d==across-1)
-        def _():
-            for a in range(3,D//across):
-                for cp in lefts(a,a-3): cp.start()
-        comm.run(2*A+B+C+d,1)
-    @pl.when(j==A+B+C+D)
-    def _():
-        for q in (0,1): put(B+C+D+1+q,made_fo.at[0]).wait()
-        lo=2*A+B+C+D
+    stream(ai,PB,B,tau[4],packed_back)
+    stream(fi0,CB,F,tau[5],lambda i,w: feed_step(i,fo0,dsl0,units[6],1,w))
+    @phase(CB,CD)
+    def _():
+        def conv_weights(cols):
+            lead=lambda k:k+PAD-taps+1
+            for b in range(8):
+                use=taps_of(taps,lead,b)
+                if not use: continue
+                top=max(a for a,_ in use)
+                parts={k:jnp.zeros((8,128),F32) for _,k in use}
+                for t0 in range(0,steps,RC):
+                    slab=pad_ref[t0+b:t0+b+RC+8*top,cols]
+                    dd=tail_ref[t0:t0+RC,cols]
+                    for a,k in use: parts[k]=parts[k]+fold(slab[8*a:8*a+RC]*dd)
+                for k,v in parts.items(): ddw_ref[k:k+1,cols]=jnp.sum(v,axis=0,keepdims=True)
+        for a in range(A//F): conv_weights(pl.ds(al((j-CB)*(A//F)*128+a*128,128),128))
+    @last(CD-1)
+    def _():
+        def after(r,v): out_ref[r,:]=v.astype(BF)
+        norm_step(tok_ref,0,0,after)
+        rows_ref[...]=jnp.zeros_like(rows_ref)
+        total=lambda v: jnp.sum(v,axis=0,keepdims=True)
+        rows=[sums_ref[0],sums_ref[2],sums_ref[4],sums_ref[6],sums_ref[8],s5_ref[0],sums_ref[1],sums_ref[3],sums_ref[5],sums_ref[7],sums_ref[9],s5_ref[1],sums_ref[11],sums_ref[12]]
+        rows=[total(v) for v in rows]+[psum_ref[0:1,:],psum_ref[1:2,:],total(sums_ref[13])]
+        L=width//S
+        for i,v in enumerate(rows):
+            for s in range(S): rows_ref[s,i:i+1,0:L]=v[:,s*L:s*L+L]
+        k=len(rows)
+        for i in range(2):
+            v=total(dbin_ref[1-i])
+            for s in range(S): rows_ref[s,k+i:k+i+1,:]=v[:,s*wide:s*wide+wide]
+        n=dtab_ref.shape[0]//S
+        for s in range(S):
+            rows_ref[s,32:32+taps,0:L]=ddw_ref[0:taps,s*L:s*L+L]
+            rows_ref[s,VECTOR_ROWS:VECTOR_ROWS+n,0:size]=dtab_ref[s*n:s*n+n,:]
+    @last(CD)
+    def _(): unit(units[7],rows_ref[...].astype(BF).reshape(S*SUB[0],wide))
+    out_units(act0,CD,units[8])
+    ticks_of(PB,EN)
+    @last(EN)
+    def _():
+        for q in (units[9]-2,units[9]-1): put(q).wait()
+        lo=sum(at[EN-1])
         comm.run(lo,comm.ticks-lo)
 
-def one_head_back(q_ref,k_ref,v_ref,p_ref,g_ref,table_ref,pick_ref,dtab_ref,ds_ref,flip,cols):
-    steps=q_ref.shape[0]; nb=steps//QB; span=steps+QB; size=cols.stop-cols.start
+def heads_back(q_ref,k_ref,v_ref,p_ref,g_ref,table_ref,pick_ref,dtab_ref,ds_ref,size):
+    steps=q_ref.shape[0]; nb=steps//QB; span=steps+QB
     scale=1.0/math.sqrt(size)
-    k=k_ref[:,cols]; v=v_ref[:,cols]; dqs=[]
-    for i in range(nb):
-        rows=slice(i*QB,(i+1)*QB)
-        q=q_ref[rows,cols]
-        p=p_ref[rows,:].astype(F32)
-        t=p*nt(g_ref[rows,cols],v)
-        ds=(t-p*jnp.sum(t,axis=1,keepdims=True)).astype(BF)
-        ds_ref[rows,:]=ds
-        wide=jnp.concatenate([nn(flip,ds),jnp.zeros((QB,span-steps),F32)],axis=1)
-        back=pltpu.roll(wide,span-QB+1,1,stride=1,stride_axis=0).astype(BF)
-        drel=nn(flip,(nt(back,pick_ref[i])*scale).astype(BF)).astype(BF)
-        dqs.append((nn(ds,k)*scale+nn(drel,table_ref[...])).astype(BF))
-        dtab_ref[...]+=tn(drel,q)
-    return jnp.concatenate(dqs,axis=0),(tn(ds_ref[...],q_ref[:,cols])*scale).astype(BF),tn(p_ref[...],g_ref[:,cols]).astype(BF)
-
-VECTOR_ROWS=64
-def late(S,packed,p,grad,table,pick,heads,hid1,ai,dx2,x1,gains,hid0,act,dsl,fi,fo,tokens,s5,s4,s23,ddw,dbin1,taps,ready,places,out_shapes,cid):
-    steps,width=x1.shape; size=width//heads; wide=SUB[1]
-    A=width//128; B=3*width//wide; C=act.shape[1]//wide; D=C; per=128//size
-    assert act.shape[1]//S==wide and width//S==SUB[0] and wide//SUB[0]<=4
-    comm=Scatter(S,ready+[B,C,1,D],places,out_shapes,common=(sum(a.shape[0] for a in ready)+B+C,VECTOR_ROWS,table.shape[0]//S))
-    head=lambda o:pl.BlockSpec((steps,128),lambda j:(0,o*A+jnp.minimum(j,A-1)))
-    tile=lambda lo,n:(lambda j:jnp.minimum(jnp.maximum(j-lo,0),n-1))
-    tb,tc=tile(A,B),tile(A+B,C)
-    ins=[packed,packed,packed,p,grad,table,pick,hid1,ai,dx2,x1,gains,hid0,act,dsl,fi,fo,tokens,s5,s4,s23,ddw,dbin1]
-    specs=[head(0),head(1),head(2),pl.BlockSpec((per,steps,steps),lambda j:(jnp.minimum(j,A-1),0,0)),head(0),whole(table.shape),whole(pick.shape),
-        whole(hid1.shape),pl.BlockSpec((width,wide),lambda j:(0,tb(j))),whole(dx2.shape),whole(x1.shape),whole(gains.shape),whole(hid0.shape),pl.BlockSpec(memory_space=pl.ANY),
-        pl.BlockSpec((steps,wide),lambda j:(0,tc(j))),pl.BlockSpec((width,wide),lambda j:(0,tc(j))),pl.BlockSpec((wide,width),lambda j:(tc(j),0)),whole(tokens.shape)]
-    specs+=[whole(a.shape) for a in (s5,s4,s23,ddw,dbin1)]
-    V=pltpu.VMEM; Z=S//2
-    scratch=[V((steps,steps),BF),V((3,steps,width),BF),V((128,size),F32),V((8,width),F32),V((steps,width),F32),V((width,steps),BF),V((steps,width),F32),V((steps,width),BF),
-        V((2,Z,2,2,SUB[0]//2,wide),BF),V((8,act.shape[1]),F32),V((5,8,width),F32),V((S,)+SUB,F32),pltpu.SemaphoreType.DMA((2,)),pltpu.SemaphoreType.DMA((3,S))]
-    return call(functools.partial(late_kernel,taps,size,VECTOR_ROWS),'attend_back_and_sums',(A+B+C+D+1,),ins,specs,[jax.ShapeDtypeStruct((steps,width),BF)],[whole((steps,width))],scratch,comm,cid)
+    flip=(lax.broadcasted_iota(jnp.int32,(QB,QB),0)+lax.broadcasted_iota(jnp.int32,(QB,QB),1)==QB-1).astype(F32).astype(BF)
+    sl=[slice(i*QB,(i+1)*QB) for i in range(nb)]
+    out=[]
+    for hh in range(q_ref.shape[1]//size):
+        cols=slice(hh*size,(hh+1)*size)
+        dss=[]
+        for r in sl:
+            p=p_ref[hh,r,:].astype(F32)
+            t=p*nt(g_ref[r,cols],v_ref[:,cols])
+            dss.append((t-p*jnp.sum(t,axis=1,keepdims=True)).astype(BF))
+        for r,ds in zip(sl,dss): ds_ref[r,:]=ds
+        xs=[nn(flip,ds) for ds in dss]
+        xs=[pltpu.roll(jnp.concatenate([x,jnp.zeros((QB,QB),F32)],axis=1),span-QB+1,1,stride=1,stride_axis=0).astype(BF) for x in xs]
+        xs=[(nt(x,pick_ref[i])*scale).astype(BF) for i,x in enumerate(xs)]
+        drel=jnp.concatenate([nn(flip,x).astype(BF) for x in xs],axis=0)
+        dq=(nn(ds_ref[...],k_ref[:,cols])*scale+nn(drel,table_ref[...])).astype(BF)
+        dtab_ref[...]+=tn(drel,q_ref[:,cols])
+        out.append((dq,(tn(ds_ref[...],q_ref[:,cols])*scale).astype(BF),tn(p_ref[hh],g_ref[:,cols]).astype(BF)))
+    return [jnp.concatenate([a[part] for a in out],axis=1) for part in range(3)]
+
+PACE=4.3; PAUSE=1; PACE2=2.0; ATICKS=1
+def backward(S,packed,p,table,pick,heads,vec,valid,tokens,s5,rest,taps,out_shapes,cid):
+    steps,width=tokens.shape; size=width//heads; wide=SUB[1]; across=width//wide
+    act1,ai,ao,pi,po=rest[12],rest[18],rest[19],rest[20],rest[21]
+    hidden=act1.shape[1]; F=hidden//wide; A=width//128; B=ai.shape[1]//wide; M0,M1,M2=[a.shape[1]//wide for a in (po,pi,ao)]
+    assert hidden//S==wide and width//S==SUB[0] and wide//SUB[0]<=4 and A%F==0
+    counts=[F,F,M0,M1,M2,B,F,1,F]
+    places=[(0,1,F),(1,1,across),(5,None,across),(4,None,2*across),(3,None,across),(2,None,3*across),(0,0,F),(6,None,1),(1,0,across)]
+    comm=Scatter(S,counts,places,out_shapes,common=(sum(counts[:7]),VECTOR_ROWS,table.shape[0]//S),pause=(sum(counts[:5]),PAUSE))
+    start=2*F+M0+1+M1+M2
+    head=lambda o:pl.BlockSpec((steps,128),lambda j:(0,o*A+jnp.minimum(jnp.maximum(j-start,0),A-1)))
+    ins=[packed,packed,packed,p,table,pick,vec,valid,tokens,s5]
+    specs=[head(0),head(1),head(2),pl.BlockSpec((128//size,steps,steps),lambda j:(jnp.minimum(jnp.maximum(j-start,0),A-1),0,0))]+[whole(a.shape) for a in ins[4:]]
+    specs+=[pl.BlockSpec(memory_space=pl.ANY)]*len(rest)
+    V=pltpu.VMEM; Z=S//2; sem=lambda *n: pltpu.SemaphoreType.DMA(n)
+    sq=lambda t: V((steps,width),t)
+    scratch=[sq(F32),sq(F32),sq(F32),V((steps,2*width),BF),V((width,steps),BF),sq(BF),V((3,steps,width),BF),V((2,Z,2,2,SUB[0]//2,wide),BF),V((steps,steps),BF),V((steps,128),BF),
+        V((2,width,wide),BF),V((2,wide,width),BF),V((2,steps,wide),BF),V((steps+PAD,width),F32),V((steps+PAD,width),F32),V((S,)+SUB,F32),V((14,8,width),F32),V((32,width),F32),V((2,8,hidden),F32),V((8,width),F32),V((128,size),F32),
+        sem(1),sem(1),sem(1),sem(3,S),sem(2),sem(2),sem(2),sem(2)]
+    return call(functools.partial(backward_kernel,taps,size),'backward_and_sums',(start+A+B+2*F+1,),ins+list(rest),specs,[jax.ShapeDtypeStruct((steps,width),BF)],[whole((steps,width))],scratch,comm,cid)
 
 class Rows:
     gain=0; shift=8; inner=16; outer=24; packed=26; mixed=28; taps=32; count=64
@@ -650,7 +692,7 @@
     def wa(slot): return wa_ref[slot].reshape(width,tile)
     want=[comm.done(2),comm.done(3),comm.done(4),comm.done(5),comm.done(6),comm.done(8)]
     at={}; done=want[0]
-    times=[20/F]*F+[10/B]*B+[35/A]*A+[3]*M0+[2]*(M1-1)+[14]+[3]*M2
+    times=[20/F]*F+[10/B]*B+[26/A]*A+[3]*M0+[2]*(M1-1)+[14]+[3]*M2
     need={cut[1]-1:want[1],cut[3]-1:want[2],cut[4]-1:want[3],cut[5]-1:want[4],cut[6]-1:comm.ticks-1}
     for st in range(cut[6]):
         target=want[0]+int((comm.ticks-1-want[0])*sum(times[:st+1])/sum(times))
@@ -730,18 +772,17 @@
         h=j-cut[2]
         for a in range(3): qkv_ref[a]=packed_ref[:,pl.ds(al(a*width+h*128,128),128)]
         scale=1.0/math.sqrt(size)
-        for i in range(steps//QB):
-            rows=slice(i*QB,(i+1)*QB); outs=[]
-            for hh in range(128//size):
-                cols=slice(hh*size,(hh+1)*size)
-                q=qkv_ref[0,rows,cols]
-                rel=pltpu.roll(nn(q,rel_ref[i]),0,1,stride=1,stride_axis=0)[:,:steps]
-                s=(nt(q,qkv_ref[1,:,cols])+rel)*scale+mask_ref[0:1,:]
-                e=jnp.exp(s-jnp.max(s,axis=1,keepdims=True))
-                p=(e*(1.0/jnp.sum(e,axis=1,keepdims=True))).astype(BF)
-                p_ref[hh,rows,:]=p
-                outs.append(nn(p,qkv_ref[2,:,cols]).astype(BF))
-            mixed_ref[rows,pl.ds(al(h*128,128),128)]=jnp.concatenate(outs,axis=1)
+        sl=[slice(i*QB,(i+1)*QB) for i in range(steps//QB)]; outs=[]
+        for hh in range(128//size):
+            cols=slice(hh*size,(hh+1)*size)
+            rels=[nn(qkv_ref[0,r,cols],rel_ref[i]) for i,r in enumerate(sl)]
+            rels=[pltpu.roll(x,0,1,stride=1,stride_axis=0)[:,:steps] for x in rels]
+            ss=[(nt(qkv_ref[0,r,cols],qkv_ref[1,:,cols])+x)*scale+mask_ref[0:1,:] for r,x in zip(sl,rels)]
+            es=[jnp.exp(s-jnp.max(s,axis=1,keepdims=True)) for s in ss]
+            ps=[(e*(1.0/jnp.sum(e,axis=1,keepdims=True))).astype(BF) for e in es]
+            for r,p in zip(sl,ps): p_ref[hh,r,:]=p
+            outs.append(jnp.concatenate([nn(p,qkv_ref[2,:,cols]).astype(BF) for p in ps],axis=0))
+        mixed_ref[:,pl.ds(al(h*128,128),128)]=jnp.concatenate(outs,axis=1)
     def join(i,slot):
         x2_ref[:,here(i)]=x1_ref[:,here(i)]+nn(mixed_ref[...],wa(slot))+vec_ref[Rows.mixed:Rows.mixed+1,here(i)]
         @pl.when(i==M0-1)
@@ -845,14 +886,9 @@
     outs,full=early(S,vectors,tokens,cotangent,valid,mask,table,pick,HEADS,weights,0)
     hid0,act0,dsl0,x1,hid1,packed,mixed,p,x2,chid,up,depth,cact,x3,hid4,act1,dsl1,dx4,result,s5,vec=outs
     fi0,fo0,ai,ao,pi,po,fi1,fo1=full[1:]
-    flat=lambda a:a.reshape(a.shape[0],S*SUB[0],SUB[1])
-    (dx3,dfi1,dfo1,dbin1,s4),_=feed_back(dx4,x3,vec,hid4,act1,dsl1,fi1,fo1,4,F32)
-    (dx2,dpv,dpo,dpi,dao,ddw,s23),_=middle_back(dx3,depth,up,chid,cact,mixed,x2,vec,valid,ao,pi,po,taps)
-    ready=[dfi1,flat(dfo1),dpo,dpi,dao]
-    across=width//SUB[1]; k=dfi1.shape[0]
-    places=[(0,1,k),(1,1,across),(5,None,across),(4,None,2*across),(3,None,across),(2,None,3*across),(0,0,k),(6,None,1),(1,0,across)]
     shapes=[feed_in.shape,feed_out.shape]+[a.shape for a in (attention_in,attention_out,pointwise_in,pointwise_out)]+[SUB]
-    (dtok,),outs=late(S,packed,p,dpv,table,pick,HEADS,hid1,ai,dx2,x1,vec,hid0,act0,dsl0,fi0,fo0,tokens,s5,s4,s23,ddw,dbin1,taps,ready,places,shapes,7)
+    rest=[dx4,x3,x2,x1,hid4,hid1,hid0,chid,cact,mixed,up,depth,act1,act0,dsl1,dsl0,fi1,fo1,ai,ao,pi,po,fi0,fo0]
+    (dtok,),outs=backward(S,packed,p,table,pick,HEADS,vec,valid,tokens,s5,rest,taps,shapes,1)
     sums=list(outs[:7])+[outs[-1]]
     if R>4:
         groups=[[g*4+i for g in range(R//4)] for i in range(4)]

time: 647 us -> 592 us (0.915)
  Pallas kernels: 615 us -> 554 us
    pallas_call x4 -> x2, Pallas kernels: 615 us -> 554 us  [call(): pl.pallas_call(kernel, grid=grid, out_shape=list(outs) + (side.out_shapes...]
where the time goes in v3:
time: 592 us; the launch traced here: 581 us
  Pallas kernels  554 us (94%)
  other arithmetic  13.5 us (2%)
  local copies, waits for them, and re-layouts  11.5 us (2%)
    pallas_call x2, Pallas kernels, call(): pl.pallas_call(kernel, grid=grid, out_shape=list(outs) + (side.out_shapes...  554 us
    convert_element_type x7, other arithmetic, local(): gfi, gfo, gai, gao, gpi, gpo, small, common = [a.astype(F32) for a in sums]  12.9 us

profile of v3, /device:TPU:0, one launch (start us, length us, event | category | flops | bytes accessed | tf_op | source)
XLA Modules:
  0.0 581.3 jit_solution(17527320341710649614)
XLA Ops:
  1.3 0.6 broadcast_in_dim.23.refs_10_
  1.9 0.8 copy.34
  2.7 0.6 pad.4.refs_11_.refs_4_
  3.4 0.8 broadcast_in_dim.20.refs_9_.refs_7_
  4.2 252.3 %gather_and_forward.1 = (bf16[512,1024]{1,0:T(8,128)(2,1)}, bf16[512,4096]{1,0:T(8,128)(2,1)}, bf16[512,4096]{1,0:T(8,128)(2,1)}, f32[512,1024]{1,0:T(8,128)}, b...) custom-call(bf16[6,128]{1,0:T(8,128)(2,1)} %refs_0_.1, ...), custom_call_target="tpu_custom_call" | custom-call | tf_op jit(solution)/shard_map/gather_and_forward/pallas_call | solution.py:290
  256.5 302.2 %backward_and_sums.1 = (bf16[512,1024]{1,0:T(8,128)(2,1)}, bf16[2,128,4096]{2,1,0:T(8,128)(2,1)}, bf16[2,512,1024]{2,1,0:T(8,128)(2,1)}, bf16[128,3072]{1,0:T(8,...) custom-call(bf16[512,3072]{1,0:T(8,128)(2,1)} %get-tuple-element.55., ...), custom_call_target="tpu_custom_call" | custom-call | tf_op jit(solution)/shard_map/backward_and_sums/pallas_call | solution.py:290
  558.7 0.0 copy-start.4
  558.7 0.0 copy-start.1
  558.7 1.4 fusion.2
  560.1 1.3 slice.38
  561.4 1.3 fusion.3
  562.7 1.3 slice.43
  564.0 0.7 slice.42
  564.8 0.1 copy.36
  564.9 0.6 slice.34
  565.5 0.9 convert_element_type.36
  566.4 0.5 slice_bitcast_fusion
  566.9 1.8 convert_element_type.40
  568.7 1.8 convert_element_type.42
  570.5 2.1 convert_element_type.41
  572.6 0.0 copy-done.4
  572.6 0.0 copy-start
  572.6 1.3 convert_element_type.39
  573.9 0.0 copy-done.1
  573.9 2.5 convert_element_type.37
  576.5 0.0 copy-done
  576.5 0.0 copy-start.2
  576.5 0.0 copy-start.3
  576.5 2.5 convert_element_type.38
  578.9 0.0 copy-done.2
  578.9 1.0 copy.40
  579.9 0.0 copy-done.3
  579.9 1.0 copy.41
  (2 shorter events, 0.0 us)
Async XLA Ops:
  558.7 14.0 %copy-start.4 = (bf16[128,3072]{1,0:T(8,128)(2,1)S(1)}, bf16[128,3072]{1,0:T(8,128)(2,1)}, u32[]{:S(2)}) copy-start(bf16[128,3072]{1,0:T(8,128)(2,1)} %get-tuple-element.87) | copy-start | bytes 2359300
  558.7 15.3 %copy-start.1 = (bf16[2,128,4096]{2,1,0:T(8,128)(2,1)S(1)}, bf16[2,128,4096]{2,1,0:T(8,128)(2,1)}, u32[]{:S(2)}) copy-start(bf16[2,128,4096]{2,1,0:T(8,128)(2,1)} %get-tuple-element.85) | copy-start | bytes 6291460
  572.6 3.8 copy-start
  576.5 2.5 copy-start.2
  576.5 3.5 copy-start.3
